TPU v7x, 32 devices: a whole 2x2x4 slice. The times are simulated.
32 devices in a mesh: dp: 4 (over y, core), ctx: 8 (over z, x).
Axes of the slice: x: 2, y: 2, z: 4, core: 2. Of those that a mesh axis runs over, the one named last changes fastest.
Arguments:
- layer_input: bfloat16 [8192, 1024], P(('dp', 'ctx')), may hold values from -6 to 6
- query_weight: bfloat16 [1024, 1024], P('dp'), may hold values from -0.75 to 0.75
- key_weight: bfloat16 [1024, 512], P('dp'), may hold values from -0.75 to 0.75
- value_weight: bfloat16 [1024, 512], P('dp'), may hold values from -0.1875 to 0.1875
- out_weight: bfloat16 [1024, 1024], P('dp'), may hold values from -1.5 to 1.5
- attn_gain: bfloat16 [1024], P('dp'), may hold values from 0.5 to 1.5
- router_weight: bfloat16 [1024, 32], P('dp'), may hold values from -0.08984375 to 0.08984375
- moe_gain: bfloat16 [1024], P('dp'), may hold values from 0.5 to 1.5
- gate_weight: bfloat16 [32, 1024, 512], P('dp'), may hold values from -0.1875 to 0.1875
- up_weight: bfloat16 [32, 1024, 512], P('dp'), may hold values from -0.1875 to 0.1875
- down_weight: bfloat16 [32, 512, 1024], P('dp'), may hold values from -0.75 to 0.75
- expert_ids: int32 [8192, 8], P(('dp', 'ctx')), may hold values from 0 to 31, all different within a row
- fill_order: int32 [32, 256], P(('dp', 'ctx')), may hold values from 0 to 255, each once within a row
- block_deal: int32 [4, 16], P('dp'), may hold values from 0 to 15, each once within a row
- seq_lengths: int32 [4, 4], P('dp'), may hold values from 1 to 1024, 2048 in all within a row
- out_grad: float32 [8192, 1024], P(('dp', 'ctx')), may hold values from -6 to 6
Outputs:
- layer_output: float32 [8192, 1024], P(('dp', 'ctx'))
- input_grad: float32 [8192, 1024], P(('dp', 'ctx'))
- query_grad: float32 [1024, 1024], P('dp')
- key_grad: float32 [1024, 512], P('dp')
- value_grad: float32 [1024, 512], P('dp')
- outproj_grad: float32 [1024, 1024], P('dp')
- attn_gain_grad: float32 [1024], P('dp')
- router_grad: float32 [1024, 32], P('dp')
- moe_gain_grad: float32 [1024], P('dp')
- gate_grad: float32 [32, 1024, 512], P('dp')
- up_grad: float32 [32, 1024, 512], P('dp')
- down_grad: float32 [32, 512, 1024], P('dp')
Inputs may be any that keep to these rules, and one draw needn't show every extreme that they name: `expert_ids`: each row names 8 different experts, and every expert is named. `fill_order`: each row is a permutation. `block_deal`: each row is a permutation. `seq_lengths`: each row sums to 2048, and its largest length is 1024.
All inputs are finite; a program needn't handle non-finite values.
Results may differ from a plain program's by a relative error of at most 0.023.
Values may be sent and summed in bfloat16 or wider, within the bound.
No kernel may reach another device: no remote copies, remote signals or barrier semaphores. Data moves between devices by JAX's collectives and lax.ppermute only.
A program may use at most 192 MiB of HBM per device.

v0:
```python
import jax
import jax.numpy as jnp
from jax import lax
from jax.sharding import PartitionSpec as P

D = 1024
QUERY_HEADS = 16
KEY_VALUE_HEADS = 8
HEAD_SIZE = 64
EXPERTS = 32
BLOCK = 128
CAP = 64
QD = 1024
KVD = 512


EPS = 1e-06
NEGATIVE_FILL = -1e30


def group_positions(block_order, seq_lens):
    token_places = (
        block_order[:, None] * BLOCK + jnp.arange(BLOCK, dtype=jnp.int32)[None, :]
    ).reshape(-1)
    seq_ends = jnp.cumsum(seq_lens, dtype=jnp.int32)
    passed = (token_places[:, None] >= seq_ends[None, :]).astype(jnp.int32)
    sequence_starts = jnp.sum(seq_lens[None, :] * passed, axis=1, dtype=jnp.int32)
    return (token_places, sequence_starts)


def rope_tables(relative):
    half_width = HEAD_SIZE // 2
    inverse = 10000.0 ** (-jnp.arange(half_width, dtype=jnp.float32) * (2.0 / HEAD_SIZE))
    angles = relative[:, None] * inverse[None, :]
    return (jnp.cos(angles)[:, None, :], jnp.sin(angles)[:, None, :])


def rotary_turn(values, cosine_table, sine_table):
    half_width = values.shape[-1] // 2
    first_half = values[..., :half_width]
    second_half = values[..., half_width:]
    return jnp.concatenate(
        [
            first_half * cosine_table - second_half * sine_table,
            second_half * cosine_table + first_half * sine_table,
        ],
        axis=-1,
    )


def rotary_backward(incoming, cosine_table, sine_table):
    half_width = incoming.shape[-1] // 2
    first_half = incoming[..., :half_width]
    second_half = incoming[..., half_width:]
    return jnp.concatenate(
        [
            first_half * cosine_table + second_half * sine_table,
            second_half * cosine_table - first_half * sine_table,
        ],
        axis=-1,
    )


def slot_tables(chosen, order_rank):
    tok_count = chosen.shape[0]
    picks = chosen.shape[1]
    choice_hits = (
        chosen[:, :, None] == jnp.arange(EXPERTS, dtype=jnp.int32)[None, None, :]
    ).astype(jnp.int32)
    per_token = jnp.sum(choice_hits, axis=1, dtype=jnp.int32)
    earlier = (order_rank[None, :] < order_rank[:, None]).astype(jnp.int32)
    prior = jnp.dot(earlier, per_token)
    slot_index = jnp.sum(choice_hits * prior[:, None, :], axis=2, dtype=jnp.int32)
    kept_pairs = slot_index < CAP
    flat_pair = chosen * CAP + jnp.minimum(slot_index, CAP - 1)
    target = jnp.where(kept_pairs, chosen * CAP + slot_index, EXPERTS * CAP).reshape(-1)
    token_ids = jnp.broadcast_to(
        jnp.arange(tok_count, dtype=jnp.int32)[:, None], (tok_count, picks)
    ).reshape(-1)
    pick_ids = jnp.broadcast_to(
        jnp.arange(picks, dtype=jnp.int32)[None, :], (tok_count, picks)
    ).reshape(-1)
    slot_token = (
        jnp.zeros((EXPERTS * CAP + 1,), jnp.int32).at[target].set(token_ids)[: EXPERTS * CAP]
    )
    slot_pick = jnp.zeros((EXPERTS * CAP + 1,), jnp.int32).at[target].set(pick_ids)[: EXPERTS * CAP]
    slot_live = (
        jnp.zeros((EXPERTS * CAP + 1,), jnp.int32)
        .at[target]
        .set(jnp.ones_like(token_ids))[: EXPERTS * CAP]
    )
    return (choice_hits, kept_pairs, flat_pair, slot_token, slot_pick, slot_live)


def masked_scores(query_block, key_block, query_places, query_starts, key_places):
    raw_scores = jnp.einsum(
        "qgrd,kgd->grqk", query_block, key_block, preferred_element_type=jnp.float32
    ) * (1.0 / HEAD_SIZE)
    allowed = (key_places[None, :] <= query_places[:, None]) & (
        key_places[None, :] >= query_starts[:, None]
    )
    return jnp.where(allowed[None, None], raw_scores, NEGATIVE_FILL)


def norm_back(grad_normed, normed, inverse_rms, gain_float):
    scaled = grad_normed * gain_float
    return inverse_rms * (scaled - normed * jnp.mean(scaled * normed, axis=-1, keepdims=True))


def on_device(
    layer_input,
    query_weight,
    key_weight,
    value_weight,
    out_weight,
    attn_gain,
    router_weight,
    moe_gain,
    gate_weight,
    up_weight,
    down_weight,
    expert_ids,
    fill_order,
    block_deal,
    seq_lengths,
    out_grad,
):
    token_rows = layer_input.shape[0]
    rotation_ratio = QUERY_HEADS // KEY_VALUE_HEADS
    scale_inv = 1.0 / HEAD_SIZE
    dense_full = (
        lax.all_gather(query_weight, "dp", axis=0, tiled=True),
        lax.all_gather(key_weight, "dp", axis=0, tiled=True),
        lax.all_gather(value_weight, "dp", axis=0, tiled=True),
        lax.all_gather(out_weight, "dp", axis=0, tiled=True),
        lax.all_gather(attn_gain, "dp", axis=0, tiled=True),
        lax.all_gather(router_weight, "dp", axis=0, tiled=True),
        lax.all_gather(moe_gain, "dp", axis=0, tiled=True),
    )
    query_full, key_full, value_full, outproj_full, gain_attn, router_full, gain_moe = dense_full
    places_all, starts_all = group_positions(block_deal[0], seq_lengths[0])
    group_rows = places_all.shape[0]
    shard_index = lax.axis_index("ctx")
    places_mine = lax.dynamic_slice_in_dim(places_all, shard_index * token_rows, token_rows)
    starts_mine = lax.dynamic_slice_in_dim(starts_all, shard_index * token_rows, token_rows)
    cosine_table, sine_table = rope_tables((places_mine - starts_mine).astype(jnp.float32))
    input_float = layer_input.astype(jnp.float32)
    rms_one = lax.rsqrt(jnp.mean(input_float * input_float, axis=-1, keepdims=True) + EPS)
    first_normed = input_float * rms_one
    gain_one = gain_attn.astype(jnp.float32)
    act_one = (first_normed * gain_one).astype(jnp.bfloat16)
    query_raw = jnp.dot(act_one, query_full, preferred_element_type=jnp.float32)
    key_unrotated = jnp.dot(act_one, key_full, preferred_element_type=jnp.float32)
    value_raw = jnp.dot(act_one, value_full, preferred_element_type=jnp.float32)
    query_entries = (
        rotary_turn(query_raw.reshape(token_rows, QUERY_HEADS, HEAD_SIZE), cosine_table, sine_table)
        .astype(jnp.bfloat16)
        .reshape(token_rows, KEY_VALUE_HEADS, rotation_ratio, HEAD_SIZE)
    )
    key_rows = (
        rotary_turn(
            key_unrotated.reshape(token_rows, KEY_VALUE_HEADS, HEAD_SIZE), cosine_table, sine_table
        )
        .astype(jnp.bfloat16)
        .reshape(token_rows, KVD)
    )
    value_rows = value_raw.astype(jnp.bfloat16)
    every_key, every_value = (
        lax.all_gather(key_rows, "ctx", axis=0, tiled=True),
        lax.all_gather(value_rows, "ctx", axis=0, tiled=True),
    )
    key_row_count = min(512, group_rows)
    block_total = group_rows // key_row_count
    key_block_list = every_key.reshape(block_total, key_row_count, KEY_VALUE_HEADS, HEAD_SIZE)
    value_block_list = every_value.reshape(block_total, key_row_count, KEY_VALUE_HEADS, HEAD_SIZE)
    place_blocks = places_all.reshape(block_total, key_row_count)

    def max_step(carry, block_in):
        running_max, running_total = carry
        key_block, key_places = block_in
        scores = masked_scores(query_entries, key_block, places_mine, starts_mine, key_places)
        new_max = jnp.maximum(running_max, jnp.max(scores, axis=-1))
        running_total = running_total * jnp.exp(running_max - new_max) + jnp.sum(
            jnp.exp(scores - new_max[..., None]), axis=-1
        )
        return ((new_max, running_total), None)

    largest_start = jnp.full(
        (KEY_VALUE_HEADS, rotation_ratio, token_rows), NEGATIVE_FILL, jnp.float32
    )
    starts_summed = jnp.zeros((KEY_VALUE_HEADS, rotation_ratio, token_rows), jnp.float32)
    (row_max, row_total), _ = lax.scan(
        max_step, (largest_start, starts_summed), (key_block_list, place_blocks)
    )
    log_total = row_max + jnp.log(row_total)

    def value_step(running, block_in):
        key_block, value_block, key_places = block_in
        scores = masked_scores(query_entries, key_block, places_mine, starts_mine, key_places)
        weights = jnp.exp(scores - log_total[..., None]).astype(jnp.bfloat16)
        return (
            running
            + jnp.einsum(
                "grqk,kgd->qgrd", weights, value_block, preferred_element_type=jnp.float32
            ),
            None,
        )

    attended_rows, _ = lax.scan(
        value_step,
        jnp.zeros((token_rows, KEY_VALUE_HEADS, rotation_ratio, HEAD_SIZE), jnp.float32),
        (key_block_list, value_block_list, place_blocks),
    )
    attended_low = attended_rows.reshape(token_rows, QD).astype(jnp.bfloat16)
    mixed = input_float + jnp.dot(attended_low, outproj_full, preferred_element_type=jnp.float32)
    rms_two = lax.rsqrt(jnp.mean(mixed * mixed, axis=-1, keepdims=True) + EPS)
    normed_two = mixed * rms_two
    gain_two = gain_moe.astype(jnp.float32)
    act_two = (normed_two * gain_two).astype(jnp.bfloat16)
    logits = jnp.dot(act_two, router_full, preferred_element_type=jnp.float32)
    choice_hits, kept_pairs, flat_pair, slot_token, slot_pick, slot_live = slot_tables(
        expert_ids, fill_order[0]
    )
    hit_float = choice_hits.astype(jnp.float32)
    chosen_logits = jnp.sum(hit_float * logits[:, None, :], axis=2)
    gates = jax.nn.softmax(chosen_logits, axis=-1)
    kept_float = kept_pairs.astype(jnp.float32)
    live_rows = slot_live[:, None] > 0
    dispatch_rows = jnp.where(live_rows, act_two[slot_token], jnp.zeros((), jnp.bfloat16)).reshape(
        EXPERTS, CAP, D
    )
    expert_rows = lax.all_to_all(dispatch_rows, "dp", split_axis=0, concat_axis=1, tiled=True)
    gate_part = jnp.einsum(
        "erd,edf->erf", expert_rows, gate_weight, preferred_element_type=jnp.float32
    )
    up_part = jnp.einsum("erd,edf->erf", expert_rows, up_weight, preferred_element_type=jnp.float32)
    sig_gate = jax.nn.sigmoid(gate_part)
    act_gate = gate_part * sig_gate
    hidden = (act_gate * up_part).astype(jnp.bfloat16)
    expert_out = jnp.einsum(
        "erf,efd->erd", hidden, down_weight, preferred_element_type=jnp.float32
    ).astype(jnp.bfloat16)
    returned = lax.all_to_all(expert_out, "dp", split_axis=1, concat_axis=0, tiled=True).reshape(
        EXPERTS * CAP, D
    )
    pair_rows = returned[flat_pair].astype(jnp.float32)
    pair_weights = gates * kept_float
    layer_output = mixed + jnp.einsum("tk,tkd->td", pair_weights, pair_rows)
    grad_gate = kept_float * jnp.einsum("td,tkd->tk", out_grad, pair_rows)
    grad_sel = gates * (grad_gate - jnp.sum(gates * grad_gate, axis=-1, keepdims=True))
    grad_logits = jnp.sum(grad_sel[:, :, None] * hit_float, axis=1).astype(jnp.bfloat16)
    slot_gates = gates[slot_token, slot_pick]
    grad_slots = (
        jnp.where(live_rows, slot_gates[:, None] * out_grad[slot_token], 0.0)
        .astype(jnp.bfloat16)
        .reshape(EXPERTS, CAP, D)
    )
    grad_expert_out = lax.all_to_all(grad_slots, "dp", split_axis=0, concat_axis=1, tiled=True)
    down_part = jnp.einsum(
        "erf,erd->efd", hidden, grad_expert_out, preferred_element_type=jnp.float32
    )
    grad_hidden = jnp.einsum(
        "erd,efd->erf", grad_expert_out, down_weight, preferred_element_type=jnp.float32
    )
    grad_gu = (grad_hidden * up_part * sig_gate * (1.0 + gate_part * (1.0 - sig_gate))).astype(
        jnp.bfloat16
    )
    grad_up = (grad_hidden * act_gate).astype(jnp.bfloat16)
    gate_part_grad = jnp.einsum(
        "erd,erf->edf", expert_rows, grad_gu, preferred_element_type=jnp.float32
    )
    up_part_grad = jnp.einsum(
        "erd,erf->edf", expert_rows, grad_up, preferred_element_type=jnp.float32
    )
    grad_expert_in = (
        jnp.einsum("erf,edf->erd", grad_gu, gate_weight, preferred_element_type=jnp.float32)
        + jnp.einsum("erf,edf->erd", grad_up, up_weight, preferred_element_type=jnp.float32)
    ).astype(jnp.bfloat16)
    grad_back = lax.all_to_all(
        grad_expert_in, "dp", split_axis=1, concat_axis=0, tiled=True
    ).reshape(EXPERTS * CAP, D)
    dense_back = (
        lax.all_gather(query_weight, "dp", axis=0, tiled=True),
        lax.all_gather(key_weight, "dp", axis=0, tiled=True),
        lax.all_gather(value_weight, "dp", axis=0, tiled=True),
        lax.all_gather(out_weight, "dp", axis=0, tiled=True),
        lax.all_gather(attn_gain, "dp", axis=0, tiled=True),
        lax.all_gather(router_weight, "dp", axis=0, tiled=True),
        lax.all_gather(moe_gain, "dp", axis=0, tiled=True),
    )
    query_back, key_back, value_back, outproj_back, gain_attn_back, router_back, gain_moe_back = (
        dense_back
    )
    grad_act_two = jnp.einsum("tk,tkd->td", kept_float, grad_back[flat_pair].astype(jnp.float32))
    grad_act_two = grad_act_two + jnp.einsum(
        "te,de->td", grad_logits, router_back, preferred_element_type=jnp.float32
    )
    router_part = jnp.einsum("td,te->de", act_two, grad_logits, preferred_element_type=jnp.float32)
    gain_two_part = jnp.sum(grad_act_two * normed_two, axis=0)
    grad_mixed = out_grad + norm_back(
        grad_act_two, normed_two, rms_two, gain_moe_back.astype(jnp.float32)
    )
    grad_mixed_low = grad_mixed.astype(jnp.bfloat16)
    outproj_part = jnp.einsum(
        "tq,td->qd", attended_low, grad_mixed_low, preferred_element_type=jnp.float32
    )
    grad_heads = (
        jnp.einsum("td,qd->tq", grad_mixed_low, outproj_back, preferred_element_type=jnp.float32)
        .astype(jnp.bfloat16)
        .reshape(token_rows, KEY_VALUE_HEADS, rotation_ratio, HEAD_SIZE)
    )
    delta = jnp.sum(grad_heads.astype(jnp.float32) * attended_rows, axis=-1).transpose(1, 2, 0)

    def grad_step(running, block_in):
        key_block, value_block, key_places = block_in
        scores = masked_scores(query_entries, key_block, places_mine, starts_mine, key_places)
        weights = jnp.exp(scores - log_total[..., None])
        value_term = jnp.einsum(
            "grqk,qgrd->kgd",
            weights.astype(jnp.bfloat16),
            grad_heads,
            preferred_element_type=jnp.float32,
        )
        weight_grad = jnp.einsum(
            "qgrd,kgd->grqk", grad_heads, value_block, preferred_element_type=jnp.float32
        )
        score_grad = (weights * (weight_grad - delta[..., None])).astype(jnp.bfloat16)
        running = (
            running
            + jnp.einsum(
                "grqk,kgd->qgrd", score_grad, key_block, preferred_element_type=jnp.float32
            )
            * scale_inv
        )
        key_term = (
            jnp.einsum(
                "grqk,qgrd->kgd", score_grad, query_entries, preferred_element_type=jnp.float32
            )
            * scale_inv
        )
        return (
            running,
            jnp.concatenate(
                [key_term.reshape(key_row_count, KVD), value_term.reshape(key_row_count, KVD)],
                axis=1,
            ),
        )

    query_grads, kv_terms = lax.scan(
        grad_step,
        jnp.zeros((token_rows, KEY_VALUE_HEADS, rotation_ratio, HEAD_SIZE), jnp.float32),
        (key_block_list, value_block_list, place_blocks),
    )
    kv_mine = lax.psum_scatter(
        kv_terms.reshape(group_rows, 2 * KVD).astype(jnp.bfloat16),
        "ctx",
        scatter_dimension=0,
        tiled=True,
    ).astype(jnp.float32)
    key_gradient_rows = kv_mine[:, :KVD]
    value_grads = kv_mine[:, KVD:]
    grad_query_raw = (
        rotary_backward(
            query_grads.reshape(token_rows, QUERY_HEADS, HEAD_SIZE), cosine_table, sine_table
        )
        .reshape(token_rows, QD)
        .astype(jnp.bfloat16)
    )
    grad_key_raw = (
        rotary_backward(
            key_gradient_rows.reshape(token_rows, KEY_VALUE_HEADS, HEAD_SIZE),
            cosine_table,
            sine_table,
        )
        .reshape(token_rows, KVD)
        .astype(jnp.bfloat16)
    )
    grad_value_raw = value_grads.astype(jnp.bfloat16)
    query_part = jnp.einsum(
        "td,tq->dq", act_one, grad_query_raw, preferred_element_type=jnp.float32
    )
    key_part = jnp.einsum("td,tq->dq", act_one, grad_key_raw, preferred_element_type=jnp.float32)
    value_part = jnp.einsum(
        "td,tq->dq", act_one, grad_value_raw, preferred_element_type=jnp.float32
    )
    grad_act_one = jnp.einsum(
        "tq,dq->td", grad_query_raw, query_back, preferred_element_type=jnp.float32
    )
    grad_act_one = grad_act_one + jnp.einsum(
        "tq,dq->td", grad_key_raw, key_back, preferred_element_type=jnp.float32
    )
    grad_act_one = grad_act_one + jnp.einsum(
        "tq,dq->td", grad_value_raw, value_back, preferred_element_type=jnp.float32
    )
    gain_one_part = jnp.sum(grad_act_one * first_normed, axis=0)
    input_grad = grad_mixed + norm_back(
        grad_act_one, first_normed, rms_one, gain_attn_back.astype(jnp.float32)
    )
    summed = (
        lax.psum(gate_part_grad.astype(jnp.bfloat16), "ctx").astype(jnp.float32),
        lax.psum(up_part_grad.astype(jnp.bfloat16), "ctx").astype(jnp.float32),
        lax.psum(down_part.astype(jnp.bfloat16), "ctx").astype(jnp.float32),
        lax.psum(query_part.astype(jnp.bfloat16), "ctx").astype(jnp.float32),
        lax.psum(key_part.astype(jnp.bfloat16), "ctx").astype(jnp.float32),
        lax.psum(value_part.astype(jnp.bfloat16), "ctx").astype(jnp.float32),
        lax.psum(outproj_part.astype(jnp.bfloat16), "ctx").astype(jnp.float32),
        lax.psum(gain_one_part.astype(jnp.bfloat16), "ctx").astype(jnp.float32),
        lax.psum(router_part.astype(jnp.bfloat16), "ctx").astype(jnp.float32),
        lax.psum(gain_two_part.astype(jnp.bfloat16), "ctx").astype(jnp.float32),
    )
    owned = (
        lax.psum_scatter(
            summed[3].astype(jnp.bfloat16), "dp", scatter_dimension=0, tiled=True
        ).astype(jnp.float32),
        lax.psum_scatter(
            summed[4].astype(jnp.bfloat16), "dp", scatter_dimension=0, tiled=True
        ).astype(jnp.float32),
        lax.psum_scatter(
            summed[5].astype(jnp.bfloat16), "dp", scatter_dimension=0, tiled=True
        ).astype(jnp.float32),
        lax.psum_scatter(
            summed[6].astype(jnp.bfloat16), "dp", scatter_dimension=0, tiled=True
        ).astype(jnp.float32),
        lax.psum_scatter(
            summed[7].astype(jnp.bfloat16), "dp", scatter_dimension=0, tiled=True
        ).astype(jnp.float32),
        lax.psum_scatter(
            summed[8].astype(jnp.bfloat16), "dp", scatter_dimension=0, tiled=True
        ).astype(jnp.float32),
        lax.psum_scatter(
            summed[9].astype(jnp.bfloat16), "dp", scatter_dimension=0, tiled=True
        ).astype(jnp.float32),
    )
    expert_sums = (summed[0], summed[1], summed[2])
    return (
        layer_output,
        input_grad,
        owned[0],
        owned[1],
        owned[2],
        owned[3],
        owned[4],
        owned[5],
        owned[6],
        expert_sums[0],
        expert_sums[1],
        expert_sums[2],
    )


def solution(mesh):
    in_specs = (
        P(("dp", "ctx"), None),
        P("dp", None),
        P("dp", None),
        P("dp", None),
        P("dp", None),
        P("dp"),
        P("dp", None),
        P("dp"),
        P("dp", None, None),
        P("dp", None, None),
        P("dp", None, None),
        P(("dp", "ctx"), None),
        P(("dp", "ctx"), None),
        P("dp", None),
        P("dp", None),
        P(("dp", "ctx"), None),
    )
    out_specs = (
        P(("dp", "ctx"), None),
        P(("dp", "ctx"), None),
        P("dp", None),
        P("dp", None),
        P("dp", None),
        P("dp", None),
        P("dp"),
        P("dp", None),
        P("dp"),
        P("dp", None, None),
        P("dp", None, None),
        P("dp", None, None),
    )
    return jax.shard_map(
        on_device, mesh=mesh, in_specs=in_specs, out_specs=out_specs, check_vma=False
    )
```

profile of v0, /device:TPU:0, one launch (start us, length us, event | category | flops | bytes accessed | tf_op | source)
XLA Modules:
  0.0 1708.6 jit_solution(17947363201074201761)
XLA Ops:
  20.1 9.0 all-gather.13.cloned.1.call-done
  31.9 15.5 all-gather.9.cloned.1.call-done
  72.9 8.2 scatter_custom_fusion.1
  84.1 41.0 %all-gather.15.cloned.1.call-done = bf16[2048,512]{0,1:T(8,128)(2,1)} async-done(((bf16[256,512]{0,1:T(8,128)(2,1)}), bf16[2048,512]{0,1:T(8,128)(2,1)}) %all-gather.15.cloned.1.call-update) | async-done | bytes 2097168 | tf_op jit(solution)/shard_map/all_gather | solution.py:169
  130.3 17.6 %while.37 = (s32[]{:T(128)}, f32[8,2,256]{2,1,0:T(2,128)S(1)}, f32[8,2,256]{2,1,0:T(2,128)S(1)}, s32[4,512]{1,0:T(4,128)S(1)}, s32[256]{0:T(256)S(1)}, /*index=5...) while((s32[]{:T(128)}, f32[8,2,256]{2,1,0:T(2,128)S(1)}, ...), condition=%wide.region_6.7_spmd.clone, body=%wide.region_3.6_spmd.clone.sunk | while | flops 283529216 | bytes 18440320 | solution.py:192
  147.9 27.3 %all-gather.11.cloned.1.call-done = bf16[2048,512]{1,0:T(8,128)(2,1)} async-done(((bf16[256,512]{1,0:T(8,128)(2,1)}), bf16[2048,512]{1,0:T(8,128)(2,1)}) %all-gather.11.cloned.1.call-update) | async-done | bytes 2097168 | tf_op jit(solution)/shard_map/all_gather | solution.py:170
  187.0 17.0 while.38
  207.6 9.6 gather_fusion
  219.7 51.2 %all_to_all.66 = bf16[32,64,1024]{2,1,0:T(8,128)(2,1)S(1)} all-to-all(bf16[32,64,1024]{2,1,0:T(8,128)(2,1)S(1)} %broadcast_select_fusion.1), channel_id=1, replica_groups=mesh['dp'=4,'ctx'=8] {'dp'}, dimensions={0} | all-to-all | bytes 8388608 | tf_op jit(solution)/shard_map/all_to_all | solution.py:232
  277.0 9.5 multiply_convert_fusion.2
  298.4 9.7 gather_fusion.3
  308.1 39.4 %all_gather.42 = bf16[1024,32]{0,1:T(8,128)(2,1)S(1)} all-gather(bf16[256,32]{0,1:T(8,128)(2,1)S(1)} %copy-done.30), channel_id=1, replica_groups=mesh['dp'=4,'ctx'=8] {'dp'}, dimensions={0}, use_global_device_ids=true | all-gather | bytes 81920 | tf_op jit(solution)/shard_map/all_gather | solution.py:137
  354.4 13.7 gather_fusion.1
  372.8 12.5 gather_fusion.2
  389.4 50.9 %all_to_all.67 = bf16[32,64,1024]{2,1,0:T(8,128)(2,1)S(1)} all-to-all(bf16[32,64,1024]{2,1,0:T(8,128)(2,1)S(1)} %select_convert_fusion), channel_id=1, replica_groups=mesh['dp'=4,'ctx'=8] {'dp'}, dimensions={0} | all-to-all | bytes 8388608 | tf_op jit(solution)/shard_map/all_to_all | solution.py:258
  442.7 12.5 multiply_convert_fusion
  455.2 9.8 fusion.110
  465.0 10.8 add_convert_fusion
  492.2 43.3 %all-to-all-done.3 = bf16[8,256,1024]{2,0,1:T(8,128)(2,1)} async-done(((bf16[8,256,1024]{2,0,1:T(8,128)(2,1)}), bf16[8,256,1024]{2,0,1:T(8,128)(2,1)}, u32[]{:S(2)}, u32[]{:S(2)}) %all-to-all-start.3) | async-done | bytes 4194336 | tf_op jit(solution)/shard_map/all_to_all | solution.py:279
  542.0 14.1 gather_fusion.4
  563.8 59.4 %while.39 = (s32[]{:T(128)}, f32[256,8,2,64]{0,3,2,1:T(8,128)}, bf16[4,512,1024]{2,1,0:T(8,128)(2,1)}, bf16[4,512,8,64]{1,3,2,0:T(8,128)(2,1)}, s32[4,512]{1,0:T...) while((s32[]{:T(128)}, f32[256,8,2,64]{0,3,2,1:T(8,128)}, ...), condition=%wide.region_23.24_spmd.clone, body=%wide.region_22.23_spmd.clone.sunk | while | flops 1366949888 | bytes 51306664 | solution.py:349
  630.6 78.4 %reduce-scatter.7.cloned.1.call-done = bf16[256,1024]{1,0:T(8,128)(2,1)} async-done(((bf16[2048,1024]{1,0:T(8,128)(2,1)}), bf16[256,1024]{1,0:T(8,128)(2,1)}) %reduce-scatter.7.cloned.1.call-update) | async-done | bytes 524304 | tf_op jit(solution)/shard_map/reduce_scatter | solution.py:354
  717.3 9.3 convolution_convert_fusion
  742.9 34.0 %reduce-scatter.9.cloned.1.call-done = bf16[256,1024]{1,0:T(8,128)(2,1)} async-done(((bf16[1024,1024]{1,0:T(8,128)(2,1)}), bf16[256,1024]{1,0:T(8,128)(2,1)}) %reduce-scatter.9.cloned.1.call-update) | async-done | bytes 524304 | tf_op jit(solution)/shard_map/reduce_scatter | solution.py:412
  776.9 28.0 %reduce-scatter.13.cloned.1.call-done = bf16[256,512]{1,0:T(8,128)(2,1)} async-done(((bf16[1024,512]{1,0:T(8,128)(2,1)}), bf16[256,512]{1,0:T(8,128)(2,1)}) %reduce-scatter.13.cloned.1.call-update) | async-done | bytes 262160 | tf_op jit(solution)/shard_map/reduce_scatter | solution.py:418
  804.9 28.0 %reduce-scatter.11.cloned.1.call-done = bf16[256,512]{1,0:T(8,128)(2,1)} async-done(((bf16[1024,512]{1,0:T(8,128)(2,1)}), bf16[256,512]{1,0:T(8,128)(2,1)}) %reduce-scatter.11.cloned.1.call-update) | async-done | bytes 262160 | tf_op jit(solution)/shard_map/reduce_scatter | solution.py:415
  846.7 8.7 reduce-scatter.17.cloned.1.call-done
  855.4 38.7 %all-reduce.2 = (bf16[256]{0:T(256)(128)(2,1)S(1)}, bf16[256,32]{0,1:T(8,128)(2,1)S(1)}, bf16[256]{0:T(256)(128)(2,1)S(1)}) all-reduce(bf16[256]{0:T(256)(128)(2,1)S(1)} %dynamic-slice.1, bf16[256,32]{0,1:T(8,128)(2,1)} %reduce-scatter.17.cloned.1.call-done, bf16[256]{0:T(256)(128)(2,1)S(1)} %dynamic-slice.3), channel_id=1, replica_groups=mesh['dp'=4,'ctx'=8] {'ctx'}, use_global_device_ids=true, to_apply=%region_35.36 | all-reduce | flops 8704 | bytes 34816 | tf_op jit(solution)/shard_map/psum | solution.py:407
  897.1 761.4 %all-reduce.7.cloned.1.call-done = (bf16[256,1024]{1,0:T(8,128)(2,1)}, bf16[256,512]{1,0:T(8,128)(2,1)}, bf16[256,512]{1,0:T(8,128)(2,1)}, bf16[256,1024]{1,0:T(...) async-done(((bf16[256,1024]{1,0:T(8,128)(2,1)}, bf16[256,512]{1,0:T(8,128)(2,1)}, ...) | async-done | bytes 26738704 | tf_op jit(solution)/shard_map/psum | solution.py:403
  1666.4 11.9 convert_element_type.218
  1678.2 11.9 convert_element_type.220
  1690.1 11.7 convert_element_type.222
  (314 shorter events, 282.5 us)
Async XLA Ops:
  7.2 40.2 %copy-start.5 = (bf16[256,1024]{1,0:T(8,128)(2,1)S(1)}, bf16[256,1024]{1,0:T(8,128)(2,1)}, u32[]{:S(2)}) copy-start(bf16[256,1024]{1,0:T(8,128)(2,1)} %param.22) | copy-start | bytes 1572868
  7.2 21.9 %all-gather.13.cloned.1.call-start = ((), (), s32[]{:S(2)}) async-start(), calls=%async_computation.12 | async-start | bytes 1310720 | tf_op jit(solution)/shard_map/all_gather | solution.py:133
  7.9 42.5 %copy-start.34 = (bf16[256]{0:T(256)(128)(2,1)S(1)}, bf16[256]{0:T(256)(128)(2,1)}, u32[]{:S(2)}) copy-start(bf16[256]{0:T(256)(128)(2,1)} %param.29) | copy-start | bytes 1540
  7.9 47.7 %copy-start.25 = (s32[256,8]{0,1:T(8,128)S(1)}, s32[256,8]{0,1:T(8,128)}, u32[]{:S(2)}) copy-start(s32[256,8]{0,1:T(8,128)} %param.33) | copy-start | bytes 24580
  7.9 47.8 %copy-start.33 = (s32[1,256]{1,0:T(1,128)S(1)}, s32[1,256]{1,0:T(1,128)}, u32[]{:S(2)}) copy-start(s32[1,256]{1,0:T(1,128)} %param.34) | copy-start | bytes 3076
  8.0 39.4 %all-gather.9.cloned.1.call-start = ((), (), s32[]{:S(2)}) async-start(), calls=%async_computation.10 | async-start | bytes 1310720 | tf_op jit(solution)/shard_map/all_gather | solution.py:134
  8.7 72.5 %all-gather.17.cloned.1.call-start = ((), (), s32[]{:S(2)}) async-start(), calls=%async_computation.14 | async-start | bytes 2621440 | tf_op jit(solution)/shard_map/all_gather | solution.py:132
  9.4 115.7 %all-gather.15.cloned.1.call-start = ((), (), s32[]{:S(2)}) async-start(), calls=%async_computation.13 | async-start | bytes 2359296 | tf_op jit(solution)/shard_map/all_gather | solution.py:169
  17.0 64.2 %copy-start.26 = (f32[4,1,256]{2,1,0:T(1,128)}, f32[4,1,256]{2,1,0:T(1,128)S(1)}, u32[]{:S(2)}) copy-start(f32[4,1,256]{2,1,0:T(1,128)S(1)} %convert_element_type.223) | copy-start | bytes 12292
  19.8 64.0 %copy-start.28 = (f32[256]{0:T(256)}, f32[256]{0:T(256)S(1)}, u32[]{:S(2)}) copy-start(f32[256]{0:T(256)S(1)} %add_rsqrt_fusion.1) | copy-start | bytes 3076
  20.0 63.8 %copy-start.20 = (f32[256,32]{0,1:T(8,128)}, f32[256,32]{0,1:T(8,128)S(1)}, u32[]{:S(2)}) copy-start(f32[256,32]{0,1:T(8,128)S(1)} %get-tuple-element.472) | copy-start | bytes 98308
  20.1 63.8 %copy-start.22 = (f32[256,32]{0,1:T(8,128)}, f32[256,32]{0,1:T(8,128)S(1)}, u32[]{:S(2)}) copy-start(f32[256,32]{0,1:T(8,128)S(1)} %get-tuple-element.473) | copy-start | bytes 98308
  31.9 143.3 %all-gather.11.cloned.1.call-start = ((), (), s32[]{:S(2)}) async-start(), calls=%async_computation.11 | async-start | bytes 2359296 | tf_op jit(solution)/shard_map/all_gather | solution.py:170
  49.8 154.3 %all-gather.19.cloned.1.call-start = ((), (), s32[]{:S(2)}) async-start(), calls=%async_computation.15 | async-start | bytes 2621440 | tf_op jit(solution)/shard_map/all_gather | solution.py:135
  204.0 13.2 copy-start.31
  204.1 13.1 copy-start.14
  207.6 139.9 %copy-start.1 = (bf16[256,1024]{1,0:T(8,128)(2,1)}, bf16[256,1024]{1,0:T(8,128)(2,1)S(1)}, u32[]{:S(2)}) copy-start(bf16[256,1024]{1,0:T(8,128)(2,1)S(1)} %multiply_convert_fusion.3) | copy-start | bytes 1572868
  219.7 51.7 %slice-start = ((s8[8388608]{0:T(1024)(128)(4,1)}), s8[4194304]{0:T(1024)(128)(4,1)S(1)}, s32[]{:S(2)}) async-start(s8[8388608]{0:T(1024)(128)(4,1)} %bitcast.293), calls=%async_computation.23 | async-start | bytes 8388608
  274.6 11.8 slice-start.2
  276.9 9.5 copy-start.13
  277.0 9.5 slice-start.3
  293.2 54.7 %all-to-all-start.1 = ((bf16[8,256,1024]{2,0,1:T(8,128)(2,1)}), bf16[8,256,1024]{2,0,1:T(8,128)(2,1)}, u32[]{:S(2)}, u32[]{:S(2)}) async-start(bf16[8,256,1024]{2,0,1:T(8,128)(2,1)} %copy.120), calls=%async_computation.1 | async-start | bytes 8388608 | tf_op jit(solution)/shard_map/all_to_all | solution.py:243
  298.4 9.7 copy-start.30
  482.3 53.2 %all-to-all-start.3 = ((bf16[8,256,1024]{2,0,1:T(8,128)(2,1)}), bf16[8,256,1024]{2,0,1:T(8,128)(2,1)}, u32[]{:S(2)}, u32[]{:S(2)}) async-start(bf16[8,256,1024]{2,0,1:T(8,128)(2,1)} %copy.124), calls=%async_computation.3 | async-start | bytes 8388608 | tf_op jit(solution)/shard_map/all_to_all | solution.py:279
  487.3 221.8 %reduce-scatter.7.cloned.1.call-start = ((), (), s32[]{:S(2)}) async-start(), calls=%async_computation.16 | async-start | bytes 4718592 | tf_op jit(solution)/shard_map/reduce_scatter | solution.py:354
  623.2 119.7 %reduce-scatter.15.cloned.1.call-start = ((), (), s32[]{:S(2)}) async-start(), calls=%async_computation.20 | async-start | bytes 2621440 | tf_op jit(solution)/shard_map/reduce_scatter | solution.py:421
  626.6 150.3 %reduce-scatter.9.cloned.1.call-start = ((), (), s32[]{:S(2)}) async-start(), calls=%async_computation.17 | async-start | bytes 2621440 | tf_op jit(solution)/shard_map/reduce_scatter | solution.py:412
  630.4 86.0 %copy-start.2 = (bf16[256,1024]{1,0:T(8,128)(2,1)S(1)}, bf16[256,1024]{1,0:T(8,128)(2,1)}, u32[]{:S(2)}) copy-start(bf16[256,1024]{1,0:T(8,128)(2,1)} %copy-done.1) | copy-start | bytes 1572868
  630.4 174.5 %reduce-scatter.13.cloned.1.call-start = ((), (), s32[]{:S(2)}) async-start(), calls=%async_computation.19 | async-start | bytes 1310720 | tf_op jit(solution)/shard_map/reduce_scatter | solution.py:418
  711.5 121.4 %reduce-scatter.11.cloned.1.call-start = ((), (), s32[]{:S(2)}) async-start(), calls=%async_computation.18 | async-start | bytes 1310720 | tf_op jit(solution)/shard_map/reduce_scatter | solution.py:415
  716.3 139.1 %reduce-scatter.17.cloned.1.call-start = ((), (), s32[]{:S(2)}) async-start(), calls=%async_computation.21 | async-start | bytes 81920 | tf_op jit(solution)/shard_map/reduce_scatter | solution.py:427
  717.3 941.3 %all-reduce.7.cloned.1.call-start = ((), (), s32[]{:S(2)}) async-start(), calls=%async_computation.22 | async-start | bytes 53477376 | tf_op jit(solution)/shard_map/psum | solution.py:403
  (23 other events, 91.1 us)
Sparse Core Ops, SparseCore 0:
  9.6 19.4 all-gather.12
  30.6 16.7 all-gather.8
  48.9 22.5 all-gather.16
  74.0 51.0 all-gather.14
  127.7 47.4 all-gather.10
  176.6 21.0 all-gather.18
  623.3 85.6 reduce-scatter.6
  711.7 31.1 reduce-scatter.14
  745.4 31.4 reduce-scatter.8
  780.0 24.8 reduce-scatter.12
  808.1 24.8 reduce-scatter.10
  835.9 19.4 reduce-scatter.16
  861.9 796.5 all-reduce.6
where the time goes:
time: 1720 us; the launch traced here: 1710 us
  waiting for transfers between devices  1080 us (63%)
  blocking collectives  197 us (11%)
  matrix products  185 us (11%)
  local copies, waits for them, and re-layouts  145 us (8%)
  other arithmetic  72.4 us (4%)
    psum x1, waiting for transfers between devices, on_device(): lax.psum(query_part.astype(jnp.bfloat16), 'ctx').astype(jnp.float32)  761 us
    reduce_scatter x1, waiting for transfers between devices, on_device(): lax.psum_scatter(kv_terms.reshape(group_rows, 2 * KVD).astype(jnp.bfloat1...  78.4 us
    all_to_all x1, blocking collectives, on_device(): lax.all_to_all(dispatch_rows, 'dp', split_axis=0, concat_axis=1, tiled=True)  51.2 us
    all_to_all x1, blocking collectives, on_device(): lax.all_to_all(grad_slots, 'dp', split_axis=0, concat_axis=1, tiled=True)  50.9 us
    all_to_all x1, waiting for transfers between devices, on_device(): lax.all_to_all(grad_expert_in, 'dp', split_axis=1, concat_axis=0, tiled=T...  43.3 us
    all_gather x1, waiting for transfers between devices, on_device(): lax.all_gather(key_rows, 'ctx', axis=0, tiled=True)  41 us
    all_gather x1, blocking collectives, on_device(): lax.all_gather(router_weight, 'dp', axis=0, tiled=True)  39.4 us
    psum x1, blocking collectives, on_device(): lax.psum(gain_one_part.astype(jnp.bfloat16), 'ctx').astype(jnp.float32)  38.7 us
  transfers between devices with their start and end apart: 15, of which 12 were waited for; matrix products, arithmetic and copies ran while one was open for 9% of the time, Pallas kernels for 0%

commit v1 on v0

v1 whole, which is shorter than its diff:
```python
import jax
import jax.numpy as jnp
from jax import lax
from jax.experimental import pallas as pl
from jax.experimental.pallas import tpu as pltpu
from jax.sharding import PartitionSpec as P

EXPERTS = 32
BLOCK = 128
CAP = 64
HEAD = 64
KVD = 512
PAIRS = 4
EPS = 1e-06
NEG = -1e30
F32 = jnp.float32
BF16 = jnp.bfloat16


def dot_nn(a, b):
    return lax.dot_general(a, b, (((1,), (0,)), ((), ())), preferred_element_type=F32)


def dot_nt(a, b):
    return lax.dot_general(a, b, (((1,), (1,)), ((), ())), preferred_element_type=F32)


def dot_tn(a, b):
    return lax.dot_general(a, b, (((0,), (0,)), ((), ())), preferred_element_type=F32)


def vmem():
    return pl.BlockSpec(memory_space=pltpu.VMEM)


def smem():
    return pl.BlockSpec(memory_space=pltpu.SMEM)


def call(body, scalars, arrays, outs, scratch=(), mib=48):
    return pl.pallas_call(
        body,
        in_specs=[smem() for _ in scalars] + [vmem() for _ in arrays],
        out_specs=[vmem() for _ in outs],
        out_shape=[jax.ShapeDtypeStruct(s, d) for s, d in outs],
        scratch_shapes=list(scratch),
        compiler_params=pltpu.CompilerParams(vmem_limit_bytes=mib << 20),
    )(*scalars, *arrays)


def xor_pairs(count, step):
    return [(i, i ^ step) for i in range(count)]


def dp_gather(block, count):
    pieces = {0: block}
    for step in range(2, count, 2):
        pieces[step] = lax.ppermute(block, "dp", xor_pairs(count, step))
    for step in range(0, count, 2):
        pieces[step + 1] = lax.ppermute(pieces[step], "dp", xor_pairs(count, 1))
    return [pieces[s] for s in range(count)]


def dp_reduce(pieces, count):
    kept = {}
    for step in range(0, count, 2):
        other = lax.ppermute(pieces[step + 1], "dp", xor_pairs(count, 1))
        kept[step] = pieces[step].astype(F32) + other.astype(F32)
    total = kept[0]
    for step in range(2, count, 2):
        other = lax.ppermute(kept[step].astype(BF16), "dp", xor_pairs(count, step))
        total = total + other.astype(F32)
    return total


def in_order(pieces, index):
    stacked = jnp.stack(pieces)
    count = len(pieces)
    bit = 1
    while bit < count:
        swapped = jnp.stack([stacked[j ^ bit] for j in range(count)])
        stacked = jnp.where((index & bit) > 0, swapped, stacked)
        bit *= 2
    return stacked


def ring_order(count):
    return [list(range(0, count, 2)) + list(range(count - 1, 0, -2))]


def ring_gather(block, count):
    return lax.all_gather(block, "ctx", axis=0, tiled=True, axis_index_groups=ring_order(count))


def ring_scatter(block, count):
    return lax.psum_scatter(
        block, "ctx", scatter_dimension=0, tiled=True, axis_index_groups=ring_order(count)
    )


def half_swap(tile, first):
    return jnp.where(first, pltpu.roll(tile, 96, 1), pltpu.roll(tile, 32, 1))


def turn(tile, cosine, sine, first):
    return tile * cosine + half_swap(tile, first) * sine


def turn_back(tile, cosine, sine, first):
    return tile * cosine - half_swap(tile, first) * sine


def lanes_of(rows):
    return lax.broadcasted_iota(jnp.int32, (rows, 128), 1)


def spread_heads(tile_a, tile_b):
    low = lanes_of(tile_a.shape[0]) < HEAD
    return jnp.concatenate(
        [
            jnp.where(low, tile_a, 0.0),
            jnp.where(low, pltpu.roll(tile_a, HEAD, 1), 0.0),
            jnp.where(low, 0.0, pltpu.roll(tile_b, HEAD, 1)),
            jnp.where(low, 0.0, tile_b),
        ],
        axis=0,
    )


def join_heads(stacked):
    rows = stacked.shape[0] // 4
    low = lanes_of(rows) < HEAD
    part = [stacked[h * rows : (h + 1) * rows] for h in range(4)]
    return (
        jnp.where(low, part[0], pltpu.roll(part[1], HEAD, 1)),
        jnp.where(low, pltpu.roll(part[2], HEAD, 1), part[3]),
    )


def norm_back(grad, normed, inverse, gain):
    scaled = grad * gain
    return inverse * (scaled - normed * jnp.mean(scaled * normed, axis=-1, keepdims=True))


def kv_body(count):
    def body(me_ref, x_ref, gain_ref, cos_ref, sin_ref, *rest):
        weights, (kv_ref, act_ref) = rest[:count], rest[count:]
        x = x_ref[...].astype(F32)
        inverse = lax.rsqrt(jnp.mean(x * x, axis=-1, keepdims=True) + EPS)
        act = (x * inverse * gain_ref[...]).astype(BF16)
        width = x.shape[1] // count
        for b in range(count):
            act_ref[b] = act[:, b * width : (b + 1) * width]
        me = me_ref[0]
        total = dot_nn(act_ref[me], weights[0][...])
        for s in range(1, count):
            total = total + dot_nn(act_ref[me ^ s], weights[s][...])
        first = (lanes_of(x.shape[0]) & 63) < 32
        cosine, sine = cos_ref[...], sin_ref[...]
        for j in range(KVD // 128):
            tile = total[:, j * 128 : (j + 1) * 128]
            kv_ref[:, j * 128 : (j + 1) * 128] = turn(tile, cosine, sine, first).astype(BF16)
        kv_ref[:, KVD:] = total[:, KVD:].astype(BF16)

    return body


def query_body(count):
    def body(me_ref, act_ref, cos_ref, sin_ref, *rest):
        weights, q_ref = rest[:count], rest[count]
        me = me_ref[0]
        total = dot_nn(act_ref[me], weights[0][...])
        for s in range(1, count):
            total = total + dot_nn(act_ref[me ^ s], weights[s][...])
        first = (lanes_of(total.shape[0]) & 63) < 32
        cosine, sine = cos_ref[...], sin_ref[...]
        for j in range(total.shape[1] // 128):
            tile = total[:, j * 128 : (j + 1) * 128]
            turned = turn(tile, cosine, sine, first).astype(BF16)
            q_ref[:, j * 128 : (j + 1) * 128] = turned * (1.0 / HEAD)

    return body


def visible(place_block, key_block, starts):
    rows = lax.broadcasted_iota(jnp.int32, (BLOCK, BLOCK), 0) + place_block * BLOCK
    keys = lax.broadcasted_iota(jnp.int32, (BLOCK, BLOCK), 1) + key_block * BLOCK
    return (keys <= rows) & (keys >= starts)


def attend_body(low_ref, high_ref, where_ref, q_ref, kv_ref, starts_ref, o_ref, ext_ref, qs, ms, ls, accs):
    low_half = lanes_of(BLOCK) < HEAD
    for qb in range(q_ref.shape[0] // BLOCK):
        rows = slice(qb * BLOCK, (qb + 1) * BLOCK)
        for j in range(PAIRS):
            qs[j] = spread_heads(
                q_ref[rows, 256 * j : 256 * j + 128].astype(F32),
                q_ref[rows, 256 * j + 128 : 256 * j + 256].astype(F32),
            ).astype(BF16)
        ms[...] = jnp.full(ms.shape, NEG, F32)
        ls[...] = jnp.zeros(ls.shape, F32)
        accs[...] = jnp.zeros(accs.shape, F32)
        high = high_ref[qb]

        def step(b, carry):
            at = pl.multiple_of(where_ref[b] * BLOCK, BLOCK)
            seen = visible(high, b, starts_ref[rows, :])[None]
            for j in range(PAIRS):
                key = kv_ref[pl.ds(at, BLOCK), 128 * j : 128 * j + 128]
                value = kv_ref[pl.ds(at, BLOCK), KVD + 128 * j : KVD + 128 * j + 128]
                scores = dot_nt(qs[j], key).reshape(4, BLOCK, BLOCK)
                scores = jnp.where(seen, scores, NEG).reshape(4 * BLOCK, BLOCK)
                old = ms[j]
                new = jnp.maximum(old, jnp.max(scores, axis=-1, keepdims=True))
                weights = jnp.exp(scores - new)
                shrink = jnp.exp(old - new)
                ls[j] = ls[j] * shrink + jnp.sum(weights, axis=-1, keepdims=True)
                accs[j] = accs[j] * shrink + dot_nn(weights.astype(BF16), value)
                ms[j] = new
            return carry

        lax.fori_loop(low_ref[qb], high + 1, step, 0)
        for j in range(PAIRS):
            attended = accs[j] / ls[j]
            total = ms[j] + jnp.log(ls[j])
            left, right = join_heads(attended)
            o_ref[rows, 256 * j : 256 * j + 128] = left.astype(BF16)
            o_ref[rows, 256 * j + 128 : 256 * j + 256] = right.astype(BF16)
            for h in range(4):
                part = slice(h * BLOCK, (h + 1) * BLOCK)
                keep = low_half if h < 2 else jnp.logical_not(low_half)
                ext_ref[j, h, rows, :] = jnp.where(keep, attended[part], total[part])


def attend_back_body(
    low_ref, high_ref, where_ref, q_ref, kv_ref, starts_ref, go_ref, ext_ref, cos_ref, sin_ref,
    gq_ref, dkv_ref, qs, gs, ds, lse, dqs, sums,
):
    first = (lanes_of(BLOCK) & 63) < 32
    sums[...] = jnp.zeros(sums.shape, F32)
    for qb in range(q_ref.shape[0] // BLOCK):
        rows = slice(qb * BLOCK, (qb + 1) * BLOCK)
        for j in range(PAIRS):
            cols = slice(256 * j, 256 * j + 128), slice(256 * j + 128, 256 * j + 256)
            qs[j] = spread_heads(
                q_ref[rows, cols[0]].astype(F32), q_ref[rows, cols[1]].astype(F32)
            ).astype(BF16)
            grad = spread_heads(
                go_ref[rows, cols[0]].astype(F32), go_ref[rows, cols[1]].astype(F32)
            )
            gs[j] = grad.astype(BF16)
            for h in range(4):
                part = slice(h * BLOCK, (h + 1) * BLOCK)
                ext = ext_ref[j, h, rows, :]
                ds[j, part, :] = jnp.sum(grad[part] * ext, axis=-1, keepdims=True)
                lse[j, part, :] = ext[:, 127:128] if h < 2 else ext[:, 0:1]
        dqs[...] = jnp.zeros(dqs.shape, F32)
        high = high_ref[qb]

        def step(b, carry):
            at = pl.multiple_of(where_ref[b] * BLOCK, BLOCK)
            seen = visible(high, b, starts_ref[rows, :])[None]
            for j in range(PAIRS):
                kcols = slice(128 * j, 128 * j + 128)
                vcols = slice(KVD + 128 * j, KVD + 128 * j + 128)
                key = kv_ref[pl.ds(at, BLOCK), kcols]
                value = kv_ref[pl.ds(at, BLOCK), vcols]
                scores = dot_nt(qs[j], key).reshape(4, BLOCK, BLOCK)
                scores = jnp.where(seen, scores, NEG).reshape(4 * BLOCK, BLOCK)
                weights = jnp.exp(scores - lse[j])
                grad = dot_nt(gs[j], value)
                score_grad = (weights * (grad - ds[j])).astype(BF16)
                dqs[j] += dot_nn(score_grad, key)
                sums[pl.ds(at, BLOCK), kcols] += dot_tn(score_grad, qs[j])
                sums[pl.ds(at, BLOCK), vcols] += dot_tn(weights.astype(BF16), gs[j])
            return carry

        lax.fori_loop(low_ref[qb], high + 1, step, 0)
        cosine, sine = cos_ref[rows, :], sin_ref[rows, :]
        for j in range(PAIRS):
            left, right = join_heads(dqs[j] * (1.0 / HEAD))
            gq_ref[rows, 256 * j : 256 * j + 128] = turn_back(left, cosine, sine, first).astype(BF16)
            gq_ref[rows, 256 * j + 128 : 256 * j + 256] = turn_back(right, cosine, sine, first).astype(
                BF16
            )
    dkv_ref[...] = sums[...].astype(BF16)


def mix_body(count):
    def body(me_ref, x_ref, o_ref, gain_ref, *rest):
        weights, (mixed_ref, act_ref, parts) = rest[:count], rest[count:]
        width = o_ref.shape[1] // count
        for b in range(count):
            parts[b] = o_ref[:, b * width : (b + 1) * width]
        me = me_ref[0]
        total = x_ref[...].astype(F32)
        for s in range(count):
            total = total + dot_nn(parts[me ^ s], weights[s][...])
        mixed_ref[...] = total
        inverse = lax.rsqrt(jnp.mean(total * total, axis=-1, keepdims=True) + EPS)
        act_ref[...] = (total * inverse * gain_ref[...]).astype(BF16)

    return body


def expert_body(count, local, rows):
    slots = local * CAP

    def body(me_ref, *refs):
        acts, grads = refs[:count], refs[count : 2 * count]
        slot_ref, hit_ref, router_ref, wg_ref, wu_ref, wd_ref = refs[2 * count : 2 * count + 6]
        (gg_ref, ug_ref, dg_ref, gate_out, dgate_ref) = refs[2 * count + 6 : 2 * count + 11]
        youts = refs[2 * count + 11 : 3 * count + 11]
        gouts = refs[3 * count + 11 : 4 * count + 11]
        gate_all, xe, gyx, dye, picks, ys, dxs = refs[4 * count + 11 :]
        e = pl.program_id(0)

        @pl.when(e == 0)
        def _():
            for s in range(count):
                part = slice(s * rows, (s + 1) * rows)
                logits = dot_nt(router_ref[...], acts[s][...])
                hit = hit_ref[:, part] > 0
                logits = jnp.where(hit, logits, NEG)
                top = jnp.max(logits, axis=0, keepdims=True)
                raised = jnp.where(hit, jnp.exp(logits - top), 0.0)
                gates = raised / jnp.sum(raised, axis=0, keepdims=True)
                gate_all[:, part] = gates
                if s == 0:
                    gate_out[...] = gates

        slot_row = slot_ref[0]
        gate_row = gate_all[pl.ds(me_ref[0] * local + e, 1), :]
        slot_id = lax.broadcasted_iota(jnp.int32, (CAP, rows), 0)
        at = pl.multiple_of(e * CAP, CAP)
        slot_gates = []
        for s in range(count):
            part = slice(s * rows, (s + 1) * rows)
            put = slice(s * CAP, (s + 1) * CAP)
            hits = slot_id == slot_row[:, part]
            pick = jnp.where(hits, 1.0, 0.0).astype(BF16)
            picks[s, pl.ds(at, CAP), :] = pick
            gate = jnp.sum(jnp.where(hits, gate_row[:, part], 0.0), axis=1, keepdims=True)
            slot_gates.append(gate)
            xe[put, :] = dot_nn(pick, acts[s][...]).astype(BF16)
            picked = dot_nn(pick, grads[s][...])
            gyx[put, :] = picked.astype(BF16)
            dye[put, :] = (gate * picked).astype(BF16)
        gate_part = dot_nn(xe[...], wg_ref[0])
        up_part = dot_nn(xe[...], wu_ref[0])
        sig = jax.nn.sigmoid(gate_part)
        act = gate_part * sig
        hidden = (act * up_part).astype(BF16)
        out = dot_nn(hidden, wd_ref[0]).astype(BF16).astype(F32)
        slot_dot = jnp.sum(gyx[...].astype(F32) * out, axis=1, keepdims=True)
        for s in range(count):
            part = slice(s * rows, (s + 1) * rows)
            put = slice(s * CAP, (s + 1) * CAP)
            hits = slot_id == slot_row[:, part]
            dgate_ref[0, :, part] = jnp.sum(jnp.where(hits, slot_dot[put], 0.0), axis=0, keepdims=True)
            ys[s, pl.ds(at, CAP), :] = (slot_gates[s] * out[put]).astype(BF16)
        dg_ref[0] = dot_tn(hidden, dye[...]).astype(BF16)
        grad_hidden = dot_nt(dye[...], wd_ref[0])
        grad_gate = (grad_hidden * up_part * sig * (1.0 + gate_part * (1.0 - sig))).astype(BF16)
        grad_up = (grad_hidden * act).astype(BF16)
        gg_ref[0] = dot_tn(xe[...], grad_gate).astype(BF16)
        ug_ref[0] = dot_tn(xe[...], grad_up).astype(BF16)
        grad_in = (dot_nt(grad_gate, wg_ref[0]) + dot_nt(grad_up, wu_ref[0])).astype(BF16)
        for s in range(count):
            dxs[s, pl.ds(at, CAP), :] = grad_in[s * CAP : (s + 1) * CAP]

        @pl.when(e == local - 1)
        def _():
            for s in range(count):
                youts[s][...] = dot_tn(picks[s], ys[s]).astype(BF16)
                gouts[s][...] = dot_tn(picks[s], dxs[s]).astype(BF16)

    def run(me, acts, grads, slots_t, hits, router_t, wg, wu, wd):
        wide = acts[0].shape[1]
        inner = wg.shape[2]
        whole = lambda shape: pl.BlockSpec(shape, lambda e: tuple(0 for _ in shape))
        each = lambda shape: pl.BlockSpec(
            (1,) + shape, lambda e: (e,) + tuple(0 for _ in shape)
        )
        tokens = count * rows
        shape = jax.ShapeDtypeStruct
        res = pl.pallas_call(
            body,
            grid=(local,),
            in_specs=[smem()]
            + [whole((rows, wide)) for _ in range(2 * count)]
            + [
                each((1, tokens)),
                whole((EXPERTS, tokens)),
                whole((EXPERTS, wide)),
                each((wide, inner)),
                each((wide, inner)),
                each((inner, wide)),
            ],
            out_specs=[
                each((wide, inner)),
                each((wide, inner)),
                each((inner, wide)),
                whole((EXPERTS, rows)),
                each((1, tokens)),
            ]
            + [whole((rows, wide)) for _ in range(2 * count)],
            out_shape=[
                shape((local, wide, inner), BF16),
                shape((local, wide, inner), BF16),
                shape((local, inner, wide), BF16),
                shape((EXPERTS, rows), F32),
                shape((local, 1, tokens), F32),
            ]
            + [shape((rows, wide), BF16) for _ in range(2 * count)],
            scratch_shapes=[
                pltpu.VMEM((EXPERTS, tokens), F32),
                pltpu.VMEM((count * CAP, wide), BF16),
                pltpu.VMEM((count * CAP, wide), BF16),
                pltpu.VMEM((count * CAP, wide), BF16),
                pltpu.VMEM((count, slots, rows), BF16),
                pltpu.VMEM((count, slots, wide), BF16),
                pltpu.VMEM((count, slots, wide), BF16),
            ],
            compiler_params=pltpu.CompilerParams(
                vmem_limit_bytes=56 << 20, dimension_semantics=("arbitrary",)
            ),
        )(me, *acts, *grads, slots_t, hits, router_t, wg, wu, wd)
        return (
            res[:3],
            res[3],
            res[4],
            res[5 : 5 + count],
            res[5 + count :],
        )

    return run


def after_body(count):
    def body(
        me_ref, mixed_ref, ga_ref, gy_ref, gain_ref, gates_ref, dgate_ref, router_ref, act_ref, o_ref,
        *rest,
    ):
        weights = rest[:count]
        gy1_ref, go_ref, rgrad_ref, ggrad_ref = rest[count : count + 4]
        wgrads = rest[count + 4 : 2 * count + 4]
        parts, gparts = rest[2 * count + 4 :]
        gates, dgate = gates_ref[...], dgate_ref[...]
        dlogits = gates * (dgate - jnp.sum(gates * dgate, axis=0, keepdims=True))
        dlogits = dlogits.astype(BF16)
        grad = ga_ref[...] + dot_tn(dlogits, router_ref[...])
        rgrad_ref[...] = dot_nn(dlogits, act_ref[...])
        mixed = mixed_ref[...]
        inverse = lax.rsqrt(jnp.mean(mixed * mixed, axis=-1, keepdims=True) + EPS)
        normed = mixed * inverse
        ggrad_ref[...] = jnp.sum(grad * normed, axis=0, keepdims=True)
        gy1 = gy_ref[...] + norm_back(grad, normed, inverse, gain_ref[...])
        gy1_ref[...] = gy1
        low = gy1.astype(BF16)
        me = me_ref[0]
        width = o_ref.shape[1] // count
        for b in range(count):
            parts[b] = o_ref[:, b * width : (b + 1) * width]
        for s in range(count):
            gparts[me ^ s] = dot_nt(low, weights[s][...]).astype(BF16)
            wgrads[s][...] = dot_tn(parts[me ^ s], low).astype(BF16)
        for b in range(count):
            go_ref[:, b * width : (b + 1) * width] = gparts[b]

    return body


def first_body(count):
    def body(me_ref, x_ref, gain_ref, cos_ref, sin_ref, act_ref, gq_ref, dkv_ref, gy1_ref, *rest):
        wq, wkv = rest[:count], rest[count : 2 * count]
        in_ref, ggrad_ref = rest[2 * count : 2 * count + 2]
        qgrads = rest[2 * count + 2 : 3 * count + 2]
        kgrads = rest[3 * count + 2 : 4 * count + 2]
        gkv, gparts = rest[4 * count + 2 :]
        rows = x_ref.shape[0]
        first = (lanes_of(rows) & 63) < 32
        cosine, sine = cos_ref[...], sin_ref[...]
        for j in range(KVD // 128):
            tile = dkv_ref[:, j * 128 : (j + 1) * 128].astype(F32)
            gkv[:, j * 128 : (j + 1) * 128] = turn_back(tile, cosine, sine, first).astype(BF16)
        gkv[:, KVD:] = dkv_ref[:, KVD:].astype(BF16)
        me = me_ref[0]
        gq = gq_ref[...]
        for s in range(count):
            gparts[me ^ s] = dot_nt(gq, wq[s][...]) + dot_nt(gkv[...], wkv[s][...])
            qgrads[s][...] = dot_tn(act_ref[me ^ s], gq).astype(BF16)
            kgrads[s][...] = dot_tn(act_ref[me ^ s], gkv[...]).astype(BF16)
        grad = jnp.concatenate([gparts[b] for b in range(count)], axis=1)
        x = x_ref[...].astype(F32)
        inverse = lax.rsqrt(jnp.mean(x * x, axis=-1, keepdims=True) + EPS)
        normed = x * inverse
        ggrad_ref[...] = jnp.sum(grad * normed, axis=0, keepdims=True)
        in_ref[...] = gy1_ref[...] + norm_back(grad, normed, inverse, gain_ref[...])

    return body


def make(n_dp, n_ctx):
    def on_device(
        layer_input, query_weight, key_weight, value_weight, out_weight, attn_gain, router_weight,
        moe_gain, gate_weight, up_weight, down_weight, expert_ids, fill_order, block_deal,
        seq_lengths, out_grad,
    ):
        rows, wide = layer_input.shape
        local = gate_weight.shape[0]
        width = wide // n_dp
        me_dp = lax.axis_index("dp").astype(jnp.int32)
        me_ctx = lax.axis_index("ctx").astype(jnp.int32)
        me = me_dp.reshape(1)
        near = rows // BLOCK

        wkv = dp_gather(jnp.concatenate([key_weight, value_weight], axis=1), n_dp)
        small = jnp.concatenate(
            [
                router_weight.T,
                attn_gain[None, :],
                moe_gain[None, :],
                jnp.zeros((14, width), BF16),
            ],
            axis=0,
        )
        small = in_order(dp_gather(small, n_dp), me_dp)
        small = small.transpose(1, 0, 2).reshape(EXPERTS + 16, wide)
        router_t = small[:EXPERTS]
        gain_one = small[EXPERTS : EXPERTS + 1].astype(F32)
        gain_two = small[EXPERTS + 1 : EXPERTS + 2].astype(F32)
        wq = dp_gather(query_weight, n_dp)

        deal, lengths = block_deal[0], seq_lengths[0]
        blocks = deal.shape[0]
        ends = jnp.cumsum(lengths, dtype=jnp.int32)
        mine = lax.dynamic_slice_in_dim(deal, me_ctx * near, near)
        places = (mine[:, None] * BLOCK + jnp.arange(BLOCK, dtype=jnp.int32)[None, :]).reshape(rows, 1)
        starts = jnp.sum(
            jnp.where(places >= ends[None, :], lengths[None, :], 0), axis=1, keepdims=True, dtype=jnp.int32
        )
        relative = (places - starts).astype(F32)
        lane = jnp.arange(128, dtype=jnp.int32)
        inverse = 10000.0 ** (-(lane % 32).astype(F32) * (2.0 / HEAD))
        angles = relative * inverse[None, :]
        cosine = jnp.cos(angles)
        sine = jnp.sin(angles) * jnp.where(lane % 64 < 32, -1.0, 1.0)[None, :]
        block_starts = jnp.sum(
            jnp.where((mine * BLOCK)[:, None] >= ends[None, :], lengths[None, :], 0), axis=1, dtype=jnp.int32
        )
        low_blocks = block_starts // BLOCK
        ring = jnp.array(ring_order(n_ctx)[0], jnp.int32)
        ring_deal = deal.reshape(n_ctx, near)[ring].reshape(blocks)
        held = jnp.arange(blocks, dtype=jnp.int32)
        where_block = jnp.sum(
            jnp.where(ring_deal[None, :] == held[:, None], held[None, :], 0), axis=1, dtype=jnp.int32
        )

        kv_mine, act_one = call(
            kv_body(n_dp),
            [me],
            [layer_input, gain_one, cosine, sine] + wkv,
            [((rows, 2 * KVD), BF16), ((n_dp, rows, width), BF16)],
        )
        every_kv = ring_gather(kv_mine, n_ctx)
        (query,) = call(query_body(n_dp), [me], [act_one, cosine, sine] + wq, [((rows, wide), BF16)])
        wo = dp_gather(out_weight, n_dp)

        ids = jnp.stack(dp_gather(expert_ids.T, n_dp))
        fill = jnp.stack(dp_gather(fill_order, n_dp))
        names = jnp.arange(EXPERTS, dtype=jnp.int32)
        hits = jnp.sum((ids[:, :, None, :] == names[None, None, :, None]).astype(F32), axis=1)
        earlier = (fill[:, 0, :, None] < fill[:, 0, None, :]).astype(BF16)
        prior = jnp.einsum(
            "set,stu->seu", hits.astype(BF16), earlier, preferred_element_type=F32
        )
        slot = jnp.where((hits > 0) & (prior < CAP), prior, -1.0).astype(jnp.int32)
        slot = lax.dynamic_slice_in_dim(slot, me_dp * local, local, axis=1)
        slots_t = slot.transpose(1, 0, 2).reshape(local, 1, n_dp * rows)
        hits_t = hits.transpose(1, 0, 2).reshape(EXPERTS, n_dp * rows)
        grads_all = dp_gather(out_grad.astype(BF16), n_dp)

        attended, extended = call(
            attend_body,
            [low_blocks, mine, where_block],
            [query, every_kv, starts],
            [((rows, wide), BF16), ((PAIRS, 4, rows, 128), F32)],
            [
                pltpu.VMEM((PAIRS, 4 * BLOCK, 128), BF16),
                pltpu.VMEM((PAIRS, 4 * BLOCK, 1), F32),
                pltpu.VMEM((PAIRS, 4 * BLOCK, 1), F32),
                pltpu.VMEM((PAIRS, 4 * BLOCK, 128), F32),
            ],
        )
        mixed, act_two = call(
            mix_body(n_dp),
            [me],
            [layer_input, attended, gain_two] + wo,
            [((rows, wide), F32), ((rows, wide), BF16)],
            [pltpu.VMEM((n_dp, rows, width), BF16)],
        )

        acts_all = dp_gather(act_two, n_dp)
        weight_grads, gates, dgates, y_parts, g_parts = expert_body(n_dp, local, rows)(
            me, acts_all, grads_all, slots_t, hits_t, router_t, gate_weight, up_weight, down_weight
        )

        expert_sums = []
        scattered = [
            ring_scatter(g.reshape(-1, g.shape[2]), n_ctx) for g in weight_grads
        ]
        for g, part in zip(weight_grads, scattered):
            expert_sums.append(ring_gather(part, n_ctx).reshape(g.shape).astype(F32))

        back = [dgates[:, 0, s * rows : (s + 1) * rows] for s in range(n_dp)]
        back = [back[0]] + [lax.ppermute(back[s], "dp", xor_pairs(n_dp, s)) for s in range(1, n_dp)]
        dgate_t = in_order(back, me_dp).reshape(EXPERTS, rows)
        grad_act_two = dp_reduce(g_parts, n_dp)
        layer_output = mixed + dp_reduce(y_parts, n_dp)
        res = call(
            after_body(n_dp),
            [me],
            [mixed, grad_act_two, out_grad, gain_two, gates, dgate_t, router_t, act_two, attended] + wo,
            [((rows, wide), F32), ((rows, wide), BF16), ((EXPERTS, wide), F32), ((1, wide), F32)]
            + [((width, wide), BF16)] * n_dp,
            [pltpu.VMEM((n_dp, rows, width), BF16), pltpu.VMEM((n_dp, rows, width), BF16)],
        )
        grad_mixed, grad_heads, router_part, gain_two_part = res[:4]
        out_parts = res[4:]
        grad_query, kv_grads = call(
            attend_back_body,
            [low_blocks, mine, where_block],
            [query, every_kv, starts, grad_heads, extended, cosine, sine],
            [((rows, wide), BF16), ((blocks * BLOCK, 2 * KVD), BF16)],
            [
                pltpu.VMEM((PAIRS, 4 * BLOCK, 128), BF16),
                pltpu.VMEM((PAIRS, 4 * BLOCK, 128), BF16),
                pltpu.VMEM((PAIRS, 4 * BLOCK, 1), F32),
                pltpu.VMEM((PAIRS, 4 * BLOCK, 1), F32),
                pltpu.VMEM((PAIRS, 4 * BLOCK, 128), F32),
                pltpu.VMEM((blocks * BLOCK, 2 * KVD), F32),
            ],
        )
        kv_grad = ring_scatter(kv_grads, n_ctx)
        res = call(
            first_body(n_dp),
            [me],
            [layer_input, gain_one, cosine, sine, act_one, grad_query, kv_grad, grad_mixed] + wq + wkv,
            [((rows, wide), F32), ((1, wide), F32)]
            + [((width, wide), BF16)] * n_dp
            + [((width, 2 * KVD), BF16)] * n_dp,
            [pltpu.VMEM((rows, 2 * KVD), BF16), pltpu.VMEM((n_dp, rows, width), F32)],
        )
        input_grad, gain_one_part = res[:2]
        q_parts, kv_parts = res[2 : 2 + n_dp], res[2 + n_dp :]

        dense = jnp.concatenate(
            [dp_reduce(part, n_dp).astype(BF16) for part in (out_parts, q_parts, kv_parts)], axis=0
        )
        dense = ring_gather(ring_scatter(dense, n_ctx), n_ctx).astype(F32)
        tiny = jnp.concatenate([router_part, gain_one_part, gain_two_part], axis=0)
        for step in [1 << b for b in range(n_ctx.bit_length() - 1)]:
            tiny = tiny + lax.ppermute(tiny, "ctx", xor_pairs(n_ctx, step))
        for step in [1 << b for b in range(n_dp.bit_length() - 1)]:
            tiny = tiny + lax.ppermute(tiny, "dp", xor_pairs(n_dp, step))
        tiny = lax.dynamic_slice_in_dim(tiny, me_dp * width, width, axis=1)
        return (
            layer_output,
            input_grad,
            dense[width : 2 * width],
            dense[2 * width :, :KVD],
            dense[2 * width :, KVD:],
            dense[:width],
            tiny[EXPERTS],
            tiny[:EXPERTS].T,
            tiny[EXPERTS + 1],
            expert_sums[0],
            expert_sums[1],
            expert_sums[2],
        )

    return on_device


def solution(mesh):
    rows2 = P(("dp", "ctx"), None)
    mat = P("dp", None)
    cube = P("dp", None, None)
    in_specs = (
        rows2, mat, mat, mat, mat, P("dp"), mat, P("dp"), cube, cube, cube, rows2, rows2, mat, mat, rows2,
    )
    out_specs = (rows2, rows2, mat, mat, mat, mat, P("dp"), mat, P("dp"), cube, cube, cube)
    return jax.shard_map(
        make(mesh.shape["dp"], mesh.shape["ctx"]),
        mesh=mesh,
        in_specs=in_specs,
        out_specs=out_specs,
        check_vma=False,
    )
```

time: 1720 us -> 963 us (0.56)
  waiting for transfers between devices: 1080 us -> 723 us
  blocking collectives: 197 us -> 0 us
  matrix products: 185 us -> 0.34 us
  local copies, waits for them, and re-layouts: 145 us -> 23 us
  Pallas kernels: 0 us -> 114 us
  other arithmetic: 72.4 us -> 55 us
    psum x1 -> x0, waiting for transfers between devices: 761 us -> none  [on_device(): lax.psum(query_part.astype(jnp.bfloat16), 'ctx').astype(jnp.float32)]
    dot_general x56 -> x1, matrix products: 185 us -> 0.34 us  [on_device(): jnp.einsum('set,stu->seu', hits.astype(BF16), earlier, preferred_element_...]
    reduce_scatter x6 -> x5, waiting for transfers between devices: 182 us -> 358 us  [ring_scatter(): lax.psum_scatter(block, 'ctx', scatter_dimension=0, tiled=True, axis_inde...]
    all_gather x6 -> x5, waiting for transfers between devices: 92.9 us -> 252 us  [ring_gather(): lax.all_gather(block, 'ctx', axis=0, tiled=True, axis_index_groups=ring_o...]
    pallas_call x0 -> x8, Pallas kernels: none -> 114 us  [the longest x7 74 us: call(): pl.pallas_call(body, in_specs=[smem() for _ in scalars] + [vmem() for _ i...]
    ppermute x0 -> x47, waiting for transfers between devices: none -> 111 us  [the longest x8 36.6 us: dp_gather(): pieces[step] = lax.ppermute(block, 'dp', xor_pairs(count, step))]
    all_to_all x2 -> x0, blocking collectives: 102 us -> none  [the longest x1 51.2 us: on_device(): lax.all_to_all(dispatch_rows, 'dp', split_axis=0, concat_axis=1, tiled=True)]
    gather x5 -> x1, local copies, waits for them, and re-layouts: 59.6 us -> 0.56 us  [on_device(): ring_deal = deal.reshape(n_ctx, near)[ring].reshape(blocks)]
  transfers between devices with their start and end apart: 15 -> 57, of which waited for: 12 -> 30; matrix products, arithmetic and copies ran while one was open for 9% -> 5% of each run, Pallas kernels for 0% -> 4%
where the time goes in v1:
time: 963 us; the launch traced here: 957 us
  waiting for transfers between devices  723 us (75%)
  Pallas kernels  114 us (12%)
  other arithmetic  55 us (6%)
  starting transfers between devices  27.3 us (3%)
  local copies, waits for them, and re-layouts  23 us (2%)
  between operations  15.3 us (2%)
    reduce_scatter x5, waiting for transfers between devices, ring_scatter(): lax.psum_scatter(block, 'ctx', scatter_dimension=0, tiled=True, axis_inde...  358 us
    all_gather x5, waiting for transfers between devices, ring_gather(): lax.all_gather(block, 'ctx', axis=0, tiled=True, axis_index_groups=ring_o...  252 us
    pallas_call x7, Pallas kernels, call(): pl.pallas_call(body, in_specs=[smem() for _ in scalars] + [vmem() for _ i...  74 us
    pallas_call x1, Pallas kernels, run(): pl.pallas_call(body, grid=(local,), in_specs=[smem()] + [whole((rows, wid...  39.7 us
    ppermute x8, waiting for transfers between devices, dp_gather(): pieces[step] = lax.ppermute(block, 'dp', xor_pairs(count, step))  36.6 us
    convert_element_type x3, other arithmetic, on_device(): expert_sums.append(ring_gather(part, n_ctx).reshape(g.shape).astype(F32))  35.5 us
    ppermute x5, waiting for transfers between devices, dp_reduce(): other = lax.ppermute(kept[step].astype(BF16), 'dp', xor_pairs(count, step))  31.6 us
    ppermute x3, waiting for transfers between devices, on_device(): tiny = tiny + lax.ppermute(tiny, 'ctx', xor_pairs(n_ctx, step))  21.3 us
  transfers between devices with their start and end apart: 57, of which 30 were waited for; matrix products, arithmetic and copies ran while one was open for 5% of the time, Pallas kernels for 4%

profile of v1, /device:TPU:0, one launch (start us, length us, event | category | flops | bytes accessed | tf_op | source)
XLA Modules:
  0.0 957.1 jit_solution(1953912413115035315)
XLA Ops:
  9.5 3.0 collective-permute-start.1
  19.4 9.4 collective-permute-done.4.rest_2_.rest_6_
  41.1 8.7 collective-permute-done.7.rest_2_
  49.8 11.2 %collective-permute-done.10.rest_2_ = bf16[256,1024]{1,0:T(8,128)(2,1)} collective-permute-done((bf16[256,1024]{1,0:T(8,128)(2,1)}, bf16[256,1024]{1,0:T(8,128)(2,1)}, u32[]{:S(2)}, u32[]{:S(2)}) %collective-permute-start.10) | collective-permute-done | bytes 524320 | tf_op jit(solution)/shard_map/ppermute | solution.py:58
  66.1 2.6 shard_map.257.q_ref
  68.7 14.4 %all-gather.6.cloned.1.call-done.kv_ref = bf16[2048,1024]{1,0:T(8,128)(2,1)} async-done(((bf16[256,1024]{1,0:T(8,128)(2,1)}), bf16[2048,1024]{1,0:T(8,128)(2,1)}) %all-gather.6.cloned.1.call-update) | async-done | bytes 4194320 | tf_op jit(solution)/shard_map/all_gather | solution.py:92
  83.8 29.9 %shard_map.258 = (bf16[256,1024]{1,0:T(8,128)(2,1)S(1)}, f32[4,4,256,128]{3,2,1,0:T(8,128)S(1)}) custom-call(s32[2]{0:T(128)S(1)} %copy-done.21, s32[2]{0:T(128)S(1)} %get-tuple-element.91.high_ref, s32[16]{0:T(128)S(1)} %select_reduce_fusion.where_ref, bf16[256,1024]{1,0:T(8,128)(2,1)S(1)} %shard_map.257.q_ref, ...), custom_call_target="tpu_custom_call" | custom-call | tf_op jit(solution)/shard_map/pallas_call | solution.py:41
  120.5 7.2 collective-permute-done.22
  134.5 39.7 %shard_map.260 = (bf16[8,1024,512]{2,1,0:T(8,128)(2,1)}, bf16[8,1024,512]{2,1,0:T(8,128)(2,1)}, bf16[8,512,1024]{2,1,0:T(8,128)(2,1)}, f32[32,256]{1,0:T(8,128)}...) custom-call(s32[1]{0:T(128)} %bitcast.me_ref, ...), custom_call_target="tpu_custom_call" | custom-call | tf_op jit(solution)/shard_map/pallas_call | solution.py:387
  180.6 11.4 %collective-permute-done.32 = f32[8,256]{1,0:T(8,128)S(1)} collective-permute-done((f32[8,256]{1,0:T(8,128)S(1)}, f32[8,256]{1,0:T(8,128)S(1)}, u32[]{:S(2)}, u32[]{:S(2)}) %collective-permute-start.32) | collective-permute-done | bytes 8224 | tf_op jit(solution)/shard_map/ppermute | solution.py:617
  192.1 2.4 convert_add_fusion.ga_ref
  194.6 5.4 shard_map.261
  200.8 25.4 %shard_map.262 = (bf16[256,1024]{1,0:T(8,128)(2,1)S(1)}, bf16[2048,1024]{1,0:T(8,128)(2,1)}) custom-call(s32[2]{0:T(128)S(1)} %copy-done.22, s32[2]{0:T(128)S(1)} %get-tuple-element.91.high_ref, s32[16]{0:T(128)S(1)} %select_reduce_fusion.where_ref, bf16[256,1024]{1,0:T(8,128)(2,1)S(1)} %shard_map.257.q_ref, ...), custom_call_target="tpu_custom_call" | custom-call | tf_op jit(solution)/shard_map/pallas_call | solution.py:41
  226.4 57.2 %reduce-scatter.6.cloned.1.call-done.dkv_ref = bf16[256,1024]{1,0:T(8,128)(2,1)} async-done(((bf16[2048,1024]{1,0:T(8,128)(2,1)}), bf16[256,1024]{1,0:T(8,128)(2,1)}) %reduce-scatter.6.cloned.1.call-update) | async-done | bytes 524304 | tf_op jit(solution)/shard_map/reduce_scatter | solution.py:96
  283.6 6.4 shard_map.263
  296.5 10.2 %collective-permute-done.35 = bf16[256,1024]{1,0:T(8,128)(2,1)S(1)} collective-permute-done((bf16[256,1024]{1,0:T(8,128)(2,1)S(1)}, bf16[256,1024]{1,0:T(8,128)(2,1)S(1)}, u32[]{:S(2)}, u32[]{:S(2)}) %collective-permute-start.35) | collective-permute-done | bytes 524320 | tf_op jit(solution)/shard_map/ppermute | solution.py:71
  307.0 10.9 %collective-permute-done.38 = bf16[256,1024]{1,0:T(8,128)(2,1)S(1)} collective-permute-done((bf16[256,1024]{1,0:T(8,128)(2,1)S(1)}, bf16[256,1024]{1,0:T(8,128)(2,1)S(1)}, u32[]{:S(2)}, u32[]{:S(2)}) %collective-permute-start.38) | collective-permute-done | bytes 524320 | tf_op jit(solution)/shard_map/ppermute | solution.py:71
  318.2 10.5 %collective-permute-done.41 = bf16[256,1024]{1,0:T(8,128)(2,1)S(1)} collective-permute-done((bf16[256,1024]{1,0:T(8,128)(2,1)S(1)}, bf16[256,1024]{1,0:T(8,128)(2,1)S(1)}, u32[]{:S(2)}, u32[]{:S(2)}) %collective-permute-start.41) | collective-permute-done | bytes 524320 | tf_op jit(solution)/shard_map/ppermute | solution.py:71
  332.1 29.4 %reduce-scatter.8.cloned.1.call-done = bf16[96,1024]{1,0:T(8,128)(2,1)} async-done(((bf16[768,1024]{1,0:T(8,128)(2,1)}), bf16[96,1024]{1,0:T(8,128)(2,1)}) %reduce-scatter.8.cloned.1.call-update) | async-done | bytes 196624 | tf_op jit(solution)/shard_map/reduce_scatter | solution.py:96
  361.6 89.9 %reduce-scatter.14.cloned.1.call-done = bf16[512,1024]{1,0:T(8,128)(2,1)} async-done(((bf16[4096,1024]{1,0:T(8,128)(2,1)}), bf16[512,1024]{1,0:T(8,128)(2,1)}) %reduce-scatter.14.cloned.1.call-update) | async-done | bytes 1048592 | tf_op jit(solution)/shard_map/reduce_scatter | solution.py:96
  451.5 90.9 %reduce-scatter.12.cloned.1.call-done = bf16[1024,512]{1,0:T(8,128)(2,1)} async-done(((bf16[8192,512]{1,0:T(8,128)(2,1)}), bf16[1024,512]{1,0:T(8,128)(2,1)}) %reduce-scatter.12.cloned.1.call-update) | async-done | bytes 1048592 | tf_op jit(solution)/shard_map/reduce_scatter | solution.py:96
  542.7 90.6 %reduce-scatter.10.cloned.1.call-done = bf16[1024,512]{1,0:T(8,128)(2,1)} async-done(((bf16[8192,512]{1,0:T(8,128)(2,1)}), bf16[1024,512]{1,0:T(8,128)(2,1)}) %reduce-scatter.10.cloned.1.call-update) | async-done | bytes 1048592 | tf_op jit(solution)/shard_map/reduce_scatter | solution.py:96
  641.6 7.9 collective-permute-done.43
  651.6 11.2 %collective-permute-done.44 = f32[34,1024]{1,0:T(8,128)S(1)} collective-permute-done((f32[34,1024]{1,0:T(8,128)S(1)}, f32[34,1024]{1,0:T(8,128)S(1)}, u32[]{:S(2)}, u32[]{:S(2)}) %collective-permute-start.44) | collective-permute-done | bytes 139296 | tf_op jit(solution)/shard_map/ppermute | solution.py:664
  667.2 3.4 collective-permute-done.46
  674.5 2.8 fusion.17
  677.3 83.2 %all-gather.14.cloned.1.call-done = bf16[4096,1024]{1,0:T(8,128)(2,1)} async-done(((bf16[512,1024]{1,0:T(8,128)(2,1)}), bf16[4096,1024]{1,0:T(8,128)(2,1)}) %all-gather.14.cloned.1.call-update) | async-done | bytes 8388624 | tf_op jit(solution)/shard_map/all_gather | solution.py:92
  760.5 11.7 %convert.9 = f32[8,512,1024]{2,1,0:T(8,128)} convert(bf16[8,512,1024]{2,1,0:T(8,128)(2,1)} %bitcast.73) | non-fusion elementwise | flops 4194304 | bytes 25165824 | tf_op jit(solution)/shard_map/convert_element_type | solution.py:614
  772.2 77.1 %all-gather.12.cloned.1.call-done = bf16[8192,512]{1,0:T(8,128)(2,1)} async-done(((bf16[1024,512]{1,0:T(8,128)(2,1)}), bf16[8192,512]{1,0:T(8,128)(2,1)}) %all-gather.12.cloned.1.call-update) | async-done | bytes 8388624 | tf_op jit(solution)/shard_map/all_gather | solution.py:92
  849.3 11.9 %convert.8 = f32[8,1024,512]{2,1,0:T(8,128)} convert(bf16[8,1024,512]{2,1,0:T(8,128)(2,1)} %bitcast.74) | non-fusion elementwise | flops 4194304 | bytes 25165824 | tf_op jit(solution)/shard_map/convert_element_type | solution.py:614
  861.2 76.8 %all-gather.10.cloned.1.call-done = bf16[8192,512]{1,0:T(8,128)(2,1)} async-done(((bf16[1024,512]{1,0:T(8,128)(2,1)}), bf16[8192,512]{1,0:T(8,128)(2,1)}) %all-gather.10.cloned.1.call-update) | async-done | bytes 8388624 | tf_op jit(solution)/shard_map/all_gather | solution.py:92
  937.9 11.9 %convert.7 = f32[8,1024,512]{2,1,0:T(8,128)} convert(bf16[8,1024,512]{2,1,0:T(8,128)(2,1)} %bitcast.75) | non-fusion elementwise | flops 4194304 | bytes 25165824 | tf_op jit(solution)/shard_map/convert_element_type | solution.py:614
  (247 shorter events, 77.3 us)
Async XLA Ops:
  7.2 75.9 %all-gather.6.cloned.1.call-start = ((), (), s32[]{:S(2)}) async-start(), calls=%async_computation.5 | async-start | bytes 4718592 | tf_op jit(solution)/shard_map/all_gather | solution.py:92
  14.5 14.4 %collective-permute-start.4 = (bf16[256,1024]{1,0:T(8,128)(2,1)S(1)}, bf16[256,1024]{1,0:T(8,128)(2,1)S(1)}, u32[]{:S(2)}, u32[]{:S(2)}) collective-permute-start(bf16[256,1024]{1,0:T(8,128)(2,1)S(1)} %constant_dynamic-update-slice_fusion.rest_0_.rest_4_), channel_id=1, source_target_pairs={{0,16},{8,24},{16,0},{24,8},{1,17},{9,25},{17,1},{25,9},{2,18},{10... | collective-permute-start | bytes 1572872 | tf_op jit(solution)/shard_map/ppermute | solution.py:58
  14.6 15.0 %collective-permute-start.3 = (bf16[256,1024]{1,0:T(8,128)(2,1)S(1)}, bf16[256,1024]{1,0:T(8,128)(2,1)S(1)}, u32[]{:S(2)}, u32[]{:S(2)}) collective-permute-start(bf16[256,1024]{1,0:T(8,128)(2,1)S(1)} %constant_dynamic-update-slice_fusion.rest_0_.rest_4_), channel_id=1, source_target_pairs={{0,8},{8,0},{16,24},{24,16},{1,9},{9,1},{17,25},{25,17},{2,10},{10... | collective-permute-start | bytes 1572872 | tf_op jit(solution)/shard_map/ppermute | solution.py:60
  34.8 248.8 %reduce-scatter.6.cloned.1.call-start = ((), (), s32[]{:S(2)}) async-start(), calls=%async_computation.6 | async-start | bytes 4718592 | tf_op jit(solution)/shard_map/reduce_scatter | solution.py:96
  34.8 14.9 %collective-permute-start.7 = (bf16[256,1024]{1,0:T(8,128)(2,1)S(1)}, bf16[256,1024]{1,0:T(8,128)(2,1)}, u32[]{:S(2)}, u32[]{:S(2)}) collective-permute-start(bf16[256,1024]{1,0:T(8,128)(2,1)S(1)} %copy-done.10), channel_id=1, source_target_pairs={{0,16},{8,24},{16,0},{24,8},{1,17},{9,25},{17,1},{25,9},{2,18},{10... | collective-permute-start | bytes 1572872 | tf_op jit(solution)/shard_map/ppermute | solution.py:58
  35.2 25.8 %collective-permute-start.10 = (bf16[256,1024]{1,0:T(8,128)(2,1)}, bf16[256,1024]{1,0:T(8,128)(2,1)}, u32[]{:S(2)}, u32[]{:S(2)}) collective-permute-start(bf16[256,1024]{1,0:T(8,128)(2,1)} %rest_0_.6), channel_id=1, source_target_pairs={{0,16},{8,24},{16,0},{24,8},{1,17},{9,25},{17,1},{25,9},{2,18},{10... | collective-permute-start | bytes 1572872 | tf_op jit(solution)/shard_map/ppermute | solution.py:58
  36.9 27.1 %collective-permute-start.6 = (bf16[256,1024]{1,0:T(8,128)(2,1)S(1)}, bf16[256,1024]{1,0:T(8,128)(2,1)}, u32[]{:S(2)}, u32[]{:S(2)}) collective-permute-start(bf16[256,1024]{1,0:T(8,128)(2,1)S(1)} %copy-done.10), channel_id=1, source_target_pairs={{0,8},{8,0},{16,24},{24,16},{1,9},{9,1},{17,25},{25,17},{2,10},{10... | collective-permute-start | bytes 1572872 | tf_op jit(solution)/shard_map/ppermute | solution.py:60
  36.9 78.1 %collective-permute-start.9 = (bf16[256,1024]{1,0:T(8,128)(2,1)}, bf16[256,1024]{1,0:T(8,128)(2,1)}, u32[]{:S(2)}, u32[]{:S(2)}) collective-permute-start(bf16[256,1024]{1,0:T(8,128)(2,1)} %rest_0_.6), channel_id=1, source_target_pairs={{0,8},{8,0},{16,24},{24,16},{1,9},{9,1},{17,25},{25,17},{2,10},{10... | collective-permute-start | bytes 1572872 | tf_op jit(solution)/shard_map/ppermute | solution.py:60
  39.5 91.4 %collective-permute-start.16 = (bf16[256,1024]{1,0:T(8,128)(2,1)}, bf16[256,1024]{1,0:T(8,128)(2,1)}, u32[]{:S(2)}, u32[]{:S(2)}) collective-permute-start(bf16[256,1024]{1,0:T(8,128)(2,1)} %convert_element_type.164.refs_4_), channel_id=1, source_target_pairs={{0,16},{8,24},{16,0},{24,8},{1,17},{9,25},{17,1},{25,9},{2,18},{10... | collective-permute-start | bytes 1572872 | tf_op jit(solution)/shard_map/ppermute | solution.py:58
  49.8 14.3 %collective-permute-start.8 = (bf16[256,1024]{1,0:T(8,128)(2,1)}, bf16[256,1024]{1,0:T(8,128)(2,1)}, u32[]{:S(2)}, u32[]{:S(2)}) collective-permute-start(bf16[256,1024]{1,0:T(8,128)(2,1)} %collective-permute-done.7.rest_2_), channel_id=1, source_target_pairs={{0,8},{8,0},{16,24},{24,16},{1,9},{9,1},{17,25},{25,17},{2,10},{10... | collective-permute-start | bytes 1572872 | tf_op jit(solution)/shard_map/ppermute | solution.py:60
  61.0 54.0 %collective-permute-start.11 = (bf16[256,1024]{1,0:T(8,128)(2,1)}, bf16[256,1024]{1,0:T(8,128)(2,1)}, u32[]{:S(2)}, u32[]{:S(2)}) collective-permute-start(bf16[256,1024]{1,0:T(8,128)(2,1)} %collective-permute-done.10.rest_2_), channel_id=1, source_target_pairs={{0,8},{8,0},{16,24},{24,16},{1,9},{9,1},{17,25},{25,17},{2,10},{10... | collective-permute-start | bytes 1572872 | tf_op jit(solution)/shard_map/ppermute | solution.py:60
  118.4 13.1 %collective-permute-start.13 = (bf16[256,1024]{1,0:T(8,128)(2,1)S(1)}, bf16[256,1024]{1,0:T(8,128)(2,1)S(1)}, u32[]{:S(2)}, u32[]{:S(2)}) collective-permute-start(bf16[256,1024]{1,0:T(8,128)(2,1)S(1)} %get-tuple-element.55.refs_0_.act_ref), channel_id=1, source_target_pairs={{0,16},{8,24},{16,0},{24,8},{1,17},{9,25},{17,1},{25,9},{2,18},{10... | collective-permute-start | bytes 1572872 | tf_op jit(solution)/shard_map/ppermute | solution.py:58
  175.3 16.8 %collective-permute-start.27 = (bf16[256,1024]{1,0:T(8,128)(2,1)}, bf16[256,1024]{1,0:T(8,128)(2,1)S(1)}, u32[]{:S(2)}, u32[]{:S(2)}) collective-permute-start(bf16[256,1024]{1,0:T(8,128)(2,1)} %get-tuple-element.61), channel_id=1, source_target_pairs={{0,8},{8,0},{16,24},{24,16},{1,9},{9,1},{17,25},{25,17},{2,10},{10... | collective-permute-start | bytes 1572872 | tf_op jit(solution)/shard_map/ppermute | solution.py:67
  177.7 14.4 %collective-permute-start.29 = (bf16[256,1024]{1,0:T(8,128)(2,1)S(1)}, bf16[256,1024]{1,0:T(8,128)(2,1)S(1)}, u32[]{:S(2)}, u32[]{:S(2)}) collective-permute-start(bf16[256,1024]{1,0:T(8,128)(2,1)S(1)} %add_convert_fusion.6), channel_id=1, source_target_pairs={{0,16},{8,24},{16,0},{24,8},{1,17},{9,25},{17,1},{25,9},{2,18},{10... | collective-permute-start | bytes 1572872 | tf_op jit(solution)/shard_map/ppermute | solution.py:71
  178.5 13.6 %collective-permute-start.32 = (f32[8,256]{1,0:T(8,128)S(1)}, f32[8,256]{1,0:T(8,128)S(1)}, u32[]{:S(2)}, u32[]{:S(2)}) collective-permute-start(f32[8,256]{1,0:T(8,128)S(1)} %bitcast.98), channel_id=1, source_target_pairs={{0,16},{8,24},{16,0},{24,8},{1,17},{9,25},{17,1},{25,9},{2,18},{10... | collective-permute-start | bytes 24584 | tf_op jit(solution)/shard_map/ppermute | solution.py:617
  226.2 135.3 %reduce-scatter.8.cloned.1.call-start = ((), (), s32[]{:S(2)}) async-start(), calls=%async_computation.7 | async-start | bytes 1769472 | tf_op jit(solution)/shard_map/reduce_scatter | solution.py:96
  226.3 64.3 %collective-permute-start.34 = (bf16[256,1024]{1,0:T(8,128)(2,1)}, bf16[256,1024]{1,0:T(8,128)(2,1)}, u32[]{:S(2)}, u32[]{:S(2)}) collective-permute-start(bf16[256,1024]{1,0:T(8,128)(2,1)} %copy-done.25), channel_id=1, source_target_pairs={{0,8},{8,0},{16,24},{24,16},{1,9},{9,1},{17,25},{25,17},{2,10},{10... | collective-permute-start | bytes 1572872 | tf_op jit(solution)/shard_map/ppermute | solution.py:67
  291.9 14.8 %collective-permute-start.35 = (bf16[256,1024]{1,0:T(8,128)(2,1)S(1)}, bf16[256,1024]{1,0:T(8,128)(2,1)S(1)}, u32[]{:S(2)}, u32[]{:S(2)}) collective-permute-start(bf16[256,1024]{1,0:T(8,128)(2,1)S(1)} %add_convert_fusion.5), channel_id=1, source_target_pairs={{0,16},{8,24},{16,0},{24,8},{1,17},{9,25},{17,1},{25,9},{2,18},{10... | collective-permute-start | bytes 1572872 | tf_op jit(solution)/shard_map/ppermute | solution.py:71
  293.4 13.5 %collective-permute-start.36 = (bf16[256,1024]{1,0:T(8,128)(2,1)S(1)}, bf16[256,1024]{1,0:T(8,128)(2,1)S(1)}, u32[]{:S(2)}, u32[]{:S(2)}) collective-permute-start(bf16[256,1024]{1,0:T(8,128)(2,1)S(1)} %get-tuple-element.77), channel_id=1, source_target_pairs={{0,8},{8,0},{16,24},{24,16},{1,9},{9,1},{17,25},{25,17},{2,10},{10... | collective-permute-start | bytes 1572872 | tf_op jit(solution)/shard_map/ppermute | solution.py:67
  293.6 24.6 %collective-permute-start.39 = (bf16[256,1024]{1,0:T(8,128)(2,1)S(1)}, bf16[256,1024]{1,0:T(8,128)(2,1)S(1)}, u32[]{:S(2)}, u32[]{:S(2)}) collective-permute-start(bf16[256,1024]{1,0:T(8,128)(2,1)S(1)} %get-tuple-element.81), channel_id=1, source_target_pairs={{0,8},{8,0},{16,24},{24,16},{1,9},{9,1},{17,25},{25,17},{2,10},{10... | collective-permute-start | bytes 1572872 | tf_op jit(solution)/shard_map/ppermute | solution.py:67
  294.2 23.8 %collective-permute-start.38 = (bf16[256,1024]{1,0:T(8,128)(2,1)S(1)}, bf16[256,1024]{1,0:T(8,128)(2,1)S(1)}, u32[]{:S(2)}, u32[]{:S(2)}) collective-permute-start(bf16[256,1024]{1,0:T(8,128)(2,1)S(1)} %add_convert_fusion.3), channel_id=1, source_target_pairs={{0,16},{8,24},{16,0},{24,8},{1,17},{9,25},{17,1},{25,9},{2,18},{10... | collective-permute-start | bytes 1572872 | tf_op jit(solution)/shard_map/ppermute | solution.py:71
  295.1 33.6 %collective-permute-start.41 = (bf16[256,1024]{1,0:T(8,128)(2,1)S(1)}, bf16[256,1024]{1,0:T(8,128)(2,1)S(1)}, u32[]{:S(2)}, u32[]{:S(2)}) collective-permute-start(bf16[256,1024]{1,0:T(8,128)(2,1)S(1)} %add_convert_fusion.1), channel_id=1, source_target_pairs={{0,16},{8,24},{16,0},{24,8},{1,17},{9,25},{17,1},{25,9},{2,18},{10... | collective-permute-start | bytes 1572872 | tf_op jit(solution)/shard_map/ppermute | solution.py:71
  330.3 121.2 %reduce-scatter.14.cloned.1.call-start = ((), (), s32[]{:S(2)}) async-start(), calls=%async_computation.13 | async-start | bytes 9437184 | tf_op jit(solution)/shard_map/reduce_scatter | solution.py:96
  330.9 211.5 %reduce-scatter.12.cloned.1.call-start = ((), (), s32[]{:S(2)}) async-start(), calls=%async_computation.11 | async-start | bytes 9437184 | tf_op jit(solution)/shard_map/reduce_scatter | solution.py:96
  331.5 301.9 %reduce-scatter.10.cloned.1.call-start = ((), (), s32[]{:S(2)}) async-start(), calls=%async_computation.9 | async-start | bytes 9437184 | tf_op jit(solution)/shard_map/reduce_scatter | solution.py:96
  332.0 340.3 %all-gather.8.cloned.1.call-start = ((), (), s32[]{:S(2)}) async-start(), calls=%async_computation.8 | async-start | bytes 1769472 | tf_op jit(solution)/shard_map/all_gather | solution.py:92
  361.5 399.0 %all-gather.14.cloned.1.call-start = ((), (), s32[]{:S(2)}) async-start(), calls=%async_computation.14 | async-start | bytes 9437184 | tf_op jit(solution)/shard_map/all_gather | solution.py:92
  451.5 397.8 %all-gather.12.cloned.1.call-start = ((), (), s32[]{:S(2)}) async-start(), calls=%async_computation.12 | async-start | bytes 9437184 | tf_op jit(solution)/shard_map/all_gather | solution.py:92
  542.4 395.5 %all-gather.10.cloned.1.call-start = ((), (), s32[]{:S(2)}) async-start(), calls=%async_computation.10 | async-start | bytes 9437184 | tf_op jit(solution)/shard_map/all_gather | solution.py:92
  633.4 32.5 %collective-permute-start.24 = (bf16[256,1024]{1,0:T(8,128)(2,1)}, bf16[256,1024]{1,0:T(8,128)(2,1)S(1)}, u32[]{:S(2)}, u32[]{:S(2)}) collective-permute-start(bf16[256,1024]{1,0:T(8,128)(2,1)} %get-tuple-element.57), channel_id=1, source_target_pairs={{0,8},{8,0},{16,24},{24,16},{1,9},{9,1},{17,25},{25,17},{2,10},{10... | collective-permute-start | bytes 1572872 | tf_op jit(solution)/shard_map/ppermute | solution.py:67
  636.5 29.4 %collective-permute-start.26 = (bf16[256,1024]{1,0:T(8,128)(2,1)}, bf16[256,1024]{1,0:T(8,128)(2,1)S(1)}, u32[]{:S(2)}, u32[]{:S(2)}) collective-permute-start(bf16[256,1024]{1,0:T(8,128)(2,1)} %add_convert_fusion.7), channel_id=1, source_target_pairs={{0,16},{8,24},{16,0},{24,8},{1,17},{9,25},{17,1},{25,9},{2,18},{10... | collective-permute-start | bytes 1572872 | tf_op jit(solution)/shard_map/ppermute | solution.py:71
  649.5 13.2 %collective-permute-start.44 = (f32[34,1024]{1,0:T(8,128)S(1)}, f32[34,1024]{1,0:T(8,128)S(1)}, u32[]{:S(2)}, u32[]{:S(2)}) collective-permute-start(f32[34,1024]{1,0:T(8,128)S(1)} %add.154), channel_id=1, source_target_pairs={{0,4},{1,5},{2,6},{3,7},{4,0},{5,1},{6,2},{7,3},{8,12},{9,13},{10,... | collective-permute-start | bytes 417800 | tf_op jit(solution)/shard_map/ppermute | solution.py:664
  (62 other events, 1924.0 us)
Sparse Core Ops, SparseCore 0:
  34.9 48.1 all-gather.5
  226.4 57.1 reduce-scatter.5
  330.4 31.0 reduce-scatter.7
  364.2 87.1 reduce-scatter.13
  454.2 88.1 reduce-scatter.11
  545.1 88.1 reduce-scatter.9
  634.9 37.4 all-gather.7
  673.9 86.5 all-gather.13
  762.0 87.2 all-gather.11
  850.7 87.2 all-gather.9

commit v2 on v1

--- a/solution.py
+++ b/solution.py
@@ -1,3 +1,5 @@
+import math
+
 import jax
 import jax.numpy as jnp
 from jax import lax
@@ -37,9 +39,16 @@
     return pl.BlockSpec(memory_space=pltpu.SMEM)
 
 
-def call(body, scalars, arrays, outs, scratch=(), mib=48):
+def cost(flops, arrays, outs):
+    moved = sum(a.size * a.dtype.itemsize for a in arrays)
+    moved += sum(math.prod(s) * jnp.dtype(d).itemsize for s, d in outs)
+    return pl.CostEstimate(flops=flops, transcendentals=0, bytes_accessed=moved)
+
+
+def call(body, scalars, arrays, outs, scratch=(), mib=48, flops=0):
     return pl.pallas_call(
         body,
+        cost_estimate=cost(flops, arrays, outs),
         in_specs=[smem() for _ in scalars] + [vmem() for _ in arrays],
         out_specs=[vmem() for _ in outs],
         out_shape=[jax.ShapeDtypeStruct(s, d) for s, d in outs],
@@ -61,16 +70,24 @@
     return [pieces[s] for s in range(count)]
 
 
-def dp_reduce(pieces, count):
-    kept = {}
+def dp_cores(pieces, count):
+    kept = []
     for step in range(0, count, 2):
         other = lax.ppermute(pieces[step + 1], "dp", xor_pairs(count, 1))
-        kept[step] = pieces[step].astype(F32) + other.astype(F32)
-    total = kept[0]
-    for step in range(2, count, 2):
-        other = lax.ppermute(kept[step].astype(BF16), "dp", xor_pairs(count, step))
+        kept.append((pieces[step].astype(F32) + other.astype(F32)).astype(BF16))
+    return kept
+
+
+def dp_rest(kept, count):
+    total = kept[0].astype(F32)
+    for i in range(1, len(kept)):
+        other = lax.ppermute(kept[i], "dp", xor_pairs(count, 2 * i))
         total = total + other.astype(F32)
     return total
+
+
+def dp_reduce(pieces, count):
+    return dp_rest(dp_cores(pieces, count), count)
 
 
 def in_order(pieces, index):
@@ -303,21 +320,20 @@
     return body
 
 
-def expert_body(count, local, rows):
-    slots = local * CAP
-
-    def body(me_ref, *refs):
-        acts, grads = refs[:count], refs[count : 2 * count]
-        slot_ref, hit_ref, router_ref, wg_ref, wu_ref, wd_ref = refs[2 * count : 2 * count + 6]
-        (gg_ref, ug_ref, dg_ref, gate_out, dgate_ref) = refs[2 * count + 6 : 2 * count + 11]
-        youts = refs[2 * count + 11 : 3 * count + 11]
-        gouts = refs[3 * count + 11 : 4 * count + 11]
-        gate_all, xe, gyx, dye, picks, ys, dxs = refs[4 * count + 11 :]
+def expert_call(blocks, rows, local, served, first, number, last_dims):
+    wide, inner = last_dims
+    tokens = blocks * rows
+
+    def body(at_ref, *refs):
+        acts, grads = refs[:blocks], refs[blocks : 2 * blocks]
+        slot_ref, hit_ref, router_ref, wg_ref, wu_ref, wd_ref = refs[2 * blocks : 2 * blocks + 6]
+        gg_ref, ug_ref, dg_ref, gate_out, dgate_ref, y_ref, dx_ref = refs[2 * blocks + 6 : 2 * blocks + 13]
+        gate_all, xe, gyx, dye = refs[2 * blocks + 13 :]
         e = pl.program_id(0)
 
         @pl.when(e == 0)
         def _():
-            for s in range(count):
+            for s in range(blocks):
                 part = slice(s * rows, (s + 1) * rows)
                 logits = dot_nt(router_ref[...], acts[s][...])
                 hit = hit_ref[:, part] > 0
@@ -330,16 +346,14 @@
                     gate_out[...] = gates
 
         slot_row = slot_ref[0]
-        gate_row = gate_all[pl.ds(me_ref[0] * local + e, 1), :]
+        gate_row = gate_all[pl.ds(at_ref[1] + e, 1), :]
         slot_id = lax.broadcasted_iota(jnp.int32, (CAP, rows), 0)
-        at = pl.multiple_of(e * CAP, CAP)
         slot_gates = []
-        for s in range(count):
+        for s in range(blocks):
             part = slice(s * rows, (s + 1) * rows)
             put = slice(s * CAP, (s + 1) * CAP)
             hits = slot_id == slot_row[:, part]
             pick = jnp.where(hits, 1.0, 0.0).astype(BF16)
-            picks[s, pl.ds(at, CAP), :] = pick
             gate = jnp.sum(jnp.where(hits, gate_row[:, part], 0.0), axis=1, keepdims=True)
             slot_gates.append(gate)
             xe[put, :] = dot_nn(pick, acts[s][...]).astype(BF16)
@@ -353,88 +367,235 @@
         hidden = (act * up_part).astype(BF16)
         out = dot_nn(hidden, wd_ref[0]).astype(BF16).astype(F32)
         slot_dot = jnp.sum(gyx[...].astype(F32) * out, axis=1, keepdims=True)
-        for s in range(count):
+        for s in range(blocks):
             part = slice(s * rows, (s + 1) * rows)
             put = slice(s * CAP, (s + 1) * CAP)
             hits = slot_id == slot_row[:, part]
             dgate_ref[0, :, part] = jnp.sum(jnp.where(hits, slot_dot[put], 0.0), axis=0, keepdims=True)
-            ys[s, pl.ds(at, CAP), :] = (slot_gates[s] * out[put]).astype(BF16)
+            y_ref[0, put, :] = (slot_gates[s] * out[put]).astype(BF16)
         dg_ref[0] = dot_tn(hidden, dye[...]).astype(BF16)
         grad_hidden = dot_nt(dye[...], wd_ref[0])
         grad_gate = (grad_hidden * up_part * sig * (1.0 + gate_part * (1.0 - sig))).astype(BF16)
         grad_up = (grad_hidden * act).astype(BF16)
         gg_ref[0] = dot_tn(xe[...], grad_gate).astype(BF16)
         ug_ref[0] = dot_tn(xe[...], grad_up).astype(BF16)
-        grad_in = (dot_nt(grad_gate, wg_ref[0]) + dot_nt(grad_up, wu_ref[0])).astype(BF16)
-        for s in range(count):
-            dxs[s, pl.ds(at, CAP), :] = grad_in[s * CAP : (s + 1) * CAP]
-
-        @pl.when(e == local - 1)
-        def _():
-            for s in range(count):
-                youts[s][...] = dot_tn(picks[s], ys[s]).astype(BF16)
-                gouts[s][...] = dot_tn(picks[s], dxs[s]).astype(BF16)
-
-    def run(me, acts, grads, slots_t, hits, router_t, wg, wu, wd):
-        wide = acts[0].shape[1]
-        inner = wg.shape[2]
-        whole = lambda shape: pl.BlockSpec(shape, lambda e: tuple(0 for _ in shape))
-        each = lambda shape: pl.BlockSpec(
-            (1,) + shape, lambda e: (e,) + tuple(0 for _ in shape)
-        )
-        tokens = count * rows
-        shape = jax.ShapeDtypeStruct
-        res = pl.pallas_call(
-            body,
-            grid=(local,),
-            in_specs=[smem()]
-            + [whole((rows, wide)) for _ in range(2 * count)]
+        dx_ref[0] = (dot_nt(grad_gate, wg_ref[0]) + dot_nt(grad_up, wu_ref[0])).astype(BF16)
+
+    def whole(*shape):
+        return pl.BlockSpec(
+            shape, lambda e, at: tuple(0 for _ in shape), pipeline_mode=pl.Buffered(1)
+        )
+
+    def each(*shape):
+        return pl.BlockSpec((1,) + shape, lambda e, at: (e,) + tuple(0 for _ in shape))
+
+    def weight(*shape):
+        return pl.BlockSpec((1,) + shape, lambda e, at: (at[0] + e,) + tuple(0 for _ in shape))
+
+    shape = jax.ShapeDtypeStruct
+    return pl.pallas_call(
+        body,
+        cost_estimate=pl.CostEstimate(
+            flops=number * blocks * CAP * wide * (18 * inner + 4 * rows),
+            transcendentals=0,
+            bytes_accessed=number * 12 * wide * inner + 4 * blocks * rows * wide,
+        ),
+        grid_spec=pltpu.PrefetchScalarGridSpec(
+            num_scalar_prefetch=1,
+            grid=(number,),
+            in_specs=[whole(rows, wide) for _ in range(2 * blocks)]
             + [
-                each((1, tokens)),
-                whole((EXPERTS, tokens)),
-                whole((EXPERTS, wide)),
-                each((wide, inner)),
-                each((wide, inner)),
-                each((inner, wide)),
+                pl.BlockSpec((1, 1, tokens), lambda e, at: (first + e, 0, 0)),
+                whole(EXPERTS, tokens),
+                whole(EXPERTS, wide),
+                weight(wide, inner),
+                weight(wide, inner),
+                weight(inner, wide),
             ],
             out_specs=[
-                each((wide, inner)),
-                each((wide, inner)),
-                each((inner, wide)),
-                whole((EXPERTS, rows)),
-                each((1, tokens)),
-            ]
-            + [whole((rows, wide)) for _ in range(2 * count)],
-            out_shape=[
-                shape((local, wide, inner), BF16),
-                shape((local, wide, inner), BF16),
-                shape((local, inner, wide), BF16),
-                shape((EXPERTS, rows), F32),
-                shape((local, 1, tokens), F32),
-            ]
-            + [shape((rows, wide), BF16) for _ in range(2 * count)],
+                each(wide, inner),
+                each(wide, inner),
+                each(inner, wide),
+                pl.BlockSpec((EXPERTS, rows), lambda e, at: (0, 0)),
+                each(1, tokens),
+                each(blocks * CAP, wide),
+                each(blocks * CAP, wide),
+            ],
             scratch_shapes=[
                 pltpu.VMEM((EXPERTS, tokens), F32),
-                pltpu.VMEM((count * CAP, wide), BF16),
-                pltpu.VMEM((count * CAP, wide), BF16),
-                pltpu.VMEM((count * CAP, wide), BF16),
-                pltpu.VMEM((count, slots, rows), BF16),
-                pltpu.VMEM((count, slots, wide), BF16),
-                pltpu.VMEM((count, slots, wide), BF16),
+                pltpu.VMEM((blocks * CAP, wide), BF16),
+                pltpu.VMEM((blocks * CAP, wide), BF16),
+                pltpu.VMEM((blocks * CAP, wide), BF16),
             ],
-            compiler_params=pltpu.CompilerParams(
-                vmem_limit_bytes=56 << 20, dimension_semantics=("arbitrary",)
-            ),
-        )(me, *acts, *grads, slots_t, hits, router_t, wg, wu, wd)
-        return (
-            res[:3],
-            res[3],
-            res[4],
-            res[5 : 5 + count],
-            res[5 + count :],
-        )
-
-    return run
+        ),
+        out_shape=[
+            shape((number, wide, inner), BF16),
+            shape((number, wide, inner), BF16),
+            shape((number, inner, wide), BF16),
+            shape((EXPERTS, rows), F32),
+            shape((number, 1, tokens), F32),
+            shape((number, blocks * CAP, wide), BF16),
+            shape((number, blocks * CAP, wide), BF16),
+        ],
+        compiler_params=pltpu.CompilerParams(
+            vmem_limit_bytes=56 << 20, dimension_semantics=("arbitrary",)
+        ),
+    )
+
+
+def combine_body(blocks, rows, groups):
+    def body(slot_ref, *refs):
+        parts, outs = refs[: len(groups)], refs[len(groups) :]
+        slot_id = lax.broadcasted_iota(jnp.int32, (CAP, rows), 0)
+        for s in range(blocks):
+            picks, slots = [], []
+            for g, (first, number) in enumerate(groups):
+                for e in range(number):
+                    hits = slot_id == slot_ref[first + e, :, s * rows : (s + 1) * rows]
+                    picks.append(jnp.where(hits, 1.0, 0.0).astype(BF16))
+                    slots.append(parts[g][e, s * CAP : (s + 1) * CAP, :])
+            outs[s][...] = dot_tn(
+                jnp.concatenate(picks, axis=0), jnp.concatenate(slots, axis=0)
+            ).astype(BF16)
+
+    return body
+
+
+def store_pair(held, here, there, places, total):
+    rows, cols = here.shape
+
+    def body(at_ref, here_ref, there_ref, *rest):
+        out_ref = rest[-1]
+
+        @pl.when(pl.program_id(0) == 0)
+        def _():
+            out_ref[0] = here_ref[...].astype(F32)
+
+        @pl.when(pl.program_id(0) == 1)
+        def _():
+            out_ref[0] = there_ref[...].astype(F32)
+
+    more = [] if held is None else [held]
+    return pl.pallas_call(
+        body,
+        grid_spec=pltpu.PrefetchScalarGridSpec(
+            num_scalar_prefetch=1,
+            grid=(2,),
+            in_specs=[pl.BlockSpec((rows, cols), lambda i, at: (0, 0))] * 2
+            + [pl.BlockSpec(memory_space=pl.ANY)] * len(more),
+            out_specs=pl.BlockSpec((1, rows, cols), lambda i, at: (at[i], 0, 0)),
+        ),
+        out_shape=jax.ShapeDtypeStruct((total, rows, cols), F32),
+        input_output_aliases={3: 0} if more else {},
+        compiler_params=pltpu.CompilerParams(
+            vmem_limit_bytes=24 << 20, dimension_semantics=("arbitrary",)
+        ),
+    )(places, here, there, *more)
+
+
+TO_INNER = [(0, 2), (1, 3), (6, 4), (7, 5)]
+ACROSS = [(2, 4), (3, 5), (4, 2), (5, 3)]
+TO_OUTER = [(2, 0), (3, 1), (4, 6), (5, 7)]
+
+
+def tie(value, marks):
+    return lax.optimization_barrier((value, marks))[0] if marks else value
+
+
+def line_step(outer, came, block, part, across, following, sent):
+    want_part, want_sent, want_done = block is not None, part is not None, sent is not None
+    given = [came] + [a for a in (block, part, across, following, sent) if a is not None]
+    outs = want_part + want_sent + want_done
+
+    def body(outer_ref, *refs):
+        ins, out = list(refs[: len(given)]), list(refs[len(given) :])
+        came_ref = ins.pop(0)
+        block_ref = ins.pop(0) if want_part else None
+        part_ref, across_ref = (ins.pop(0), ins.pop(0)) if want_sent else (None, None)
+        following_ref = ins.pop(0) if following is not None else None
+        sent_ref = ins.pop(0) if want_done else None
+        part_out = out.pop(0) if want_part else None
+        sent_out = out.pop(0) if want_sent else None
+        done_out = out.pop(0) if want_done else None
+
+        @pl.when(outer_ref[0] == 0)
+        def _():
+            if want_part:
+                part_out[...] = block_ref[...] + came_ref[...]
+            if want_sent:
+                sent_out[...] = part_ref[...] + across_ref[...]
+            if want_done:
+                done_out[...] = sent_ref[...]
+
+        @pl.when(outer_ref[0] == 1)
+        def _():
+            if following is not None:
+                sent_out[...] = following_ref[...]
+            if want_done:
+                done_out[...] = came_ref[...]
+
+    res = call(body, [outer], given, [(came.shape, BF16)] * outs, mib=24)
+    res = list(res)
+    return [res.pop(0) if w else None for w in (want_part, want_sent, want_done)]
+
+
+class LineSums:
+    LAG = 3
+
+    def __init__(self, me, beside, base, base_there, total):
+        self.outer = ((me < 2) | (me >= 6)).astype(jnp.int32).reshape(1)
+        self.beside, self.base, self.base_there, self.total = beside, base, base_there, total
+        self.blocks, self.held = [], [None, None, None]
+        self.sent, self.parts, self.across = {}, [], []
+        self.swaps, self.marks, self.done = [], [], 0
+
+    def feed(self, results):
+        for e in range(results[0].shape[0]):
+            self.blocks += [results[m][e] for m in range(3)]
+
+    def store(self):
+        if self.done < len(self.swaps):
+            here, there = self.swaps[self.done]
+            e, m = divmod(self.done, 3)
+            places = jnp.stack([self.base + e, self.base_there + e])
+            self.held[m] = store_pair(self.held[m], here, there, places, self.total)
+            self.done += 1
+
+    def step(self, after=()):
+        t, count = len(self.marks), len(self.blocks)
+        new, old = t < count, t >= self.LAG
+        sent = self.sent[t] if old else self.blocks[t]
+        kept = [h for h in self.held if h is not None]
+        sent, kept, _ = lax.optimization_barrier((sent, kept, list(after)))
+        self.held[: len(kept)] = kept
+        came = lax.ppermute(sent, "ctx", (TO_INNER if new else []) + (TO_OUTER if old else []))
+        self.marks.append(came)
+        turn_back = 0 < t <= count
+        shape = self.blocks[t % 3].shape
+        more = turn_back and t + 2 < count
+        part, _, finished = line_step(
+            self.outer, came, self.blocks[t] if new else None, None, None, None, sent if old else None
+        ) if new or old else (None, None, None)
+        if turn_back:
+            _, self.sent[t + 2], _ = line_step(
+                self.outer, self.across[t - 1], None, self.parts[t - 1], self.across[t - 1],
+                self.blocks[t + 2] if more else None, None,
+            )
+        if new:
+            self.parts.append(part)
+            self.across.append(lax.ppermute(part, "ctx", ACROSS))
+        if len(self.swaps) > 1:
+            self.store()
+        if old:
+            self.swaps.append((finished, lax.ppermute(finished, "ctx", self.beside)))
+
+    def hold(self, value):
+        return tie(value, self.marks[-2:-1])
+
+    def finish(self):
+        while self.done < len(self.swaps):
+            self.store()
+        return self.held
 
 
 def after_body(count):
@@ -515,6 +676,12 @@
         me = me_dp.reshape(1)
         near = rows // BLOCK
 
+        pairs = n_ctx == 8 and local % 2 == 0
+        served = local // 2 if pairs else local
+        beside = xor_pairs(n_ctx, 1)
+        column = me_ctx & 1 if pairs else jnp.zeros((), jnp.int32)
+        grad_low = out_grad.astype(BF16)
+        grad_beside = lax.ppermute(grad_low, "ctx", beside) if pairs else None
         wkv = dp_gather(jnp.concatenate([key_weight, value_weight], axis=1), n_dp)
         small = jnp.concatenate(
             [
@@ -560,26 +727,38 @@
         kv_mine, act_one = call(
             kv_body(n_dp),
             [me],
-            [layer_input, gain_one, cosine, sine] + wkv,
+            [tie(layer_input, [grad_beside] if pairs else []), gain_one, cosine, sine] + wkv,
             [((rows, 2 * KVD), BF16), ((n_dp, rows, width), BF16)],
         )
         every_kv = ring_gather(kv_mine, n_ctx)
         (query,) = call(query_body(n_dp), [me], [act_one, cosine, sine] + wq, [((rows, wide), BF16)])
         wo = dp_gather(out_weight, n_dp)
 
-        ids = jnp.stack(dp_gather(expert_ids.T, n_dp))
-        fill = jnp.stack(dp_gather(fill_order, n_dp))
+        def reach(block):
+            pieces = dp_gather(block, n_dp)
+            if pairs:
+                pieces = pieces + dp_gather(lax.ppermute(block, "ctx", beside), n_dp)
+            return pieces
+
+        table = jnp.concatenate([expert_ids.T, fill_order], axis=0)
+        table = jnp.stack(reach(table))
+        ids, fill = table[:, :-1], table[:, -1]
+        held_blocks = table.shape[0]
         names = jnp.arange(EXPERTS, dtype=jnp.int32)
         hits = jnp.sum((ids[:, :, None, :] == names[None, None, :, None]).astype(F32), axis=1)
-        earlier = (fill[:, 0, :, None] < fill[:, 0, None, :]).astype(BF16)
+        earlier = (fill[:, :, None] < fill[:, None, :]).astype(BF16)
         prior = jnp.einsum(
             "set,stu->seu", hits.astype(BF16), earlier, preferred_element_type=F32
         )
         slot = jnp.where((hits > 0) & (prior < CAP), prior, -1.0).astype(jnp.int32)
-        slot = lax.dynamic_slice_in_dim(slot, me_dp * local, local, axis=1)
-        slots_t = slot.transpose(1, 0, 2).reshape(local, 1, n_dp * rows)
-        hits_t = hits.transpose(1, 0, 2).reshape(EXPERTS, n_dp * rows)
-        grads_all = dp_gather(out_grad.astype(BF16), n_dp)
+        base = column * served
+        slot = lax.dynamic_slice_in_dim(slot, me_dp * local + base, served, axis=1)
+        slots_t = slot.transpose(1, 0, 2).reshape(served, 1, held_blocks * rows)
+        hits_t = hits.transpose(1, 0, 2).reshape(EXPERTS, held_blocks * rows)
+        grads_all = dp_gather(grad_low, n_dp)
+        if pairs:
+            grads_all = grads_all + dp_gather(grad_beside, n_dp)
+        query, grads_all, wo = lax.optimization_barrier((query, grads_all, wo))
 
         attended, extended = call(
             attend_body,
@@ -592,6 +771,7 @@
                 pltpu.VMEM((PAIRS, 4 * BLOCK, 1), F32),
                 pltpu.VMEM((PAIRS, 4 * BLOCK, 128), F32),
             ],
+            flops=rows * blocks * BLOCK * wide * 4,
         )
         mixed, act_two = call(
             mix_body(n_dp),
@@ -601,27 +781,72 @@
             [pltpu.VMEM((n_dp, rows, width), BF16)],
         )
 
-        acts_all = dp_gather(act_two, n_dp)
-        weight_grads, gates, dgates, y_parts, g_parts = expert_body(n_dp, local, rows)(
-            me, acts_all, grads_all, slots_t, hits_t, router_t, gate_weight, up_weight, down_weight
-        )
-
-        expert_sums = []
-        scattered = [
-            ring_scatter(g.reshape(-1, g.shape[2]), n_ctx) for g in weight_grads
-        ]
-        for g, part in zip(weight_grads, scattered):
-            expert_sums.append(ring_gather(part, n_ctx).reshape(g.shape).astype(F32))
-
-        back = [dgates[:, 0, s * rows : (s + 1) * rows] for s in range(n_dp)]
+        acts_all = reach(act_two)
+        groups = [(0, 1), (1, served - 1)] if pairs else [(0, served)]
+        results = []
+        line = LineSums(me_ctx, beside, base, (1 - column) * served, local) if pairs else None
+
+        def step(*after):
+            if pairs:
+                line.step(after)
+
+        def hold(value):
+            return value
+
+        for first, number in groups:
+            at = jnp.stack([base + first, me_dp * local + base + first])
+            results.append(
+                expert_call(
+                    held_blocks, rows, local, served, first, number, gate_weight.shape[1:]
+                )(
+                    at, *acts_all, *grads_all, slots_t, hits_t, router_t, gate_weight, up_weight,
+                    down_weight,
+                )
+            )
+            if pairs:
+                line.feed(results[-1])
+            step(*[res[4] for res in results[1:]])
+        gates = results[0][3]
+
+        def combine(index, after):
+            return call(
+                combine_body(held_blocks, rows, groups),
+                [],
+                [hold(tie(slots_t, after))] + [res[index] for res in results],
+                [((rows, wide), BF16)] * held_blocks,
+            )
+
+        def settle(parts, between):
+            kept = [dp_cores(parts[s : s + n_dp], n_dp) for s in range(0, held_blocks, n_dp)]
+            between(kept)
+            totals = [dp_rest(hold(k), n_dp) for k in kept]
+            between(totals)
+            totals = hold(totals)
+            if pairs:
+                totals[0] = totals[0] + lax.ppermute(
+                    totals[1].astype(BF16), "ctx", beside
+                ).astype(F32)
+            return totals[0]
+
+        dgates = jnp.concatenate([res[4] for res in results], axis=0)[:, 0]
+        back = [dgates[:, s * rows : (s + 1) * rows] for s in range(held_blocks)]
+        if pairs:
+            other = lax.ppermute(jnp.stack(back[n_dp:]), "ctx", beside)
+            own = jnp.stack(back[:n_dp])
+            back = jnp.where(
+                column == 0,
+                jnp.concatenate([own, other], axis=1),
+                jnp.concatenate([other, own], axis=1),
+            )
         back = [back[0]] + [lax.ppermute(back[s], "dp", xor_pairs(n_dp, s)) for s in range(1, n_dp)]
         dgate_t = in_order(back, me_dp).reshape(EXPERTS, rows)
-        grad_act_two = dp_reduce(g_parts, n_dp)
-        layer_output = mixed + dp_reduce(y_parts, n_dp)
+        g_parts = combine(6, [])
+        grad_act_two = settle(g_parts, lambda values: None)
+        step(grad_act_two)
         res = call(
             after_body(n_dp),
             [me],
-            [mixed, grad_act_two, out_grad, gain_two, gates, dgate_t, router_t, act_two, attended] + wo,
+            [mixed, hold(grad_act_two), out_grad, gain_two, gates, dgate_t, router_t, act_two, attended] + wo,
             [((rows, wide), F32), ((rows, wide), BF16), ((EXPERTS, wide), F32), ((1, wide), F32)]
             + [((width, wide), BF16)] * n_dp,
             [pltpu.VMEM((n_dp, rows, width), BF16), pltpu.VMEM((n_dp, rows, width), BF16)],
@@ -631,7 +856,7 @@
         grad_query, kv_grads = call(
             attend_back_body,
             [low_blocks, mine, where_block],
-            [query, every_kv, starts, grad_heads, extended, cosine, sine],
+            [query, every_kv, starts, hold(grad_heads), extended, cosine, sine],
             [((rows, wide), BF16), ((blocks * BLOCK, 2 * KVD), BF16)],
             [
                 pltpu.VMEM((PAIRS, 4 * BLOCK, 128), BF16),
@@ -641,12 +866,19 @@
                 pltpu.VMEM((PAIRS, 4 * BLOCK, 128), F32),
                 pltpu.VMEM((blocks * BLOCK, 2 * KVD), F32),
             ],
-        )
+            flops=rows * blocks * BLOCK * wide * 10,
+        )
+        step(grad_query)
         kv_grad = ring_scatter(kv_grads, n_ctx)
+        y_parts = combine(5, [grad_query])
+        y_total = settle(y_parts, lambda values: None)
+        layer_output = mixed + y_total
+        dense_out = dp_reduce(hold(out_parts), n_dp).astype(BF16)
+        step(layer_output)
         res = call(
             first_body(n_dp),
             [me],
-            [layer_input, gain_one, cosine, sine, act_one, grad_query, kv_grad, grad_mixed] + wq + wkv,
+            [layer_input, gain_one, cosine, sine, act_one, grad_query, hold(kv_grad), grad_mixed] + wq + wkv,
             [((rows, wide), F32), ((1, wide), F32)]
             + [((width, wide), BF16)] * n_dp
             + [((width, 2 * KVD), BF16)] * n_dp,
@@ -654,17 +886,29 @@
         )
         input_grad, gain_one_part = res[:2]
         q_parts, kv_parts = res[2 : 2 + n_dp], res[2 + n_dp :]
-
-        dense = jnp.concatenate(
-            [dp_reduce(part, n_dp).astype(BF16) for part in (out_parts, q_parts, kv_parts)], axis=0
-        )
+        step(gain_one_part)
+
+        dense_q = dp_reduce(hold(q_parts), n_dp).astype(BF16)
+        dense_kv = dp_reduce(kv_parts, n_dp).astype(BF16)
+        dense = jnp.concatenate([dense_out, dense_q, dense_kv], axis=0)
         dense = ring_gather(ring_scatter(dense, n_ctx), n_ctx).astype(F32)
         tiny = jnp.concatenate([router_part, gain_one_part, gain_two_part], axis=0)
-        for step in [1 << b for b in range(n_ctx.bit_length() - 1)]:
-            tiny = tiny + lax.ppermute(tiny, "ctx", xor_pairs(n_ctx, step))
-        for step in [1 << b for b in range(n_dp.bit_length() - 1)]:
-            tiny = tiny + lax.ppermute(tiny, "dp", xor_pairs(n_dp, step))
+        for bit in [1 << b for b in range(n_ctx.bit_length() - 1)]:
+            tiny = tiny + lax.ppermute(tiny, "ctx", xor_pairs(n_ctx, bit))
+        for bit in [1 << b for b in range(n_dp.bit_length() - 1)]:
+            tiny = tiny + lax.ppermute(tiny, "dp", xor_pairs(n_dp, bit))
         tiny = lax.dynamic_slice_in_dim(tiny, me_dp * width, width, axis=1)
+        if pairs:
+            while len(line.marks) < len(line.blocks) + line.LAG:
+                line.step()
+            expert_sums = line.finish()
+        else:
+            expert_sums = [
+                ring_gather(ring_scatter(g.reshape(-1, g.shape[2]), n_ctx), n_ctx)
+                .reshape(g.shape)
+                .astype(F32)
+                for g in results[0][:3]
+            ]
         return (
             layer_output,
             input_grad,

time: 963 us -> 808 us (0.84)
  waiting for transfers between devices: 723 us -> 340 us
  starting transfers between devices: 27.3 us -> 147 us
  Pallas kernels: 114 us -> 213 us
  local copies, waits for them, and re-layouts: 23 us -> 51.4 us
  other arithmetic: 55 us -> 33.6 us
    reduce_scatter x5 -> x2, waiting for transfers between devices: 358 us -> 0.01 us  [ring_scatter(): lax.psum_scatter(block, 'ctx', scatter_dimension=0, tiled=True, axis_inde...]
    all_gather x5 -> x2, waiting for transfers between devices: 252 us -> 0.01 us  [ring_gather(): lax.all_gather(block, 'ctx', axis=0, tiled=True, axis_index_groups=ring_o...]
    ppermute x20 -> x71, waiting for transfers between devices: 58.7 us -> 276 us  [the longest x15 161 us: step(): lax.ppermute(sent, 'ctx', (TO_INNER if new else []) + (TO_OUTER if old el...]
    ppermute x20 -> x71, starting transfers between devices: 14 us -> 128 us  [the longest x15 75.8 us: step(): lax.ppermute(sent, 'ctx', (TO_INNER if new else []) + (TO_OUTER if old el...]
    pallas_call x8 -> x50, Pallas kernels: 114 us -> 213 us  [the longest x36 111 us: call(): pl.pallas_call(body, cost_estimate=cost(flops, arrays, outs), in_specs=[s...]
    unnamed x78 -> x237, local copies, waits for them, and re-layouts: 9.49 us -> 36.7 us
    convert_element_type x12 -> x13, other arithmetic: 42.2 us -> 15 us  [the longest x7 7.85 us: dp_cores(): kept.append((pieces[step].astype(F32) + other.astype(F32)).astype(BF16))]
    ppermute x8 -> x10, waiting for transfers between devices: 36.6 us -> 54.7 us  [dp_gather(): pieces[step] = lax.ppermute(block, 'dp', xor_pairs(count, step))]
  transfers between devices with their start and end apart: 57 -> 108, of which waited for: 30 -> 35; matrix products, arithmetic and copies ran while one was open for 5% -> 6% of each run, Pallas kernels for 4% -> 16%
where the time goes in v2:
time: 808 us; the launch traced here: 801 us
  waiting for transfers between devices  340 us (42%)
  Pallas kernels  213 us (26%)
  starting transfers between devices  147 us (18%)
  local copies, waits for them, and re-layouts  51.4 us (6%)
  other arithmetic  33.6 us (4%)
  between operations  15.7 us (2%)
    ppermute x15, waiting for transfers between devices, step(): lax.ppermute(sent, 'ctx', (TO_INNER if new else []) + (TO_OUTER if old el...  161 us
    pallas_call x36, Pallas kernels, call(): pl.pallas_call(body, cost_estimate=cost(flops, arrays, outs), in_specs=[s...  111 us
    ppermute x15, starting transfers between devices, step(): lax.ppermute(sent, 'ctx', (TO_INNER if new else []) + (TO_OUTER if old el...  75.8 us
    ppermute x12, waiting for transfers between devices, step(): self.swaps.append((finished, lax.ppermute(finished, 'ctx', self.beside)))  58.1 us
    ppermute x10, waiting for transfers between devices, dp_gather(): pieces[step] = lax.ppermute(block, 'dp', xor_pairs(count, step))  54.7 us
    pallas_call x2, Pallas kernels, on_device(): expert_call(held_blocks, rows, local, served, first, number, gate_weight....  52.2 us
    pallas_call x12, Pallas kernels, store_pair(): pl.pallas_call(body, grid_spec=pltpu.PrefetchScalarGridSpec(num_scalar_pr...  48.9 us
    unnamed x237, local copies, waits for them, and re-layouts  36.7 us
  transfers between devices with their start and end apart: 108, of which 35 were waited for; matrix products, arithmetic and copies ran while one was open for 6% of the time, Pallas kernels for 16%

profile of v2, /device:TPU:0, one launch (start us, length us, event | category | flops | bytes accessed | tf_op | source)
XLA Modules:
  0.0 801.1 jit_solution(9720588786208803381)
XLA Ops:
  44.6 5.6 collective-permute-done.20
  57.0 8.3 %collective-permute-done.11.refs_10_ = bf16[256,1024]{1,0:T(8,128)(2,1)S(1)} collective-permute-done((bf16[256,1024]{1,0:T(8,128)(2,1)}, bf16[256,1024]{1,0:T(8,128)(2,1)S(1)}, u32[]{:S(2)}, u32[]{:S(2)}) %collective-permute-start.11) | collective-permute-done | bytes 524320 | tf_op jit(solution)/shard_map/ppermute | solution.py:67
  65.3 11.2 %collective-permute-done.17.rest_2_ = bf16[256,1024]{1,0:T(8,128)(2,1)S(1)} collective-permute-done((bf16[256,1024]{1,0:T(8,128)(2,1)S(1)}, bf16[256,1024]{1,0:T(8,128)(2,1)S(1)}, u32[]{:S(2)}, u32[]{:S(2)}) %collective-permute-start.17) | collective-permute-done | bytes 524320 | tf_op jit(solution)/shard_map/ppermute | solution.py:67
  77.0 9.4 %collective-permute-done.14.refs_14_ = bf16[256,1024]{1,0:T(8,128)(2,1)S(1)} collective-permute-done((bf16[256,1024]{1,0:T(8,128)(2,1)}, bf16[256,1024]{1,0:T(8,128)(2,1)S(1)}, u32[]{:S(2)}, u32[]{:S(2)}) %collective-permute-start.14) | collective-permute-done | bytes 524320 | tf_op jit(solution)/shard_map/ppermute | solution.py:67
  97.6 23.8 %shard_map.258 = (bf16[256,1024]{1,0:T(8,128)(2,1)S(1)}, f32[4,4,256,128]{3,2,1,0:T(8,128)S(1)}) custom-call(s32[2]{0:T(128)S(1)} %copy-done.83, s32[2]{0:T(128)S(1)} %get-tuple-element.265.high_ref, s32[16]{0:T(128)S(1)} %copy-done.81, bf16[256,1024]{1,0:T(8,128)(2,1)S(1)} %shard_map.257.q_ref, bf16[2048,1024]{1,0:T(8,128)(2,1)} %all-gather.3.cloned.1.call-done.kv_ref, ...), custom_call_target="tpu_custom_call" | custom-call | flops 2147483648 | bytes 7341056 | tf_op jit(solution)/shard_map/pallas_call | solution.py:49
  132.0 7.5 collective-permute-done.29.refs_4_
  144.9 11.0 %collective-permute-done.31.refs_6_ = bf16[256,1024]{1,0:T(8,128)(2,1)} collective-permute-done((bf16[256,1024]{1,0:T(8,128)(2,1)}, bf16[256,1024]{1,0:T(8,128)(2,1)}, u32[]{:S(2)}, u32[]{:S(2)}) %collective-permute-start.31) | collective-permute-done | bytes 524320 | tf_op jit(solution)/shard_map/ppermute | solution.py:67
  158.7 14.4 %shard_map.260 = (bf16[1,1024,512]{2,1,0:T(8,128)(2,1)}, bf16[1,1024,512]{2,1,0:T(8,128)(2,1)}, bf16[1,512,1024]{2,1,0:T(8,128)(2,1)}, f32[32,256]{1,0:T(8,128)}...) custom-call(s32[2]{0:T(128)} %get-tuple-element.303.at_ref, ...), custom_call_target="tpu_custom_call" | custom-call | flops 5368709120 | bytes 14680064 | tf_op jit(solution)/shard_map/pallas_call | solution.py:799
  173.1 37.9 %shard_map.261 = (bf16[3,1024,512]{2,1,0:T(8,128)(2,1)}, bf16[3,1024,512]{2,1,0:T(8,128)(2,1)}, bf16[3,512,1024]{2,1,0:T(8,128)(2,1)}, f32[32,256]{1,0:T(8,128)}...) custom-call(s32[2]{0:T(128)} %get-tuple-element.304.at_ref, ...), custom_call_target="tpu_custom_call" | custom-call | flops 16106127360 | bytes 27262976 | tf_op jit(solution)/shard_map/pallas_call | solution.py:799
  225.1 7.9 collective-permute-done.38
  236.5 7.3 collective-permute-done.43
  254.5 21.0 %shard_map.264 = (bf16[256,1024]{1,0:T(8,128)(2,1)S(1)}, bf16[2048,1024]{1,0:T(8,128)(2,1)}) custom-call(s32[2]{0:T(128)S(1)} %copy-done.84, s32[2]{0:T(128)S(1)} %get-tuple-element.265.high_ref, s32[16]{0:T(128)S(1)} %copy-done.82, bf16[256,1024]{1,0:T(8,128)(2,1)S(1)} %copy-done.59, bf16[2048,1024]{1,0:T(8,128)(2,1)} %all-gather.3.cloned.1.call-done.kv_ref, ...), custom_call_target="tpu_custom_call" | custom-call | flops 5368709120 | bytes 12321792 | tf_op jit(solution)/shard_map/pallas_call | solution.py:49
  292.5 11.0 %collective-permute-done.65.refs_0_ = bf16[1024,512]{1,0:T(8,128)(2,1)} collective-permute-done((bf16[1024,512]{1,0:T(8,128)(2,1)S(1)}, bf16[1024,512]{1,0:T(8,128)(2,1)}, u32[]{:S(2)}, u32[]{:S(2)}) %collective-permute-start.65) | collective-permute-done | bytes 1048608 | tf_op jit(solution)/shard_map/ppermute | solution.py:571
  307.1 41.2 %collective-permute-done.77.refs_0_ = bf16[1024,512]{1,0:T(8,128)(2,1)} collective-permute-done((bf16[1024,512]{1,0:T(8,128)(2,1)S(1)}, bf16[1024,512]{1,0:T(8,128)(2,1)}, u32[]{:S(2)}, u32[]{:S(2)}) %collective-permute-start.77) | collective-permute-done | bytes 1048608 | tf_op jit(solution)/shard_map/ppermute | solution.py:571
  348.3 7.3 collective-permute-start.73
  362.5 24.0 %collective-permute-done.73.refs_0_ = bf16[512,1024]{1,0:T(8,128)(2,1)S(1)} collective-permute-done((bf16[512,1024]{1,0:T(8,128)(2,1)S(1)}, bf16[512,1024]{1,0:T(8,128)(2,1)S(1)}, u32[]{:S(2)}, u32[]{:S(2)}) %collective-permute-start.73) | collective-permute-done | bytes 1048608 | tf_op jit(solution)/shard_map/ppermute | solution.py:571
  386.5 9.8 %collective-permute-start.67 = (bf16[1024,512]{1,0:T(8,128)(2,1)S(1)}, bf16[1024,512]{1,0:T(8,128)(2,1)S(1)}, u32[]{:S(2)}, u32[]{:S(2)}) collective-permute-start(bf16[1024,512]{1,0:T(8,128)(2,1)S(1)} %shard_map.268.refs_2_), channel_id=1, source_target_pairs={{0,2},{1,3},{6,4},{7,5},{2,0},{3,1},{4,6},{5,7},{8,10},{9,11},{14,... | collective-permute-start | bytes 3145736 | tf_op jit(solution)/shard_map/ppermute | solution.py:571
  401.8 22.5 %collective-permute-start.79 = (bf16[1024,512]{1,0:T(8,128)(2,1)}, bf16[1024,512]{1,0:T(8,128)(2,1)}, u32[]{:S(2)}, u32[]{:S(2)}) collective-permute-start(bf16[1024,512]{1,0:T(8,128)(2,1)} %shard_map.279.refs_2_), channel_id=1, source_target_pairs={{0,2},{1,3},{6,4},{7,5},{2,0},{3,1},{4,6},{5,7},{8,10},{9,11},{14,... | collective-permute-start | bytes 3145736 | tf_op jit(solution)/shard_map/ppermute | solution.py:571
  434.4 6.6 shard_map.266
  443.5 17.4 %collective-permute-start.75 = (bf16[512,1024]{1,0:T(8,128)(2,1)S(1)}, bf16[512,1024]{1,0:T(8,128)(2,1)S(1)}, u32[]{:S(2)}, u32[]{:S(2)}) collective-permute-start(bf16[512,1024]{1,0:T(8,128)(2,1)S(1)} %copy-done.13), channel_id=1, source_target_pairs={{0,2},{1,3},{6,4},{7,5},{2,0},{3,1},{4,6},{5,7},{8,10},{9,11},{14,... | collective-permute-start | bytes 3145736 | tf_op jit(solution)/shard_map/ppermute | solution.py:571
  471.2 13.2 %collective-permute-done.75.refs_0_ = bf16[512,1024]{1,0:T(8,128)(2,1)S(1)} collective-permute-done((bf16[512,1024]{1,0:T(8,128)(2,1)S(1)}, bf16[512,1024]{1,0:T(8,128)(2,1)S(1)}, u32[]{:S(2)}, u32[]{:S(2)}) %collective-permute-start.75) | collective-permute-done | bytes 1048608 | tf_op jit(solution)/shard_map/ppermute | solution.py:571
  516.2 16.6 %collective-permute-done.82.there_ref = bf16[512,1024]{1,0:T(8,128)(2,1)} collective-permute-done((bf16[512,1024]{1,0:T(8,128)(2,1)}, bf16[512,1024]{1,0:T(8,128)(2,1)}, u32[]{:S(2)}, u32[]{:S(2)}) %collective-permute-start.82) | collective-permute-done | bytes 1048608 | tf_op jit(solution)/shard_map/ppermute | solution.py:590
  547.3 12.2 %collective-permute-done.88.refs_0_ = bf16[1024,512]{1,0:T(8,128)(2,1)} collective-permute-done((bf16[1024,512]{1,0:T(8,128)(2,1)}, bf16[1024,512]{1,0:T(8,128)(2,1)}, u32[]{:S(2)}, u32[]{:S(2)}) %collective-permute-start.88) | collective-permute-done | bytes 1048608 | tf_op jit(solution)/shard_map/ppermute | solution.py:571
  566.1 14.6 %collective-permute-done.86.refs_0_ = bf16[512,1024]{1,0:T(8,128)(2,1)} collective-permute-done((bf16[512,1024]{1,0:T(8,128)(2,1)}, bf16[512,1024]{1,0:T(8,128)(2,1)}, u32[]{:S(2)}, u32[]{:S(2)}) %collective-permute-start.86) | collective-permute-done | bytes 1048608 | tf_op jit(solution)/shard_map/ppermute | solution.py:571
  604.8 12.0 %collective-permute-done.91.there_ref = bf16[512,1024]{1,0:T(8,128)(2,1)S(1)} collective-permute-done((bf16[512,1024]{1,0:T(8,128)(2,1)S(1)}, bf16[512,1024]{1,0:T(8,128)(2,1)S(1)}, u32[]{:S(2)}, u32[]{:S(2)}) %collective-permute-start.91) | collective-permute-done | bytes 1048608 | tf_op jit(solution)/shard_map/ppermute | solution.py:590
  626.0 15.8 %collective-permute-done.96.refs_0_ = bf16[1024,512]{1,0:T(8,128)(2,1)S(1)} collective-permute-done((bf16[1024,512]{1,0:T(8,128)(2,1)S(1)}, bf16[1024,512]{1,0:T(8,128)(2,1)S(1)}, u32[]{:S(2)}, u32[]{:S(2)}) %collective-permute-start.96) | collective-permute-done | bytes 1048608 | tf_op jit(solution)/shard_map/ppermute | solution.py:571
  644.2 23.8 %collective-permute-done.94.refs_0_ = bf16[512,1024]{1,0:T(8,128)(2,1)} collective-permute-done((bf16[512,1024]{1,0:T(8,128)(2,1)}, bf16[512,1024]{1,0:T(8,128)(2,1)}, u32[]{:S(2)}, u32[]{:S(2)}) %collective-permute-start.94) | collective-permute-done | bytes 1048608 | tf_op jit(solution)/shard_map/ppermute | solution.py:571
  680.0 7.9 collective-permute-done.98.there_ref
  694.7 13.0 %collective-permute-done.99.there_ref = bf16[512,1024]{1,0:T(8,128)(2,1)} collective-permute-done((bf16[512,1024]{1,0:T(8,128)(2,1)}, bf16[512,1024]{1,0:T(8,128)(2,1)}, u32[]{:S(2)}, u32[]{:S(2)}) %collective-permute-start.99) | collective-permute-done | bytes 1048608 | tf_op jit(solution)/shard_map/ppermute | solution.py:590
  732.5 19.8 %collective-permute-done.61 = f32[34,1024]{1,0:T(8,128)S(1)} collective-permute-done((f32[34,1024]{1,0:T(8,128)S(1)}, f32[34,1024]{1,0:T(8,128)S(1)}, u32[]{:S(2)}, u32[]{:S(2)}) %collective-permute-start.61) | collective-permute-done | bytes 139296 | tf_op jit(solution)/shard_map/ppermute | solution.py:897
  752.4 6.9 collective-permute-done.62
  781.7 8.5 %collective-permute-done.103.there_ref = bf16[512,1024]{1,0:T(8,128)(2,1)S(1)} collective-permute-done((bf16[512,1024]{1,0:T(8,128)(2,1)}, bf16[512,1024]{1,0:T(8,128)(2,1)S(1)}, u32[]{:S(2)}, u32[]{:S(2)}) %collective-permute-start.103) | collective-permute-done | bytes 1048608 | tf_op jit(solution)/shard_map/ppermute | solution.py:590
  (558 shorter events, 316.1 us)
Async XLA Ops:
  7.2 89.1 %all-gather.3.cloned.1.call-start = ((), (), s32[]{:S(2)}) async-start(), calls=%async_computation.2 | async-start | bytes 4718592 | tf_op jit(solution)/shard_map/all_gather | solution.py:109
  35.3 396.0 %reduce-scatter.3.cloned.1.call-start = ((), (), s32[]{:S(2)}) async-start(), calls=%async_computation.3 | async-start | bytes 4718592 | tf_op jit(solution)/shard_map/reduce_scatter | solution.py:113
  276.4 367.9 %reduce-scatter.5.cloned.1.call-start = ((), (), s32[]{:S(2)}) async-start(), calls=%async_computation.4 | async-start | bytes 1769472 | tf_op jit(solution)/shard_map/reduce_scatter | solution.py:113
  279.9 68.4 %collective-permute-start.77 = (bf16[1024,512]{1,0:T(8,128)(2,1)S(1)}, bf16[1024,512]{1,0:T(8,128)(2,1)}, u32[]{:S(2)}, u32[]{:S(2)}) collective-permute-start(bf16[1024,512]{1,0:T(8,128)(2,1)S(1)} %bitcast.120), channel_id=1, source_target_pairs={{0,2},{1,3},{6,4},{7,5},{8,10},{9,11},{14,12},{15,13},{16,18},{17,... | collective-permute-start | bytes 3145736 | tf_op jit(solution)/shard_map/ppermute | solution.py:571
  292.5 64.3 %collective-permute-start.45 = (bf16[256,1024]{1,0:T(8,128)(2,1)}, bf16[256,1024]{1,0:T(8,128)(2,1)}, u32[]{:S(2)}, u32[]{:S(2)}) collective-permute-start(bf16[256,1024]{1,0:T(8,128)(2,1)} %get-tuple-element.179), channel_id=1, source_target_pairs={{0,8},{8,0},{16,24},{24,16},{1,9},{9,1},{17,25},{25,17},{2,10},{10... | collective-permute-start | bytes 1572872 | tf_op jit(solution)/shard_map/ppermute | solution.py:76
  304.7 56.5 %collective-permute-start.66 = (bf16[1024,512]{1,0:T(8,128)(2,1)S(1)}, bf16[1024,512]{1,0:T(8,128)(2,1)S(1)}, u32[]{:S(2)}, u32[]{:S(2)}) collective-permute-start(bf16[1024,512]{1,0:T(8,128)(2,1)S(1)} %shard_map.267.refs_1_), channel_id=1, source_target_pairs={{2,4},{3,5},{4,2},{5,3},{10,12},{11,13},{12,10},{13,11},{18,20},{1... | collective-permute-start | bytes 3145736 | tf_op jit(solution)/shard_map/ppermute | solution.py:586
  305.6 53.2 %collective-permute-start.47 = (bf16[256,1024]{1,0:T(8,128)(2,1)S(1)}, bf16[256,1024]{1,0:T(8,128)(2,1)S(1)}, u32[]{:S(2)}, u32[]{:S(2)}) collective-permute-start(bf16[256,1024]{1,0:T(8,128)(2,1)S(1)} %copy-done.80), channel_id=1, source_target_pairs={{0,8},{8,0},{16,24},{24,16},{1,9},{9,1},{17,25},{25,17},{2,10},{10... | collective-permute-start | bytes 1572872 | tf_op jit(solution)/shard_map/ppermute | solution.py:76
  307.0 52.1 %collective-permute-start.49 = (bf16[256,1024]{1,0:T(8,128)(2,1)S(1)}, bf16[256,1024]{1,0:T(8,128)(2,1)S(1)}, u32[]{:S(2)}, u32[]{:S(2)}) collective-permute-start(bf16[256,1024]{1,0:T(8,128)(2,1)S(1)} %add_convert_fusion.10), channel_id=1, source_target_pairs={{0,16},{8,24},{16,0},{24,8},{1,17},{9,25},{17,1},{25,9},{2,18},{10... | collective-permute-start | bytes 1572872 | tf_op jit(solution)/shard_map/ppermute | solution.py:84
  348.3 38.2 %collective-permute-start.73 = (bf16[512,1024]{1,0:T(8,128)(2,1)S(1)}, bf16[512,1024]{1,0:T(8,128)(2,1)S(1)}, u32[]{:S(2)}, u32[]{:S(2)}) collective-permute-start(bf16[512,1024]{1,0:T(8,128)(2,1)S(1)} %bitcast.118), channel_id=1, source_target_pairs={{0,2},{1,3},{6,4},{7,5},{8,10},{9,11},{14,12},{15,13},{16,18},{17,... | collective-permute-start | bytes 3145736 | tf_op jit(solution)/shard_map/ppermute | solution.py:571
  356.8 39.5 %collective-permute-start.78 = (bf16[1024,512]{1,0:T(8,128)(2,1)S(1)}, bf16[1024,512]{1,0:T(8,128)(2,1)S(1)}, u32[]{:S(2)}, u32[]{:S(2)}) collective-permute-start(bf16[1024,512]{1,0:T(8,128)(2,1)S(1)} %shard_map.278.refs_1_), channel_id=1, source_target_pairs={{2,4},{3,5},{4,2},{5,3},{10,12},{11,13},{12,10},{13,11},{18,20},{1... | collective-permute-start | bytes 3145736 | tf_op jit(solution)/shard_map/ppermute | solution.py:586
  358.8 40.6 %collective-permute-start.44 = (bf16[256,1024]{1,0:T(8,128)(2,1)S(1)}, bf16[256,1024]{1,0:T(8,128)(2,1)S(1)}, u32[]{:S(2)}, u32[]{:S(2)}) collective-permute-start(bf16[256,1024]{1,0:T(8,128)(2,1)S(1)} %copy-done.78), channel_id=1, source_target_pairs={{0,8},{8,0},{16,24},{24,16},{1,9},{9,1},{17,25},{25,17},{2,10},{10... | collective-permute-start | bytes 1572872 | tf_op jit(solution)/shard_map/ppermute | solution.py:76
  359.0 40.3 %collective-permute-start.46 = (bf16[256,1024]{1,0:T(8,128)(2,1)S(1)}, bf16[256,1024]{1,0:T(8,128)(2,1)S(1)}, u32[]{:S(2)}, u32[]{:S(2)}) collective-permute-start(bf16[256,1024]{1,0:T(8,128)(2,1)S(1)} %add_convert_fusion.12), channel_id=1, source_target_pairs={{0,16},{8,24},{16,0},{24,8},{1,17},{9,25},{17,1},{25,9},{2,18},{10... | collective-permute-start | bytes 1572872 | tf_op jit(solution)/shard_map/ppermute | solution.py:84
  361.2 38.2 %collective-permute-start.50 = (bf16[256,1024]{1,0:T(8,128)(2,1)S(1)}, bf16[256,1024]{1,0:T(8,128)(2,1)S(1)}, u32[]{:S(2)}, u32[]{:S(2)}) collective-permute-start(bf16[256,1024]{1,0:T(8,128)(2,1)S(1)} %add_convert_fusion.9), channel_id=1, source_target_pairs={{0,1},{1,0},{2,3},{3,2},{4,5},{5,4},{6,7},{7,6},{8,9},{9,8},{10,11... | collective-permute-start | bytes 1572872 | tf_op jit(solution)/shard_map/ppermute | solution.py:826
  401.8 59.2 %collective-permute-start.79 = (bf16[1024,512]{1,0:T(8,128)(2,1)}, bf16[1024,512]{1,0:T(8,128)(2,1)}, u32[]{:S(2)}, u32[]{:S(2)}) collective-permute-start(bf16[1024,512]{1,0:T(8,128)(2,1)} %shard_map.279.refs_2_), channel_id=1, source_target_pairs={{0,2},{1,3},{6,4},{7,5},{2,0},{3,1},{4,6},{5,7},{8,10},{9,11},{14,... | collective-permute-start | bytes 3145736 | tf_op jit(solution)/shard_map/ppermute | solution.py:571
  425.7 38.7 %collective-permute-start.68 = (bf16[1024,512]{1,0:T(8,128)(2,1)}, bf16[1024,512]{1,0:T(8,128)(2,1)}, u32[]{:S(2)}, u32[]{:S(2)}) collective-permute-start(bf16[1024,512]{1,0:T(8,128)(2,1)} %get-tuple-element.205.refs_1_), channel_id=1, source_target_pairs={{2,4},{3,5},{4,2},{5,3},{10,12},{11,13},{12,10},{13,11},{18,20},{1... | collective-permute-start | bytes 3145736 | tf_op jit(solution)/shard_map/ppermute | solution.py:586
  427.3 38.8 %collective-permute-start.69 = (bf16[1024,512]{1,0:T(8,128)(2,1)}, bf16[1024,512]{1,0:T(8,128)(2,1)}, u32[]{:S(2)}, u32[]{:S(2)}) collective-permute-start(bf16[1024,512]{1,0:T(8,128)(2,1)} %get-tuple-element.206.here_ref), channel_id=1, source_target_pairs={{0,1},{1,0},{2,3},{3,2},{4,5},{5,4},{6,7},{7,6},{8,9},{9,8},{10,11... | collective-permute-start | bytes 3145736 | tf_op jit(solution)/shard_map/ppermute | solution.py:590
  443.5 40.9 %collective-permute-start.75 = (bf16[512,1024]{1,0:T(8,128)(2,1)S(1)}, bf16[512,1024]{1,0:T(8,128)(2,1)S(1)}, u32[]{:S(2)}, u32[]{:S(2)}) collective-permute-start(bf16[512,1024]{1,0:T(8,128)(2,1)S(1)} %copy-done.13), channel_id=1, source_target_pairs={{0,2},{1,3},{6,4},{7,5},{2,0},{3,1},{4,6},{5,7},{8,10},{9,11},{14,... | collective-permute-start | bytes 3145736 | tf_op jit(solution)/shard_map/ppermute | solution.py:571
  495.9 44.4 %collective-permute-start.70 = (bf16[1024,512]{1,0:T(8,128)(2,1)}, bf16[1024,512]{1,0:T(8,128)(2,1)}, u32[]{:S(2)}, u32[]{:S(2)}) collective-permute-start(bf16[1024,512]{1,0:T(8,128)(2,1)} %shard_map.270.refs_2_), channel_id=1, source_target_pairs={{0,2},{1,3},{6,4},{7,5},{2,0},{3,1},{4,6},{5,7},{8,10},{9,11},{14,... | collective-permute-start | bytes 3145736 | tf_op jit(solution)/shard_map/ppermute | solution.py:571
  514.0 45.5 %collective-permute-start.88 = (bf16[1024,512]{1,0:T(8,128)(2,1)}, bf16[1024,512]{1,0:T(8,128)(2,1)}, u32[]{:S(2)}, u32[]{:S(2)}) collective-permute-start(bf16[1024,512]{1,0:T(8,128)(2,1)} %shard_map.281.refs_2_), channel_id=1, source_target_pairs={{0,2},{1,3},{6,4},{7,5},{2,0},{3,1},{4,6},{5,7},{8,10},{9,11},{14,... | collective-permute-start | bytes 3145736 | tf_op jit(solution)/shard_map/ppermute | solution.py:571
  516.1 261.7 %all-gather.5.cloned.1.call-start = ((), (), s32[]{:S(2)}) async-start(), calls=%async_computation.5 | async-start | bytes 1769472 | tf_op jit(solution)/shard_map/all_gather | solution.py:109
  540.3 40.4 %collective-permute-start.86 = (bf16[512,1024]{1,0:T(8,128)(2,1)}, bf16[512,1024]{1,0:T(8,128)(2,1)}, u32[]{:S(2)}, u32[]{:S(2)}) collective-permute-start(bf16[512,1024]{1,0:T(8,128)(2,1)} %shard_map.277.refs_2_), channel_id=1, source_target_pairs={{0,2},{1,3},{6,4},{7,5},{2,0},{3,1},{4,6},{5,7},{8,10},{9,11},{14,... | collective-permute-start | bytes 3145736 | tf_op jit(solution)/shard_map/ppermute | solution.py:571
  543.2 41.0 %collective-permute-start.71 = (bf16[1024,512]{1,0:T(8,128)(2,1)}, bf16[1024,512]{1,0:T(8,128)(2,1)}, u32[]{:S(2)}, u32[]{:S(2)}) collective-permute-start(bf16[1024,512]{1,0:T(8,128)(2,1)} %get-tuple-element.208.refs_1_), channel_id=1, source_target_pairs={{2,4},{3,5},{4,2},{5,3},{10,12},{11,13},{12,10},{13,11},{18,20},{1... | collective-permute-start | bytes 3145736 | tf_op jit(solution)/shard_map/ppermute | solution.py:586
  544.8 43.2 %collective-permute-start.72 = (bf16[1024,512]{1,0:T(8,128)(2,1)}, bf16[1024,512]{1,0:T(8,128)(2,1)}, u32[]{:S(2)}, u32[]{:S(2)}) collective-permute-start(bf16[1024,512]{1,0:T(8,128)(2,1)} %get-tuple-element.209.here_ref), channel_id=1, source_target_pairs={{0,1},{1,0},{2,3},{3,2},{4,5},{5,4},{6,7},{7,6},{8,9},{9,8},{10,11... | collective-permute-start | bytes 3145736 | tf_op jit(solution)/shard_map/ppermute | solution.py:590
  601.5 40.3 %collective-permute-start.96 = (bf16[1024,512]{1,0:T(8,128)(2,1)S(1)}, bf16[1024,512]{1,0:T(8,128)(2,1)S(1)}, u32[]{:S(2)}, u32[]{:S(2)}) collective-permute-start(bf16[1024,512]{1,0:T(8,128)(2,1)S(1)} %shard_map.290.refs_2_), channel_id=1, source_target_pairs={{0,2},{1,3},{6,4},{7,5},{2,0},{3,1},{4,6},{5,7},{8,10},{9,11},{14,... | collective-permute-start | bytes 3145736 | tf_op jit(solution)/shard_map/ppermute | solution.py:571
  619.5 48.5 %collective-permute-start.94 = (bf16[512,1024]{1,0:T(8,128)(2,1)}, bf16[512,1024]{1,0:T(8,128)(2,1)}, u32[]{:S(2)}, u32[]{:S(2)}) collective-permute-start(bf16[512,1024]{1,0:T(8,128)(2,1)} %shard_map.288.refs_2_), channel_id=1, source_target_pairs={{0,2},{1,3},{6,4},{7,5},{2,0},{3,1},{4,6},{5,7},{8,10},{9,11},{14,... | collective-permute-start | bytes 3145736 | tf_op jit(solution)/shard_map/ppermute | solution.py:571
  623.5 48.3 %collective-permute-start.84 = (bf16[1024,512]{1,0:T(8,128)(2,1)}, bf16[1024,512]{1,0:T(8,128)(2,1)S(1)}, u32[]{:S(2)}, u32[]{:S(2)}) collective-permute-start(bf16[1024,512]{1,0:T(8,128)(2,1)} %get-tuple-element.229.refs_1_), channel_id=1, source_target_pairs={{2,4},{3,5},{4,2},{5,3},{10,12},{11,13},{12,10},{13,11},{18,20},{1... | collective-permute-start | bytes 3145736 | tf_op jit(solution)/shard_map/ppermute | solution.py:586
  624.2 49.0 %collective-permute-start.85 = (bf16[1024,512]{1,0:T(8,128)(2,1)}, bf16[1024,512]{1,0:T(8,128)(2,1)}, u32[]{:S(2)}, u32[]{:S(2)}) collective-permute-start(bf16[1024,512]{1,0:T(8,128)(2,1)} %get-tuple-element.230.here_ref), channel_id=1, source_target_pairs={{0,1},{1,0},{2,3},{3,2},{4,5},{5,4},{6,7},{7,6},{8,9},{9,8},{10,11... | collective-permute-start | bytes 3145736 | tf_op jit(solution)/shard_map/ppermute | solution.py:590
  643.9 44.0 %collective-permute-start.98 = (bf16[1024,512]{1,0:T(8,128)(2,1)}, bf16[1024,512]{1,0:T(8,128)(2,1)}, u32[]{:S(2)}, u32[]{:S(2)}) collective-permute-start(bf16[1024,512]{1,0:T(8,128)(2,1)} %get-tuple-element.252.here_ref), channel_id=1, source_target_pairs={{0,1},{1,0},{2,3},{3,2},{4,5},{5,4},{6,7},{7,6},{8,9},{9,8},{10,11... | collective-permute-start | bytes 3145736 | tf_op jit(solution)/shard_map/ppermute | solution.py:590
  677.5 45.6 %collective-permute-start.92 = (bf16[1024,512]{1,0:T(8,128)(2,1)S(1)}, bf16[1024,512]{1,0:T(8,128)(2,1)S(1)}, u32[]{:S(2)}, u32[]{:S(2)}) collective-permute-start(bf16[1024,512]{1,0:T(8,128)(2,1)S(1)} %shard_map.286.refs_1_), channel_id=1, source_target_pairs={{2,0},{3,1},{4,6},{5,7},{10,8},{11,9},{12,14},{13,15},{18,16},{19,... | collective-permute-start | bytes 3145736 | tf_op jit(solution)/shard_map/ppermute | solution.py:571
  712.0 50.8 %collective-permute-start.102 = (bf16[512,1024]{1,0:T(8,128)(2,1)S(1)}, bf16[512,1024]{1,0:T(8,128)(2,1)}, u32[]{:S(2)}, u32[]{:S(2)}) collective-permute-start(bf16[512,1024]{1,0:T(8,128)(2,1)S(1)} %shard_map.296.refs_1_), channel_id=1, source_target_pairs={{2,0},{3,1},{4,6},{5,7},{10,8},{11,9},{12,14},{13,15},{18,16},{19,... | collective-permute-start | bytes 3145736 | tf_op jit(solution)/shard_map/ppermute | solution.py:571
  723.2 46.8 %collective-permute-start.93 = (bf16[1024,512]{1,0:T(8,128)(2,1)S(1)}, bf16[1024,512]{1,0:T(8,128)(2,1)}, u32[]{:S(2)}, u32[]{:S(2)}) collective-permute-start(bf16[1024,512]{1,0:T(8,128)(2,1)S(1)} %shard_map.294.here_ref), channel_id=1, source_target_pairs={{0,1},{1,0},{2,3},{3,2},{4,5},{5,4},{6,7},{7,6},{8,9},{9,8},{10,11... | collective-permute-start | bytes 3145736 | tf_op jit(solution)/shard_map/ppermute | solution.py:590
  730.3 43.6 %collective-permute-start.101 = (bf16[1024,512]{1,0:T(8,128)(2,1)S(1)}, bf16[1024,512]{1,0:T(8,128)(2,1)}, u32[]{:S(2)}, u32[]{:S(2)}) collective-permute-start(bf16[1024,512]{1,0:T(8,128)(2,1)S(1)} %shard_map.302.here_ref), channel_id=1, source_target_pairs={{0,1},{1,0},{2,3},{3,2},{4,5},{5,4},{6,7},{7,6},{8,9},{9,8},{10,11... | collective-permute-start | bytes 3145736 | tf_op jit(solution)/shard_map/ppermute | solution.py:590
  (189 other events, 2963.0 us)
Sparse Core Ops, SparseCore 0:
  35.4 49.0 all-gather.2
  276.5 96.3 reduce-scatter.2
  516.2 37.3 reduce-scatter.4
  644.4 41.9 all-gather.4

commit v3 on v2

--- a/solution.py
+++ b/solution.py
@@ -205,7 +205,7 @@
     return (keys <= rows) & (keys >= starts)
 
 
-def attend_body(low_ref, high_ref, where_ref, q_ref, kv_ref, starts_ref, o_ref, ext_ref, qs, ms, ls, accs):
+def attend_body(low_ref, high_ref, where_ref, q_ref, kv_ref, starts_ref, o_ref, ext_ref, qs, tops, sums, accs):
     low_half = lanes_of(BLOCK) < HEAD
     for qb in range(q_ref.shape[0] // BLOCK):
         rows = slice(qb * BLOCK, (qb + 1) * BLOCK)
@@ -214,32 +214,43 @@
                 q_ref[rows, 256 * j : 256 * j + 128].astype(F32),
                 q_ref[rows, 256 * j + 128 : 256 * j + 256].astype(F32),
             ).astype(BF16)
-        ms[...] = jnp.full(ms.shape, NEG, F32)
-        ls[...] = jnp.zeros(ls.shape, F32)
+        tops[...] = jnp.full(tops.shape, NEG, F32)
+        sums[...] = jnp.zeros(sums.shape, F32)
         accs[...] = jnp.zeros(accs.shape, F32)
-        high = high_ref[qb]
-
-        def step(b, carry):
+        low, high = low_ref[qb], high_ref[qb]
+
+        def scores_of(b, at, seen, j):
+            key = kv_ref[pl.ds(at, BLOCK), 128 * j : 128 * j + 128]
+            scores = dot_nt(qs[j], key).reshape(4, BLOCK, BLOCK)
+            return jnp.where(seen, scores, NEG).reshape(4 * BLOCK, BLOCK)
+
+        def find_top(b, carry):
             at = pl.multiple_of(where_ref[b] * BLOCK, BLOCK)
             seen = visible(high, b, starts_ref[rows, :])[None]
             for j in range(PAIRS):
-                key = kv_ref[pl.ds(at, BLOCK), 128 * j : 128 * j + 128]
+                tops[j] = jnp.maximum(tops[j], scores_of(b, at, seen, j))
+            return carry
+
+        lax.fori_loop(low, high + 1, find_top, 0)
+        for j in range(PAIRS):
+            top = jnp.max(tops[j], axis=-1, keepdims=True)
+            tops[j] = jnp.broadcast_to(top, tops.shape[1:])
+
+        def gather_values(b, carry):
+            at = pl.multiple_of(where_ref[b] * BLOCK, BLOCK)
+            seen = visible(high, b, starts_ref[rows, :])[None]
+            for j in range(PAIRS):
                 value = kv_ref[pl.ds(at, BLOCK), KVD + 128 * j : KVD + 128 * j + 128]
-                scores = dot_nt(qs[j], key).reshape(4, BLOCK, BLOCK)
-                scores = jnp.where(seen, scores, NEG).reshape(4 * BLOCK, BLOCK)
-                old = ms[j]
-                new = jnp.maximum(old, jnp.max(scores, axis=-1, keepdims=True))
-                weights = jnp.exp(scores - new)
-                shrink = jnp.exp(old - new)
-                ls[j] = ls[j] * shrink + jnp.sum(weights, axis=-1, keepdims=True)
-                accs[j] = accs[j] * shrink + dot_nn(weights.astype(BF16), value)
-                ms[j] = new
+                weights = jnp.exp(scores_of(b, at, seen, j) - tops[j])
+                sums[j] += weights
+                accs[j] += dot_nn(weights.astype(BF16), value)
             return carry
 
-        lax.fori_loop(low_ref[qb], high + 1, step, 0)
+        lax.fori_loop(low, high + 1, gather_values, 0)
         for j in range(PAIRS):
-            attended = accs[j] / ls[j]
-            total = ms[j] + jnp.log(ls[j])
+            weight = jnp.sum(sums[j], axis=-1, keepdims=True)
+            attended = accs[j] / weight
+            total = tops[j] + jnp.log(weight)
             left, right = join_heads(attended)
             o_ref[rows, 256 * j : 256 * j + 128] = left.astype(BF16)
             o_ref[rows, 256 * j + 128 : 256 * j + 256] = right.astype(BF16)
@@ -269,8 +280,11 @@
             for h in range(4):
                 part = slice(h * BLOCK, (h + 1) * BLOCK)
                 ext = ext_ref[j, h, rows, :]
-                ds[j, part, :] = jnp.sum(grad[part] * ext, axis=-1, keepdims=True)
-                lse[j, part, :] = ext[:, 127:128] if h < 2 else ext[:, 0:1]
+                flat = (BLOCK, BLOCK)
+                delta = jnp.sum(grad[part] * ext, axis=-1, keepdims=True)
+                total = ext[:, 127:128] if h < 2 else ext[:, 0:1]
+                ds[j, part, :] = jnp.broadcast_to(delta, flat)
+                lse[j, part, :] = jnp.broadcast_to(total, flat)
         dqs[...] = jnp.zeros(dqs.shape, F32)
         high = high_ref[qb]
 
@@ -589,8 +603,8 @@
         if old:
             self.swaps.append((finished, lax.ppermute(finished, "ctx", self.beside)))
 
-    def hold(self, value):
-        return tie(value, self.marks[-2:-1])
+    def hold(self, value, step):
+        return tie(value, self.marks[step : step + 1] + self.across[max(step - 1, 0) : step])
 
     def finish(self):
         while self.done < len(self.swaps):
@@ -767,8 +781,8 @@
             [((rows, wide), BF16), ((PAIRS, 4, rows, 128), F32)],
             [
                 pltpu.VMEM((PAIRS, 4 * BLOCK, 128), BF16),
-                pltpu.VMEM((PAIRS, 4 * BLOCK, 1), F32),
-                pltpu.VMEM((PAIRS, 4 * BLOCK, 1), F32),
+                pltpu.VMEM((PAIRS, 4 * BLOCK, 128), F32),
+                pltpu.VMEM((PAIRS, 4 * BLOCK, 128), F32),
                 pltpu.VMEM((PAIRS, 4 * BLOCK, 128), F32),
             ],
             flops=rows * blocks * BLOCK * wide * 4,
@@ -790,8 +804,8 @@
             if pairs:
                 line.step(after)
 
-        def hold(value):
-            return value
+        def hold(value, step):
+            return line.hold(value, step) if pairs else value
 
         for first, number in groups:
             at = jnp.stack([base + first, me_dp * local + base + first])
@@ -812,16 +826,15 @@
             return call(
                 combine_body(held_blocks, rows, groups),
                 [],
-                [hold(tie(slots_t, after))] + [res[index] for res in results],
+                [tie(slots_t, after)] + [res[index] for res in results],
                 [((rows, wide), BF16)] * held_blocks,
             )
 
         def settle(parts, between):
             kept = [dp_cores(parts[s : s + n_dp], n_dp) for s in range(0, held_blocks, n_dp)]
             between(kept)
-            totals = [dp_rest(hold(k), n_dp) for k in kept]
+            totals = [dp_rest(k, n_dp) for k in kept]
             between(totals)
-            totals = hold(totals)
             if pairs:
                 totals[0] = totals[0] + lax.ppermute(
                     totals[1].astype(BF16), "ctx", beside
@@ -840,13 +853,13 @@
             )
         back = [back[0]] + [lax.ppermute(back[s], "dp", xor_pairs(n_dp, s)) for s in range(1, n_dp)]
         dgate_t = in_order(back, me_dp).reshape(EXPERTS, rows)
-        g_parts = combine(6, [])
+        g_parts = combine(6, line.marks[:1] if pairs else [])
         grad_act_two = settle(g_parts, lambda values: None)
         step(grad_act_two)
         res = call(
             after_body(n_dp),
             [me],
-            [mixed, hold(grad_act_two), out_grad, gain_two, gates, dgate_t, router_t, act_two, attended] + wo,
+            [mixed, hold(grad_act_two, 1), out_grad, gain_two, gates, dgate_t, router_t, act_two, attended] + wo,
             [((rows, wide), F32), ((rows, wide), BF16), ((EXPERTS, wide), F32), ((1, wide), F32)]
             + [((width, wide), BF16)] * n_dp,
             [pltpu.VMEM((n_dp, rows, width), BF16), pltpu.VMEM((n_dp, rows, width), BF16)],
@@ -856,29 +869,29 @@
         grad_query, kv_grads = call(
             attend_back_body,
             [low_blocks, mine, where_block],
-            [query, every_kv, starts, hold(grad_heads), extended, cosine, sine],
+            [query, every_kv, starts, grad_heads, extended, cosine, sine],
             [((rows, wide), BF16), ((blocks * BLOCK, 2 * KVD), BF16)],
             [
                 pltpu.VMEM((PAIRS, 4 * BLOCK, 128), BF16),
                 pltpu.VMEM((PAIRS, 4 * BLOCK, 128), BF16),
-                pltpu.VMEM((PAIRS, 4 * BLOCK, 1), F32),
-                pltpu.VMEM((PAIRS, 4 * BLOCK, 1), F32),
+                pltpu.VMEM((PAIRS, 4 * BLOCK, 128), F32),
+                pltpu.VMEM((PAIRS, 4 * BLOCK, 128), F32),
                 pltpu.VMEM((PAIRS, 4 * BLOCK, 128), F32),
                 pltpu.VMEM((blocks * BLOCK, 2 * KVD), F32),
             ],
             flops=rows * blocks * BLOCK * wide * 10,
         )
         step(grad_query)
-        kv_grad = ring_scatter(kv_grads, n_ctx)
+        kv_grad = ring_scatter(hold(kv_grads, 2), n_ctx)
         y_parts = combine(5, [grad_query])
         y_total = settle(y_parts, lambda values: None)
         layer_output = mixed + y_total
-        dense_out = dp_reduce(hold(out_parts), n_dp).astype(BF16)
+        dense_out = dp_reduce(out_parts, n_dp).astype(BF16)
         step(layer_output)
         res = call(
             first_body(n_dp),
             [me],
-            [layer_input, gain_one, cosine, sine, act_one, grad_query, hold(kv_grad), grad_mixed] + wq + wkv,
+            [layer_input, gain_one, cosine, sine, act_one, grad_query, kv_grad, grad_mixed] + wq + wkv,
             [((rows, wide), F32), ((1, wide), F32)]
             + [((width, wide), BF16)] * n_dp
             + [((width, 2 * KVD), BF16)] * n_dp,
@@ -888,7 +901,7 @@
         q_parts, kv_parts = res[2 : 2 + n_dp], res[2 + n_dp :]
         step(gain_one_part)
 
-        dense_q = dp_reduce(hold(q_parts), n_dp).astype(BF16)
+        dense_q = dp_reduce(q_parts, n_dp).astype(BF16)
         dense_kv = dp_reduce(kv_parts, n_dp).astype(BF16)
         dense = jnp.concatenate([dense_out, dense_q, dense_kv], axis=0)
         dense = ring_gather(ring_scatter(dense, n_ctx), n_ctx).astype(F32)

time: 808 us -> 736 us (0.911)
  starting transfers between devices: 147 us -> 103 us
  Pallas kernels: 213 us -> 198 us
  waiting for transfers between devices: 340 us -> 331 us
    ppermute x15, waiting for transfers between devices: 161 us -> 128 us  [step(): lax.ppermute(sent, 'ctx', (TO_INNER if new else []) + (TO_OUTER if old el...]
    ppermute x15, starting transfers between devices: 75.8 us -> 42.8 us  [step(): lax.ppermute(sent, 'ctx', (TO_INNER if new else []) + (TO_OUTER if old el...]
    ppermute x7, waiting for transfers between devices: 7.89 us -> 22.2 us  [dp_rest(): other = lax.ppermute(kept[i], 'dp', xor_pairs(count, 2 * i))]
    ppermute x12, starting transfers between devices: 17.9 us -> 7.51 us  [step(): self.swaps.append((finished, lax.ppermute(finished, 'ctx', self.beside)))]
    ppermute x2, waiting for transfers between devices: 2.47 us -> 11.3 us  [settle(): lax.ppermute(totals[1].astype(BF16), 'ctx', beside).astype(F32)]
    pallas_call x2, Pallas kernels: 52.2 us -> 44.1 us  [on_device(): expert_call(held_blocks, rows, local, served, first, number, gate_weight....]
    unnamed x237 -> x251, local copies, waits for them, and re-layouts: 36.7 us -> 29.9 us
  transfers between devices with their start and end apart: 108 -> 108, of which waited for: 35 -> 36; matrix products, arithmetic and copies ran while one was open for 6% -> 7% of each run, Pallas kernels for 16% -> 24%
where the time goes in v3:
time: 736 us; the launch traced here: 725 us
  waiting for transfers between devices  331 us (45%)
  Pallas kernels  198 us (27%)
  starting transfers between devices  103 us (14%)
  local copies, waits for them, and re-layouts  45.2 us (6%)
  other arithmetic  31 us (4%)
  between operations  15.9 us (2%)
    ppermute x15, waiting for transfers between devices, step(): lax.ppermute(sent, 'ctx', (TO_INNER if new else []) + (TO_OUTER if old el...  128 us
    pallas_call x36, Pallas kernels, call(): pl.pallas_call(body, cost_estimate=cost(flops, arrays, outs), in_specs=[s...  105 us
    ppermute x12, waiting for transfers between devices, step(): self.swaps.append((finished, lax.ppermute(finished, 'ctx', self.beside)))  54.5 us
    ppermute x10, waiting for transfers between devices, dp_gather(): pieces[step] = lax.ppermute(block, 'dp', xor_pairs(count, step))  53.3 us
    pallas_call x12, Pallas kernels, store_pair(): pl.pallas_call(body, grid_spec=pltpu.PrefetchScalarGridSpec(num_scalar_pr...  48.9 us
    pallas_call x2, Pallas kernels, on_device(): expert_call(held_blocks, rows, local, served, first, number, gate_weight....  44.1 us
    ppermute x15, starting transfers between devices, step(): lax.ppermute(sent, 'ctx', (TO_INNER if new else []) + (TO_OUTER if old el...  42.8 us
    ppermute x3, waiting for transfers between devices, on_device(): tiny = tiny + lax.ppermute(tiny, 'ctx', xor_pairs(n_ctx, bit))  32.2 us
  transfers between devices with their start and end apart: 108, of which 36 were waited for; matrix products, arithmetic and copies ran while one was open for 7% of the time, Pallas kernels for 24%

profile of v3, /device:TPU:0, one launch (start us, length us, event | category | flops | bytes accessed | tf_op | source)
XLA Modules:
  0.0 725.1 jit_solution(12073300960347977708)
XLA Ops:
  44.7 5.6 collective-permute-done.20
  56.5 8.8 %collective-permute-done.11.refs_10_ = bf16[256,1024]{1,0:T(8,128)(2,1)S(1)} collective-permute-done((bf16[256,1024]{1,0:T(8,128)(2,1)}, bf16[256,1024]{1,0:T(8,128)(2,1)S(1)}, u32[]{:S(2)}, u32[]{:S(2)}) %collective-permute-start.11) | collective-permute-done | bytes 524320 | tf_op jit(solution)/shard_map/ppermute | solution.py:67
  65.3 11.2 %collective-permute-done.17.rest_2_ = bf16[256,1024]{1,0:T(8,128)(2,1)S(1)} collective-permute-done((bf16[256,1024]{1,0:T(8,128)(2,1)S(1)}, bf16[256,1024]{1,0:T(8,128)(2,1)S(1)}, u32[]{:S(2)}, u32[]{:S(2)}) %collective-permute-start.17) | collective-permute-done | bytes 524320 | tf_op jit(solution)/shard_map/ppermute | solution.py:67
  77.1 9.4 %collective-permute-done.14.refs_14_ = bf16[256,1024]{1,0:T(8,128)(2,1)S(1)} collective-permute-done((bf16[256,1024]{1,0:T(8,128)(2,1)}, bf16[256,1024]{1,0:T(8,128)(2,1)S(1)}, u32[]{:S(2)}, u32[]{:S(2)}) %collective-permute-start.14) | collective-permute-done | bytes 524320 | tf_op jit(solution)/shard_map/ppermute | solution.py:67
  99.0 15.8 %shard_map.258 = (bf16[256,1024]{1,0:T(8,128)(2,1)S(1)}, f32[4,4,256,128]{3,2,1,0:T(8,128)S(1)}) custom-call(s32[2]{0:T(128)S(1)} %copy-done.85, s32[2]{0:T(128)S(1)} %get-tuple-element.271.high_ref, s32[16]{0:T(128)S(1)} %select_reduce_fusion.where_ref, bf16[256,1024]{1,0:T(8,128)(2,1)S(1)} %copy-done.66, ...), custom_call_target="tpu_custom_call" | custom-call | flops 2147483648 | bytes 7341056 | tf_op jit(solution)/shard_map/pallas_call | solution.py:49
  120.1 8.6 %collective-permute-done.29.refs_4_ = bf16[256,1024]{1,0:T(8,128)(2,1)S(1)} collective-permute-done((bf16[256,1024]{1,0:T(8,128)(2,1)S(1)}, bf16[256,1024]{1,0:T(8,128)(2,1)S(1)}, u32[]{:S(2)}, u32[]{:S(2)}) %collective-permute-start.29) | collective-permute-done | bytes 524320 | tf_op jit(solution)/shard_map/ppermute | solution.py:754
  133.7 10.8 %collective-permute-done.31.refs_6_ = bf16[256,1024]{1,0:T(8,128)(2,1)S(1)} collective-permute-done((bf16[256,1024]{1,0:T(8,128)(2,1)S(1)}, bf16[256,1024]{1,0:T(8,128)(2,1)S(1)}, u32[]{:S(2)}, u32[]{:S(2)}) %collective-permute-start.31) | collective-permute-done | bytes 524320 | tf_op jit(solution)/shard_map/ppermute | solution.py:67
  148.2 14.3 %shard_map.260 = (bf16[1,1024,512]{2,1,0:T(8,128)(2,1)}, bf16[1,1024,512]{2,1,0:T(8,128)(2,1)}, bf16[1,512,1024]{2,1,0:T(8,128)(2,1)}, f32[32,256]{1,0:T(8,128)}...) custom-call(s32[2]{0:T(128)} %get-tuple-element.309.at_ref, ...), custom_call_target="tpu_custom_call" | custom-call | flops 5368709120 | bytes 14680064 | tf_op jit(solution)/shard_map/pallas_call | solution.py:813
  166.5 29.8 %shard_map.261 = (bf16[3,1024,512]{2,1,0:T(8,128)(2,1)}, bf16[3,1024,512]{2,1,0:T(8,128)(2,1)}, bf16[3,512,1024]{2,1,0:T(8,128)(2,1)}, f32[32,256]{1,0:T(8,128)}...) custom-call(s32[2]{0:T(128)} %get-tuple-element.310.at_ref, ...), custom_call_target="tpu_custom_call" | custom-call | flops 16106127360 | bytes 27262976 | tf_op jit(solution)/shard_map/pallas_call | solution.py:813
  207.6 9.4 %collective-permute-done.39 = bf16[256,1024]{1,0:T(8,128)(2,1)S(1)} collective-permute-done((bf16[256,1024]{1,0:T(8,128)(2,1)S(1)}, bf16[256,1024]{1,0:T(8,128)(2,1)S(1)}, u32[]{:S(2)}, u32[]{:S(2)}) %collective-permute-start.39) | collective-permute-done | bytes 524320 | tf_op jit(solution)/shard_map/ppermute | solution.py:84
  221.5 9.7 %collective-permute-done.43 = f32[4,4,256]{2,1,0:T(4,128)S(1)} collective-permute-done((f32[4,4,256]{2,1,0:T(4,128)S(1)}, f32[4,4,256]{2,1,0:T(4,128)S(1)}, u32[]{:S(2)}, u32[]{:S(2)}) %collective-permute-start.43) | collective-permute-done | bytes 16416 | tf_op jit(solution)/shard_map/ppermute | solution.py:847
  237.0 6.5 collective-permute-start.54
  253.6 23.8 %shard_map.265 = (bf16[256,1024]{1,0:T(8,128)(2,1)S(1)}, bf16[2048,1024]{1,0:T(8,128)(2,1)}) custom-call(s32[2]{0:T(128)S(1)} %copy-done.86, s32[2]{0:T(128)S(1)} %get-tuple-element.271.high_ref, s32[16]{0:T(128)S(1)} %copy-done.84, bf16[256,1024]{1,0:T(8,128)(2,1)S(1)} %copy-done.67, bf16[2048,1024]{1,0:T(8,128)(2,1)} %all-gather.3.cloned.1.call-done.kv_ref, ...), custom_call_target="tpu_custom_call" | custom-call | flops 5368709120 | bytes 12321792 | tf_op jit(solution)/shard_map/pallas_call | solution.py:49
  288.8 12.5 %collective-permute-done.52 = bf16[256,1024]{1,0:T(8,128)(2,1)S(1)} collective-permute-done((bf16[256,1024]{1,0:T(8,128)(2,1)S(1)}, bf16[256,1024]{1,0:T(8,128)(2,1)S(1)}, u32[]{:S(2)}, u32[]{:S(2)}) %collective-permute-start.52) | collective-permute-done | bytes 524320 | tf_op jit(solution)/shard_map/ppermute | solution.py:84
  303.1 9.1 %collective-permute-start.70 = (bf16[1024,512]{1,0:T(8,128)(2,1)S(1)}, bf16[1024,512]{1,0:T(8,128)(2,1)S(1)}, u32[]{:S(2)}, u32[]{:S(2)}) collective-permute-start(bf16[1024,512]{1,0:T(8,128)(2,1)S(1)} %shard_map.269.refs_2_), channel_id=1, source_target_pairs={{0,2},{1,3},{6,4},{7,5},{2,0},{3,1},{4,6},{5,7},{8,10},{9,11},{14,... | collective-permute-start | bytes 3145736 | tf_op jit(solution)/shard_map/ppermute | solution.py:585
  315.7 11.3 %collective-permute-done.53 = bf16[256,1024]{1,0:T(8,128)(2,1)S(1)} collective-permute-done((bf16[256,1024]{1,0:T(8,128)(2,1)S(1)}, bf16[256,1024]{1,0:T(8,128)(2,1)S(1)}, u32[]{:S(2)}, u32[]{:S(2)}) %collective-permute-start.53) | collective-permute-done | bytes 524320 | tf_op jit(solution)/shard_map/ppermute | solution.py:839
  328.4 30.5 %collective-permute-done.70.refs_0_ = bf16[1024,512]{1,0:T(8,128)(2,1)S(1)} collective-permute-done((bf16[1024,512]{1,0:T(8,128)(2,1)S(1)}, bf16[1024,512]{1,0:T(8,128)(2,1)S(1)}, u32[]{:S(2)}, u32[]{:S(2)}) %collective-permute-start.70) | collective-permute-done | bytes 1048608 | tf_op jit(solution)/shard_map/ppermute | solution.py:585
  371.0 6.6 shard_map.268
  377.7 5.8 collective-permute-start.77
  394.1 12.8 %collective-permute-done.77.refs_0_ = bf16[512,1024]{1,0:T(8,128)(2,1)S(1)} collective-permute-done((bf16[512,1024]{1,0:T(8,128)(2,1)S(1)}, bf16[512,1024]{1,0:T(8,128)(2,1)S(1)}, u32[]{:S(2)}, u32[]{:S(2)}) %collective-permute-start.77) | collective-permute-done | bytes 1048608 | tf_op jit(solution)/shard_map/ppermute | solution.py:585
  438.5 15.3 %collective-permute-done.82.there_ref = bf16[512,1024]{1,0:T(8,128)(2,1)} collective-permute-done((bf16[512,1024]{1,0:T(8,128)(2,1)}, bf16[512,1024]{1,0:T(8,128)(2,1)}, u32[]{:S(2)}, u32[]{:S(2)}) %collective-permute-start.82) | collective-permute-done | bytes 1048608 | tf_op jit(solution)/shard_map/ppermute | solution.py:604
  465.8 18.4 %collective-permute-done.88.refs_0_ = bf16[1024,512]{1,0:T(8,128)(2,1)} collective-permute-done((bf16[1024,512]{1,0:T(8,128)(2,1)}, bf16[1024,512]{1,0:T(8,128)(2,1)}, u32[]{:S(2)}, u32[]{:S(2)}) %collective-permute-start.88) | collective-permute-done | bytes 1048608 | tf_op jit(solution)/shard_map/ppermute | solution.py:585
  489.1 15.9 %collective-permute-done.86.refs_0_ = bf16[512,1024]{1,0:T(8,128)(2,1)} collective-permute-done((bf16[512,1024]{1,0:T(8,128)(2,1)}, bf16[512,1024]{1,0:T(8,128)(2,1)}, u32[]{:S(2)}, u32[]{:S(2)}) %collective-permute-start.86) | collective-permute-done | bytes 1048608 | tf_op jit(solution)/shard_map/ppermute | solution.py:585
  527.2 11.6 %collective-permute-done.91.there_ref = bf16[512,1024]{1,0:T(8,128)(2,1)S(1)} collective-permute-done((bf16[512,1024]{1,0:T(8,128)(2,1)S(1)}, bf16[512,1024]{1,0:T(8,128)(2,1)S(1)}, u32[]{:S(2)}, u32[]{:S(2)}) %collective-permute-start.91) | collective-permute-done | bytes 1048608 | tf_op jit(solution)/shard_map/ppermute | solution.py:604
  547.5 17.9 %collective-permute-done.96.refs_0_ = bf16[1024,512]{1,0:T(8,128)(2,1)S(1)} collective-permute-done((bf16[1024,512]{1,0:T(8,128)(2,1)S(1)}, bf16[1024,512]{1,0:T(8,128)(2,1)S(1)}, u32[]{:S(2)}, u32[]{:S(2)}) %collective-permute-start.96) | collective-permute-done | bytes 1048608 | tf_op jit(solution)/shard_map/ppermute | solution.py:585
  568.7 23.1 %collective-permute-done.94.refs_0_ = bf16[512,1024]{1,0:T(8,128)(2,1)} collective-permute-done((bf16[512,1024]{1,0:T(8,128)(2,1)}, bf16[512,1024]{1,0:T(8,128)(2,1)}, u32[]{:S(2)}, u32[]{:S(2)}) %collective-permute-start.94) | collective-permute-done | bytes 1048608 | tf_op jit(solution)/shard_map/ppermute | solution.py:585
  605.3 5.1 collective-permute-done.98.there_ref
  617.2 13.4 %collective-permute-done.99.there_ref = bf16[512,1024]{1,0:T(8,128)(2,1)} collective-permute-done((bf16[512,1024]{1,0:T(8,128)(2,1)}, bf16[512,1024]{1,0:T(8,128)(2,1)}, u32[]{:S(2)}, u32[]{:S(2)}) %collective-permute-start.99) | collective-permute-done | bytes 1048608 | tf_op jit(solution)/shard_map/ppermute | solution.py:604
  647.2 9.1 %collective-permute-done.100.refs_0_ = bf16[1024,512]{1,0:T(8,128)(2,1)S(1)} collective-permute-done((bf16[1024,512]{1,0:T(8,128)(2,1)S(1)}, bf16[1024,512]{1,0:T(8,128)(2,1)S(1)}, u32[]{:S(2)}, u32[]{:S(2)}) %collective-permute-start.100) | collective-permute-done | bytes 1048608 | tf_op jit(solution)/shard_map/ppermute | solution.py:585
  656.4 20.9 %collective-permute-done.66 = f32[34,1024]{1,0:T(8,128)S(1)} collective-permute-done((f32[34,1024]{1,0:T(8,128)S(1)}, f32[34,1024]{1,0:T(8,128)S(1)}, u32[]{:S(2)}, u32[]{:S(2)}) %collective-permute-start.66) | collective-permute-done | bytes 139296 | tf_op jit(solution)/shard_map/ppermute | solution.py:910
  677.4 6.9 collective-permute-done.67
  705.0 9.2 %collective-permute-done.103.there_ref = bf16[512,1024]{1,0:T(8,128)(2,1)S(1)} collective-permute-done((bf16[512,1024]{1,0:T(8,128)(2,1)}, bf16[512,1024]{1,0:T(8,128)(2,1)S(1)}, u32[]{:S(2)}, u32[]{:S(2)}) %collective-permute-start.103) | collective-permute-done | bytes 1048608 | tf_op jit(solution)/shard_map/ppermute | solution.py:604
  (572 shorter events, 290.2 us)
Async XLA Ops:
  7.2 90.1 %all-gather.3.cloned.1.call-start = ((), (), s32[]{:S(2)}) async-start(), calls=%async_computation.2 | async-start | bytes 4718592 | tf_op jit(solution)/shard_map/all_gather | solution.py:109
  35.3 332.6 %reduce-scatter.3.cloned.1.call-start = ((), (), s32[]{:S(2)}) async-start(), calls=%async_computation.3 | async-start | bytes 4718592 | tf_op jit(solution)/shard_map/reduce_scatter | solution.py:113
  52.3 34.1 %collective-permute-start.14 = (bf16[256,1024]{1,0:T(8,128)(2,1)}, bf16[256,1024]{1,0:T(8,128)(2,1)S(1)}, u32[]{:S(2)}, u32[]{:S(2)}) collective-permute-start(bf16[256,1024]{1,0:T(8,128)(2,1)} %collective-permute-done.refs_12_), channel_id=1, source_target_pairs={{0,16},{8,24},{16,0},{24,8},{1,17},{9,25},{17,1},{25,9},{2,18},{10... | collective-permute-start | bytes 1572872 | tf_op jit(solution)/shard_map/ppermute | solution.py:67
  56.0 37.6 %collective-permute-start.16 = (bf16[256,1024]{1,0:T(8,128)(2,1)S(1)}, bf16[256,1024]{1,0:T(8,128)(2,1)S(1)}, u32[]{:S(2)}, u32[]{:S(2)}) collective-permute-start(bf16[256,1024]{1,0:T(8,128)(2,1)S(1)} %copy-done.27), channel_id=1, source_target_pairs={{0,8},{8,0},{16,24},{24,16},{1,9},{9,1},{17,25},{25,17},{2,10},{10... | collective-permute-start | bytes 1572872 | tf_op jit(solution)/shard_map/ppermute | solution.py:69
  162.5 33.8 %collective-permute-start.33 = (bf16[1024,512]{1,0:T(8,128)(2,1)}, bf16[1024,512]{1,0:T(8,128)(2,1)S(1)}, u32[]{:S(2)}, u32[]{:S(2)}) collective-permute-start(bf16[1024,512]{1,0:T(8,128)(2,1)} %bitcast.122), channel_id=1, source_target_pairs={{0,2},{1,3},{6,4},{7,5},{8,10},{9,11},{14,12},{15,13},{16,18},{17,... | collective-permute-start | bytes 3145736 | tf_op jit(solution)/shard_map/ppermute | solution.py:585
  233.4 44.8 %collective-permute-start.55 = (bf16[1024,512]{1,0:T(8,128)(2,1)S(1)}, bf16[1024,512]{1,0:T(8,128)(2,1)S(1)}, u32[]{:S(2)}, u32[]{:S(2)}) collective-permute-start(bf16[1024,512]{1,0:T(8,128)(2,1)S(1)} %shard_map.267.refs_1_), channel_id=1, source_target_pairs={{2,4},{3,5},{4,2},{5,3},{10,12},{11,13},{12,10},{13,11},{18,20},{1... | collective-permute-start | bytes 3145736 | tf_op jit(solution)/shard_map/ppermute | solution.py:600
  237.0 42.2 %collective-permute-start.54 = (bf16[512,1024]{1,0:T(8,128)(2,1)S(1)}, bf16[512,1024]{1,0:T(8,128)(2,1)S(1)}, u32[]{:S(2)}, u32[]{:S(2)}) collective-permute-start(bf16[512,1024]{1,0:T(8,128)(2,1)S(1)} %bitcast.118), channel_id=1, source_target_pairs={{0,2},{1,3},{6,4},{7,5},{8,10},{9,11},{14,12},{15,13},{16,18},{17,... | collective-permute-start | bytes 3145736 | tf_op jit(solution)/shard_map/ppermute | solution.py:585
  280.2 288.5 %reduce-scatter.5.cloned.1.call-start = ((), (), s32[]{:S(2)}) async-start(), calls=%async_computation.4 | async-start | bytes 1769472 | tf_op jit(solution)/shard_map/reduce_scatter | solution.py:113
  303.1 55.8 %collective-permute-start.70 = (bf16[1024,512]{1,0:T(8,128)(2,1)S(1)}, bf16[1024,512]{1,0:T(8,128)(2,1)S(1)}, u32[]{:S(2)}, u32[]{:S(2)}) collective-permute-start(bf16[1024,512]{1,0:T(8,128)(2,1)S(1)} %shard_map.269.refs_2_), channel_id=1, source_target_pairs={{0,2},{1,3},{6,4},{7,5},{2,0},{3,1},{4,6},{5,7},{8,10},{9,11},{14,... | collective-permute-start | bytes 3145736 | tf_op jit(solution)/shard_map/ppermute | solution.py:585
  312.2 51.6 %collective-permute-start.76 = (bf16[512,1024]{1,0:T(8,128)(2,1)S(1)}, bf16[512,1024]{1,0:T(8,128)(2,1)S(1)}, u32[]{:S(2)}, u32[]{:S(2)}) collective-permute-start(bf16[512,1024]{1,0:T(8,128)(2,1)S(1)} %shard_map.275.refs_1_), channel_id=1, source_target_pairs={{2,4},{3,5},{4,2},{5,3},{10,12},{11,13},{12,10},{13,11},{18,20},{1... | collective-permute-start | bytes 3145736 | tf_op jit(solution)/shard_map/ppermute | solution.py:600
  328.4 55.2 %collective-permute-start.79 = (bf16[1024,512]{1,0:T(8,128)(2,1)}, bf16[1024,512]{1,0:T(8,128)(2,1)}, u32[]{:S(2)}, u32[]{:S(2)}) collective-permute-start(bf16[1024,512]{1,0:T(8,128)(2,1)} %shard_map.279.refs_2_), channel_id=1, source_target_pairs={{0,2},{1,3},{6,4},{7,5},{2,0},{3,1},{4,6},{5,7},{8,10},{9,11},{14,... | collective-permute-start | bytes 3145736 | tf_op jit(solution)/shard_map/ppermute | solution.py:585
  387.0 35.5 %collective-permute-start.80 = (bf16[1024,512]{1,0:T(8,128)(2,1)}, bf16[1024,512]{1,0:T(8,128)(2,1)}, u32[]{:S(2)}, u32[]{:S(2)}) collective-permute-start(bf16[1024,512]{1,0:T(8,128)(2,1)} %get-tuple-element.225.refs_1_), channel_id=1, source_target_pairs={{2,4},{3,5},{4,2},{5,3},{10,12},{11,13},{12,10},{13,11},{18,20},{1... | collective-permute-start | bytes 3145736 | tf_op jit(solution)/shard_map/ppermute | solution.py:600
  420.6 40.6 %collective-permute-start.73 = (bf16[1024,512]{1,0:T(8,128)(2,1)}, bf16[1024,512]{1,0:T(8,128)(2,1)}, u32[]{:S(2)}, u32[]{:S(2)}) collective-permute-start(bf16[1024,512]{1,0:T(8,128)(2,1)} %shard_map.271.refs_2_), channel_id=1, source_target_pairs={{0,2},{1,3},{6,4},{7,5},{2,0},{3,1},{4,6},{5,7},{8,10},{9,11},{14,... | collective-permute-start | bytes 3145736 | tf_op jit(solution)/shard_map/ppermute | solution.py:585
  422.6 35.4 %collective-permute-start.78 = (bf16[512,1024]{1,0:T(8,128)(2,1)}, bf16[512,1024]{1,0:T(8,128)(2,1)}, u32[]{:S(2)}, u32[]{:S(2)}) collective-permute-start(bf16[512,1024]{1,0:T(8,128)(2,1)} %get-tuple-element.222.refs_1_), channel_id=1, source_target_pairs={{2,4},{3,5},{4,2},{5,3},{10,12},{11,13},{12,10},{13,11},{18,20},{1... | collective-permute-start | bytes 3145736 | tf_op jit(solution)/shard_map/ppermute | solution.py:600
  434.8 49.4 %collective-permute-start.88 = (bf16[1024,512]{1,0:T(8,128)(2,1)}, bf16[1024,512]{1,0:T(8,128)(2,1)}, u32[]{:S(2)}, u32[]{:S(2)}) collective-permute-start(bf16[1024,512]{1,0:T(8,128)(2,1)} %shard_map.281.refs_2_), channel_id=1, source_target_pairs={{0,2},{1,3},{6,4},{7,5},{2,0},{3,1},{4,6},{5,7},{8,10},{9,11},{14,... | collective-permute-start | bytes 3145736 | tf_op jit(solution)/shard_map/ppermute | solution.py:585
  438.4 262.8 %all-gather.5.cloned.1.call-start = ((), (), s32[]{:S(2)}) async-start(), calls=%async_computation.5 | async-start | bytes 1769472 | tf_op jit(solution)/shard_map/all_gather | solution.py:109
  461.2 43.8 %collective-permute-start.86 = (bf16[512,1024]{1,0:T(8,128)(2,1)}, bf16[512,1024]{1,0:T(8,128)(2,1)}, u32[]{:S(2)}, u32[]{:S(2)}) collective-permute-start(bf16[512,1024]{1,0:T(8,128)(2,1)} %shard_map.278.refs_2_), channel_id=1, source_target_pairs={{0,2},{1,3},{6,4},{7,5},{2,0},{3,1},{4,6},{5,7},{8,10},{9,11},{14,... | collective-permute-start | bytes 3145736 | tf_op jit(solution)/shard_map/ppermute | solution.py:585
  464.2 44.4 %collective-permute-start.74 = (bf16[1024,512]{1,0:T(8,128)(2,1)}, bf16[1024,512]{1,0:T(8,128)(2,1)}, u32[]{:S(2)}, u32[]{:S(2)}) collective-permute-start(bf16[1024,512]{1,0:T(8,128)(2,1)} %get-tuple-element.218.refs_1_), channel_id=1, source_target_pairs={{2,4},{3,5},{4,2},{5,3},{10,12},{11,13},{12,10},{13,11},{18,20},{1... | collective-permute-start | bytes 3145736 | tf_op jit(solution)/shard_map/ppermute | solution.py:600
  465.8 45.0 %collective-permute-start.75 = (bf16[1024,512]{1,0:T(8,128)(2,1)}, bf16[1024,512]{1,0:T(8,128)(2,1)}, u32[]{:S(2)}, u32[]{:S(2)}) collective-permute-start(bf16[1024,512]{1,0:T(8,128)(2,1)} %get-tuple-element.219.here_ref), channel_id=1, source_target_pairs={{0,1},{1,0},{2,3},{3,2},{4,5},{5,4},{6,7},{7,6},{8,9},{9,8},{10,11... | collective-permute-start | bytes 3145736 | tf_op jit(solution)/shard_map/ppermute | solution.py:604
  525.5 40.0 %collective-permute-start.96 = (bf16[1024,512]{1,0:T(8,128)(2,1)S(1)}, bf16[1024,512]{1,0:T(8,128)(2,1)S(1)}, u32[]{:S(2)}, u32[]{:S(2)}) collective-permute-start(bf16[1024,512]{1,0:T(8,128)(2,1)S(1)} %shard_map.290.refs_2_), channel_id=1, source_target_pairs={{0,2},{1,3},{6,4},{7,5},{2,0},{3,1},{4,6},{5,7},{8,10},{9,11},{14,... | collective-permute-start | bytes 3145736 | tf_op jit(solution)/shard_map/ppermute | solution.py:585
  541.5 50.4 %collective-permute-start.94 = (bf16[512,1024]{1,0:T(8,128)(2,1)}, bf16[512,1024]{1,0:T(8,128)(2,1)}, u32[]{:S(2)}, u32[]{:S(2)}) collective-permute-start(bf16[512,1024]{1,0:T(8,128)(2,1)} %shard_map.288.refs_2_), channel_id=1, source_target_pairs={{0,2},{1,3},{6,4},{7,5},{2,0},{3,1},{4,6},{5,7},{8,10},{9,11},{14,... | collective-permute-start | bytes 3145736 | tf_op jit(solution)/shard_map/ppermute | solution.py:585
  546.0 49.6 %collective-permute-start.84 = (bf16[1024,512]{1,0:T(8,128)(2,1)}, bf16[1024,512]{1,0:T(8,128)(2,1)S(1)}, u32[]{:S(2)}, u32[]{:S(2)}) collective-permute-start(bf16[1024,512]{1,0:T(8,128)(2,1)} %get-tuple-element.235.refs_1_), channel_id=1, source_target_pairs={{2,4},{3,5},{4,2},{5,3},{10,12},{11,13},{12,10},{13,11},{18,20},{1... | collective-permute-start | bytes 3145736 | tf_op jit(solution)/shard_map/ppermute | solution.py:600
  546.7 51.8 %collective-permute-start.85 = (bf16[1024,512]{1,0:T(8,128)(2,1)}, bf16[1024,512]{1,0:T(8,128)(2,1)}, u32[]{:S(2)}, u32[]{:S(2)}) collective-permute-start(bf16[1024,512]{1,0:T(8,128)(2,1)} %get-tuple-element.236.here_ref), channel_id=1, source_target_pairs={{0,1},{1,0},{2,3},{3,2},{4,5},{5,4},{6,7},{7,6},{8,9},{9,8},{10,11... | collective-permute-start | bytes 3145736 | tf_op jit(solution)/shard_map/ppermute | solution.py:604
  566.9 37.2 %collective-permute-start.97 = (bf16[1024,512]{1,0:T(8,128)(2,1)}, bf16[1024,512]{1,0:T(8,128)(2,1)S(1)}, u32[]{:S(2)}, u32[]{:S(2)}) collective-permute-start(bf16[1024,512]{1,0:T(8,128)(2,1)} %get-tuple-element.256.refs_1_), channel_id=1, source_target_pairs={{2,4},{3,5},{4,2},{5,3},{10,12},{11,13},{12,10},{13,11},{18,20},{1... | collective-permute-start | bytes 3145736 | tf_op jit(solution)/shard_map/ppermute | solution.py:600
  567.6 42.8 %collective-permute-start.98 = (bf16[1024,512]{1,0:T(8,128)(2,1)}, bf16[1024,512]{1,0:T(8,128)(2,1)}, u32[]{:S(2)}, u32[]{:S(2)}) collective-permute-start(bf16[1024,512]{1,0:T(8,128)(2,1)} %get-tuple-element.258.here_ref), channel_id=1, source_target_pairs={{0,1},{1,0},{2,3},{3,2},{4,5},{5,4},{6,7},{7,6},{8,9},{9,8},{10,11... | collective-permute-start | bytes 3145736 | tf_op jit(solution)/shard_map/ppermute | solution.py:604
  595.6 35.0 %collective-permute-start.99 = (bf16[512,1024]{1,0:T(8,128)(2,1)}, bf16[512,1024]{1,0:T(8,128)(2,1)}, u32[]{:S(2)}, u32[]{:S(2)}) collective-permute-start(bf16[512,1024]{1,0:T(8,128)(2,1)} %get-tuple-element.263.here_ref), channel_id=1, source_target_pairs={{0,1},{1,0},{2,3},{3,2},{4,5},{5,4},{6,7},{7,6},{8,9},{9,8},{10,11... | collective-permute-start | bytes 3145736 | tf_op jit(solution)/shard_map/ppermute | solution.py:604
  602.8 43.3 %collective-permute-start.92 = (bf16[1024,512]{1,0:T(8,128)(2,1)S(1)}, bf16[1024,512]{1,0:T(8,128)(2,1)S(1)}, u32[]{:S(2)}, u32[]{:S(2)}) collective-permute-start(bf16[1024,512]{1,0:T(8,128)(2,1)S(1)} %shard_map.286.refs_1_), channel_id=1, source_target_pairs={{2,0},{3,1},{4,6},{5,7},{10,8},{11,9},{12,14},{13,15},{18,16},{19,... | collective-permute-start | bytes 3145736 | tf_op jit(solution)/shard_map/ppermute | solution.py:585
  614.7 41.5 %collective-permute-start.100 = (bf16[1024,512]{1,0:T(8,128)(2,1)S(1)}, bf16[1024,512]{1,0:T(8,128)(2,1)S(1)}, u32[]{:S(2)}, u32[]{:S(2)}) collective-permute-start(bf16[1024,512]{1,0:T(8,128)(2,1)S(1)} %shard_map.298.refs_1_), channel_id=1, source_target_pairs={{2,0},{3,1},{4,6},{5,7},{10,8},{11,9},{12,14},{13,15},{18,16},{19,... | collective-permute-start | bytes 3145736 | tf_op jit(solution)/shard_map/ppermute | solution.py:585
  634.8 51.9 %collective-permute-start.102 = (bf16[512,1024]{1,0:T(8,128)(2,1)S(1)}, bf16[512,1024]{1,0:T(8,128)(2,1)}, u32[]{:S(2)}, u32[]{:S(2)}) collective-permute-start(bf16[512,1024]{1,0:T(8,128)(2,1)S(1)} %shard_map.296.refs_1_), channel_id=1, source_target_pairs={{2,0},{3,1},{4,6},{5,7},{10,8},{11,9},{12,14},{13,15},{18,16},{19,... | collective-permute-start | bytes 3145736 | tf_op jit(solution)/shard_map/ppermute | solution.py:585
  641.6 35.7 %collective-permute-start.66 = (f32[34,1024]{1,0:T(8,128)S(1)}, f32[34,1024]{1,0:T(8,128)S(1)}, u32[]{:S(2)}, u32[]{:S(2)}) collective-permute-start(f32[34,1024]{1,0:T(8,128)S(1)} %fusion.15), channel_id=1, source_target_pairs={{0,2},{1,3},{2,0},{3,1},{4,6},{5,7},{6,4},{7,5},{8,10},{9,11},{10,... | collective-permute-start | bytes 417800 | tf_op jit(solution)/shard_map/ppermute | solution.py:910
  646.1 47.2 %collective-permute-start.93 = (bf16[1024,512]{1,0:T(8,128)(2,1)S(1)}, bf16[1024,512]{1,0:T(8,128)(2,1)}, u32[]{:S(2)}, u32[]{:S(2)}) collective-permute-start(bf16[1024,512]{1,0:T(8,128)(2,1)S(1)} %shard_map.294.here_ref), channel_id=1, source_target_pairs={{0,1},{1,0},{2,3},{3,2},{4,5},{5,4},{6,7},{7,6},{8,9},{9,8},{10,11... | collective-permute-start | bytes 3145736 | tf_op jit(solution)/shard_map/ppermute | solution.py:604
  656.3 41.0 %collective-permute-start.101 = (bf16[1024,512]{1,0:T(8,128)(2,1)S(1)}, bf16[1024,512]{1,0:T(8,128)(2,1)}, u32[]{:S(2)}, u32[]{:S(2)}) collective-permute-start(bf16[1024,512]{1,0:T(8,128)(2,1)S(1)} %shard_map.302.here_ref), channel_id=1, source_target_pairs={{0,1},{1,0},{2,3},{3,2},{4,5},{5,4},{6,7},{7,6},{8,9},{9,8},{10,11... | collective-permute-start | bytes 3145736 | tf_op jit(solution)/shard_map/ppermute | solution.py:604
  (196 other events, 2697.0 us)
Sparse Core Ops, SparseCore 0:
  35.5 49.0 all-gather.2
  280.3 85.3 reduce-scatter.2
  438.6 38.7 reduce-scatter.4
  568.8 39.4 all-gather.4

commit v4 on v3

--- a/solution.py
+++ b/solution.py
@@ -475,36 +475,31 @@
     return body
 
 
-def store_pair(held, here, there, places, total):
+def store_pair(held, here, there, column, e, served):
     rows, cols = here.shape
-
-    def body(at_ref, here_ref, there_ref, *rest):
-        out_ref = rest[-1]
-
-        @pl.when(pl.program_id(0) == 0)
-        def _():
-            out_ref[0] = here_ref[...].astype(F32)
-
-        @pl.when(pl.program_id(0) == 1)
-        def _():
-            out_ref[0] = there_ref[...].astype(F32)
+    part = rows // 4
+
+    def body(column_ref, here_ref, there_ref, *rest):
+        rest[-1][column_ref[0], 0] = here_ref[...].astype(F32)
+        rest[-1][1 - column_ref[0], 0] = there_ref[...].astype(F32)
 
     more = [] if held is None else [held]
     return pl.pallas_call(
         body,
+        cost_estimate=pl.CostEstimate(flops=0, transcendentals=0, bytes_accessed=12 * rows * cols),
         grid_spec=pltpu.PrefetchScalarGridSpec(
             num_scalar_prefetch=1,
-            grid=(2,),
-            in_specs=[pl.BlockSpec((rows, cols), lambda i, at: (0, 0))] * 2
+            grid=(4,),
+            in_specs=[pl.BlockSpec((part, cols), lambda i, c: (i, 0))] * 2
             + [pl.BlockSpec(memory_space=pl.ANY)] * len(more),
-            out_specs=pl.BlockSpec((1, rows, cols), lambda i, at: (at[i], 0, 0)),
+            out_specs=pl.BlockSpec((2, 1, part, cols), lambda i, c: (0, e, i, 0)),
         ),
-        out_shape=jax.ShapeDtypeStruct((total, rows, cols), F32),
+        out_shape=jax.ShapeDtypeStruct((2, served, rows, cols), F32),
         input_output_aliases={3: 0} if more else {},
         compiler_params=pltpu.CompilerParams(
             vmem_limit_bytes=24 << 20, dimension_semantics=("arbitrary",)
         ),
-    )(places, here, there, *more)
+    )(column, here, there, *more)
 
 
 TO_INNER = [(0, 2), (1, 3), (6, 4), (7, 5)]
@@ -556,9 +551,10 @@
 class LineSums:
     LAG = 3
 
-    def __init__(self, me, beside, base, base_there, total):
+    def __init__(self, me, beside, served):
         self.outer = ((me < 2) | (me >= 6)).astype(jnp.int32).reshape(1)
-        self.beside, self.base, self.base_there, self.total = beside, base, base_there, total
+        self.column = (me & 1).astype(jnp.int32).reshape(1)
+        self.beside, self.served = beside, served
         self.blocks, self.held = [], [None, None, None]
         self.sent, self.parts, self.across = {}, [], []
         self.swaps, self.marks, self.done = [], [], 0
@@ -571,8 +567,7 @@
         if self.done < len(self.swaps):
             here, there = self.swaps[self.done]
             e, m = divmod(self.done, 3)
-            places = jnp.stack([self.base + e, self.base_there + e])
-            self.held[m] = store_pair(self.held[m], here, there, places, self.total)
+            self.held[m] = store_pair(self.held[m], here, there, self.column, e, self.served)
             self.done += 1
 
     def step(self, after=()):
@@ -609,7 +604,7 @@
     def finish(self):
         while self.done < len(self.swaps):
             self.store()
-        return self.held
+        return [h.reshape((2 * self.served,) + h.shape[2:]) for h in self.held]
 
 
 def after_body(count):
@@ -798,7 +793,7 @@
         acts_all = reach(act_two)
         groups = [(0, 1), (1, served - 1)] if pairs else [(0, served)]
         results = []
-        line = LineSums(me_ctx, beside, base, (1 - column) * served, local) if pairs else None
+        line = LineSums(me_ctx, beside, served) if pairs else None
 
         def step(*after):
             if pairs:

time: 736 us -> 728 us (0.989)
  Pallas kernels: 198 us -> 163 us
  starting transfers between devices: 103 us -> 136 us
  waiting for transfers between devices: 331 us -> 339 us
    pallas_call x36, Pallas kernels: 105 us -> 78 us  [call(): pl.pallas_call(body, cost_estimate=cost(flops, arrays, outs), in_specs=[s...]
    ppermute x12, waiting for transfers between devices: 54.5 us -> 74.7 us  [step(): self.swaps.append((finished, lax.ppermute(finished, 'ctx', self.beside)))]
    ppermute x15, starting transfers between devices: 42.8 us -> 61 us  [step(): lax.ppermute(sent, 'ctx', (TO_INNER if new else []) + (TO_OUTER if old el...]
    ppermute x12, starting transfers between devices: 7.51 us -> 17.9 us  [step(): self.swaps.append((finished, lax.ppermute(finished, 'ctx', self.beside)))]
    ppermute x2, waiting for transfers between devices: 11.3 us -> 1.94 us  [settle(): lax.ppermute(totals[1].astype(BF16), 'ctx', beside).astype(F32)]
    pallas_call x12, Pallas kernels: 48.9 us -> 41 us  [store_pair(): pl.pallas_call(body, cost_estimate=pl.CostEstimate(flops=0, transcendenta...]
    ppermute x15, waiting for transfers between devices: 128 us -> 120 us  [step(): lax.ppermute(sent, 'ctx', (TO_INNER if new else []) + (TO_OUTER if old el...]
    unnamed x251 -> x223, local copies, waits for them, and re-layouts: 29.9 us -> 26.3 us
  transfers between devices with their start and end apart: 108 -> 108, of which waited for: 36 -> 39; matrix products, arithmetic and copies ran while one was open for 7% -> 7% of each run, Pallas kernels for 24% -> 19%
where the time goes in v4:
time: 728 us; the launch traced here: 724 us
  waiting for transfers between devices  339 us (47%)
  Pallas kernels  163 us (22%)
  starting transfers between devices  136 us (19%)
  local copies, waits for them, and re-layouts  41.7 us (6%)
  other arithmetic  27.7 us (4%)
  between operations  15.8 us (2%)
    ppermute x15, waiting for transfers between devices, step(): lax.ppermute(sent, 'ctx', (TO_INNER if new else []) + (TO_OUTER if old el...  120 us
    pallas_call x36, Pallas kernels, call(): pl.pallas_call(body, cost_estimate=cost(flops, arrays, outs), in_specs=[s...  78 us
    ppermute x12, waiting for transfers between devices, step(): self.swaps.append((finished, lax.ppermute(finished, 'ctx', self.beside)))  74.7 us
    ppermute x15, starting transfers between devices, step(): lax.ppermute(sent, 'ctx', (TO_INNER if new else []) + (TO_OUTER if old el...  61 us
    ppermute x10, waiting for transfers between devices, dp_gather(): pieces[step] = lax.ppermute(block, 'dp', xor_pairs(count, step))  53.2 us
    pallas_call x2, Pallas kernels, on_device(): expert_call(held_blocks, rows, local, served, first, number, gate_weight....  44.1 us
    pallas_call x12, Pallas kernels, store_pair(): pl.pallas_call(body, cost_estimate=pl.CostEstimate(flops=0, transcendenta...  41 us
    ppermute x3, waiting for transfers between devices, on_device(): tiny = tiny + lax.ppermute(tiny, 'ctx', xor_pairs(n_ctx, bit))  32.5 us
  transfers between devices with their start and end apart: 108, of which 39 were waited for; matrix products, arithmetic and copies ran while one was open for 7% of the time, Pallas kernels for 19%

profile of v4, /device:TPU:0, one launch (start us, length us, event | category | flops | bytes accessed | tf_op | source)
XLA Modules:
  0.0 723.9 jit_solution(2124716142801334533)
XLA Ops:
  44.7 5.6 collective-permute-done.20
  56.5 8.8 %collective-permute-done.11.refs_10_ = bf16[256,1024]{1,0:T(8,128)(2,1)S(1)} collective-permute-done((bf16[256,1024]{1,0:T(8,128)(2,1)}, bf16[256,1024]{1,0:T(8,128)(2,1)S(1)}, u32[]{:S(2)}, u32[]{:S(2)}) %collective-permute-start.11) | collective-permute-done | bytes 524320 | tf_op jit(solution)/shard_map/ppermute | solution.py:67
  65.3 11.2 %collective-permute-done.17.rest_2_ = bf16[256,1024]{1,0:T(8,128)(2,1)S(1)} collective-permute-done((bf16[256,1024]{1,0:T(8,128)(2,1)S(1)}, bf16[256,1024]{1,0:T(8,128)(2,1)S(1)}, u32[]{:S(2)}, u32[]{:S(2)}) %collective-permute-start.17) | collective-permute-done | bytes 524320 | tf_op jit(solution)/shard_map/ppermute | solution.py:67
  77.1 9.4 %collective-permute-done.14.refs_14_ = bf16[256,1024]{1,0:T(8,128)(2,1)S(1)} collective-permute-done((bf16[256,1024]{1,0:T(8,128)(2,1)}, bf16[256,1024]{1,0:T(8,128)(2,1)S(1)}, u32[]{:S(2)}, u32[]{:S(2)}) %collective-permute-start.14) | collective-permute-done | bytes 524320 | tf_op jit(solution)/shard_map/ppermute | solution.py:67
  99.0 10.8 %shard_map.258 = (bf16[256,1024]{1,0:T(8,128)(2,1)S(1)}, f32[4,4,256,128]{3,2,1,0:T(8,128)S(1)}) custom-call(s32[2]{0:T(128)S(1)} %copy-done.73, s32[2]{0:T(128)S(1)} %get-tuple-element.271.high_ref, s32[16]{0:T(128)S(1)} %select_reduce_fusion.where_ref, bf16[256,1024]{1,0:T(8,128)(2,1)S(1)} %copy-done.60, ...), custom_call_target="tpu_custom_call" | custom-call | flops 2147483648 | bytes 7341056 | tf_op jit(solution)/shard_map/pallas_call | solution.py:49
  118.7 7.9 %collective-permute-done.29.refs_4_ = bf16[256,1024]{1,0:T(8,128)(2,1)S(1)} collective-permute-done((bf16[256,1024]{1,0:T(8,128)(2,1)S(1)}, bf16[256,1024]{1,0:T(8,128)(2,1)S(1)}, u32[]{:S(2)}, u32[]{:S(2)}) %collective-permute-start.29) | collective-permute-done | bytes 524320 | tf_op jit(solution)/shard_map/ppermute | solution.py:749
  132.1 10.5 %collective-permute-done.31.refs_6_ = bf16[256,1024]{1,0:T(8,128)(2,1)S(1)} collective-permute-done((bf16[256,1024]{1,0:T(8,128)(2,1)S(1)}, bf16[256,1024]{1,0:T(8,128)(2,1)S(1)}, u32[]{:S(2)}, u32[]{:S(2)}) %collective-permute-start.31) | collective-permute-done | bytes 524320 | tf_op jit(solution)/shard_map/ppermute | solution.py:67
  146.1 14.3 %shard_map.260 = (bf16[1,1024,512]{2,1,0:T(8,128)(2,1)}, bf16[1,1024,512]{2,1,0:T(8,128)(2,1)}, bf16[1,512,1024]{2,1,0:T(8,128)(2,1)}, f32[32,256]{1,0:T(8,128)}...) custom-call(s32[2]{0:T(128)} %get-tuple-element.309.at_ref, ...), custom_call_target="tpu_custom_call" | custom-call | flops 5368709120 | bytes 14680064 | tf_op jit(solution)/shard_map/pallas_call | solution.py:808
  160.4 10.0 %collective-permute-start.33 = (bf16[1024,512]{1,0:T(8,128)(2,1)}, bf16[1024,512]{1,0:T(8,128)(2,1)S(1)}, u32[]{:S(2)}, u32[]{:S(2)}) collective-permute-start(bf16[1024,512]{1,0:T(8,128)(2,1)} %bitcast.120), channel_id=1, source_target_pairs={{0,2},{1,3},{6,4},{7,5},{8,10},{9,11},{14,12},{15,13},{16,18},{17,... | collective-permute-start | bytes 3145736 | tf_op jit(solution)/shard_map/ppermute | solution.py:580
  170.4 29.8 %shard_map.261 = (bf16[3,1024,512]{2,1,0:T(8,128)(2,1)}, bf16[3,1024,512]{2,1,0:T(8,128)(2,1)}, bf16[3,512,1024]{2,1,0:T(8,128)(2,1)}, f32[32,256]{1,0:T(8,128)}...) custom-call(s32[2]{0:T(128)} %get-tuple-element.310.at_ref, ...), custom_call_target="tpu_custom_call" | custom-call | flops 16106127360 | bytes 27262976 | tf_op jit(solution)/shard_map/pallas_call | solution.py:808
  211.5 9.4 %collective-permute-done.39 = bf16[256,1024]{1,0:T(8,128)(2,1)S(1)} collective-permute-done((bf16[256,1024]{1,0:T(8,128)(2,1)S(1)}, bf16[256,1024]{1,0:T(8,128)(2,1)S(1)}, u32[]{:S(2)}, u32[]{:S(2)}) %collective-permute-start.39) | collective-permute-done | bytes 524320 | tf_op jit(solution)/shard_map/ppermute | solution.py:84
  225.4 9.8 %collective-permute-done.43 = f32[4,4,256]{2,1,0:T(4,128)S(1)} collective-permute-done((f32[4,4,256]{2,1,0:T(4,128)S(1)}, f32[4,4,256]{2,1,0:T(4,128)S(1)}, u32[]{:S(2)}, u32[]{:S(2)}) %collective-permute-start.43) | collective-permute-done | bytes 16416 | tf_op jit(solution)/shard_map/ppermute | solution.py:842
  240.9 6.5 collective-permute-start.54
  257.6 16.9 %shard_map.265 = (bf16[256,1024]{1,0:T(8,128)(2,1)S(1)}, bf16[2048,1024]{1,0:T(8,128)(2,1)}) custom-call(s32[2]{0:T(128)S(1)} %copy-done.74, s32[2]{0:T(128)S(1)} %get-tuple-element.271.high_ref, s32[16]{0:T(128)S(1)} %copy-done.72, bf16[256,1024]{1,0:T(8,128)(2,1)S(1)} %copy-done.61, bf16[2048,1024]{1,0:T(8,128)(2,1)} %all-gather.3.cloned.1.call-done.kv_ref, ...), custom_call_target="tpu_custom_call" | custom-call | flops 5368709120 | bytes 12321792 | tf_op jit(solution)/shard_map/pallas_call | solution.py:49
  283.6 6.9 collective-permute-start.52
  291.2 11.9 %collective-permute-done.52 = bf16[256,1024]{1,0:T(8,128)(2,1)S(1)} collective-permute-done((bf16[256,1024]{1,0:T(8,128)(2,1)S(1)}, bf16[256,1024]{1,0:T(8,128)(2,1)S(1)}, u32[]{:S(2)}, u32[]{:S(2)}) %collective-permute-start.52) | collective-permute-done | bytes 524320 | tf_op jit(solution)/shard_map/ppermute | solution.py:84
  305.1 18.4 %collective-permute-start.70 = (bf16[1024,512]{1,0:T(8,128)(2,1)S(1)}, bf16[1024,512]{1,0:T(8,128)(2,1)S(1)}, u32[]{:S(2)}, u32[]{:S(2)}) collective-permute-start(bf16[1024,512]{1,0:T(8,128)(2,1)S(1)} %shard_map.269.refs_2_), channel_id=1, source_target_pairs={{0,2},{1,3},{6,4},{7,5},{2,0},{3,1},{4,6},{5,7},{8,10},{9,11},{14,... | collective-permute-start | bytes 3145736 | tf_op jit(solution)/shard_map/ppermute | solution.py:580
  330.2 5.4 collective-permute-start.79
  335.6 33.1 %collective-permute-done.70.refs_0_ = bf16[1024,512]{1,0:T(8,128)(2,1)S(1)} collective-permute-done((bf16[1024,512]{1,0:T(8,128)(2,1)S(1)}, bf16[1024,512]{1,0:T(8,128)(2,1)S(1)}, u32[]{:S(2)}, u32[]{:S(2)}) %collective-permute-start.70) | collective-permute-done | bytes 1048608 | tf_op jit(solution)/shard_map/ppermute | solution.py:580
  381.3 6.6 shard_map.268
  400.2 14.6 %collective-permute-done.77.refs_0_ = bf16[512,1024]{1,0:T(8,128)(2,1)S(1)} collective-permute-done((bf16[512,1024]{1,0:T(8,128)(2,1)S(1)}, bf16[512,1024]{1,0:T(8,128)(2,1)S(1)}, u32[]{:S(2)}, u32[]{:S(2)}) %collective-permute-start.77) | collective-permute-done | bytes 1048608 | tf_op jit(solution)/shard_map/ppermute | solution.py:580
  443.6 18.6 %collective-permute-done.82.there_ref = bf16[512,1024]{1,0:T(8,128)(2,1)} collective-permute-done((bf16[512,1024]{1,0:T(8,128)(2,1)}, bf16[512,1024]{1,0:T(8,128)(2,1)}, u32[]{:S(2)}, u32[]{:S(2)}) %collective-permute-start.82) | collective-permute-done | bytes 1048608 | tf_op jit(solution)/shard_map/ppermute | solution.py:599
  473.2 16.0 %collective-permute-done.88.refs_0_ = bf16[1024,512]{1,0:T(8,128)(2,1)} collective-permute-done((bf16[1024,512]{1,0:T(8,128)(2,1)}, bf16[1024,512]{1,0:T(8,128)(2,1)}, u32[]{:S(2)}, u32[]{:S(2)}) %collective-permute-start.88) | collective-permute-done | bytes 1048608 | tf_op jit(solution)/shard_map/ppermute | solution.py:580
  492.7 17.2 %collective-permute-done.86.refs_0_ = bf16[512,1024]{1,0:T(8,128)(2,1)S(1)} collective-permute-done((bf16[512,1024]{1,0:T(8,128)(2,1)S(1)}, bf16[512,1024]{1,0:T(8,128)(2,1)S(1)}, u32[]{:S(2)}, u32[]{:S(2)}) %collective-permute-start.86) | collective-permute-done | bytes 1048608 | tf_op jit(solution)/shard_map/ppermute | solution.py:580
  527.3 15.3 %collective-permute-done.91.there_ref = bf16[512,1024]{1,0:T(8,128)(2,1)S(1)} collective-permute-done((bf16[512,1024]{1,0:T(8,128)(2,1)S(1)}, bf16[512,1024]{1,0:T(8,128)(2,1)S(1)}, u32[]{:S(2)}, u32[]{:S(2)}) %collective-permute-start.91) | collective-permute-done | bytes 1048608 | tf_op jit(solution)/shard_map/ppermute | solution.py:599
  552.4 11.0 %collective-permute-done.96.refs_0_ = bf16[1024,512]{1,0:T(8,128)(2,1)S(1)} collective-permute-done((bf16[1024,512]{1,0:T(8,128)(2,1)S(1)}, bf16[1024,512]{1,0:T(8,128)(2,1)S(1)}, u32[]{:S(2)}, u32[]{:S(2)}) %collective-permute-start.96) | collective-permute-done | bytes 1048608 | tf_op jit(solution)/shard_map/ppermute | solution.py:580
  567.2 22.1 %collective-permute-done.94.refs_0_ = bf16[512,1024]{1,0:T(8,128)(2,1)} collective-permute-done((bf16[512,1024]{1,0:T(8,128)(2,1)}, bf16[512,1024]{1,0:T(8,128)(2,1)}, u32[]{:S(2)}, u32[]{:S(2)}) %collective-permute-start.94) | collective-permute-done | bytes 1048608 | tf_op jit(solution)/shard_map/ppermute | solution.py:580
  602.4 11.7 %collective-permute-done.98.there_ref = bf16[1024,512]{1,0:T(8,128)(2,1)} collective-permute-done((bf16[1024,512]{1,0:T(8,128)(2,1)}, bf16[1024,512]{1,0:T(8,128)(2,1)}, u32[]{:S(2)}, u32[]{:S(2)}) %collective-permute-start.98) | collective-permute-done | bytes 1048608 | tf_op jit(solution)/shard_map/ppermute | solution.py:599
  619.6 14.4 %collective-permute-done.99.there_ref = bf16[512,1024]{1,0:T(8,128)(2,1)S(1)} collective-permute-done((bf16[512,1024]{1,0:T(8,128)(2,1)S(1)}, bf16[512,1024]{1,0:T(8,128)(2,1)S(1)}, u32[]{:S(2)}, u32[]{:S(2)}) %collective-permute-start.99) | collective-permute-done | bytes 1048608 | tf_op jit(solution)/shard_map/ppermute | solution.py:599
  653.1 22.0 %collective-permute-done.66 = f32[34,1024]{1,0:T(8,128)S(1)} collective-permute-done((f32[34,1024]{1,0:T(8,128)S(1)}, f32[34,1024]{1,0:T(8,128)S(1)}, u32[]{:S(2)}, u32[]{:S(2)}) %collective-permute-start.66) | collective-permute-done | bytes 139296 | tf_op jit(solution)/shard_map/ppermute | solution.py:905
  675.2 7.0 collective-permute-done.67
  703.0 9.9 %collective-permute-done.103.there_ref = bf16[512,1024]{1,0:T(8,128)(2,1)S(1)} collective-permute-done((bf16[512,1024]{1,0:T(8,128)(2,1)}, bf16[512,1024]{1,0:T(8,128)(2,1)S(1)}, u32[]{:S(2)}, u32[]{:S(2)}) %collective-permute-start.103) | collective-permute-done | bytes 1048608 | tf_op jit(solution)/shard_map/ppermute | solution.py:599
  (540 shorter events, 285.1 us)
Async XLA Ops:
  7.2 90.1 %all-gather.3.cloned.1.call-start = ((), (), s32[]{:S(2)}) async-start(), calls=%async_computation.2 | async-start | bytes 4718592 | tf_op jit(solution)/shard_map/all_gather | solution.py:109
  35.3 342.8 %reduce-scatter.3.cloned.1.call-start = ((), (), s32[]{:S(2)}) async-start(), calls=%async_computation.3 | async-start | bytes 4718592 | tf_op jit(solution)/shard_map/reduce_scatter | solution.py:113
  56.0 37.6 %collective-permute-start.16 = (bf16[256,1024]{1,0:T(8,128)(2,1)S(1)}, bf16[256,1024]{1,0:T(8,128)(2,1)S(1)}, u32[]{:S(2)}, u32[]{:S(2)}) collective-permute-start(bf16[256,1024]{1,0:T(8,128)(2,1)S(1)} %copy-done.25), channel_id=1, source_target_pairs={{0,8},{8,0},{16,24},{24,16},{1,9},{9,1},{17,25},{25,17},{2,10},{10... | collective-permute-start | bytes 1572872 | tf_op jit(solution)/shard_map/ppermute | solution.py:69
  160.4 39.8 %collective-permute-start.33 = (bf16[1024,512]{1,0:T(8,128)(2,1)}, bf16[1024,512]{1,0:T(8,128)(2,1)S(1)}, u32[]{:S(2)}, u32[]{:S(2)}) collective-permute-start(bf16[1024,512]{1,0:T(8,128)(2,1)} %bitcast.120), channel_id=1, source_target_pairs={{0,2},{1,3},{6,4},{7,5},{8,10},{9,11},{14,12},{15,13},{16,18},{17,... | collective-permute-start | bytes 3145736 | tf_op jit(solution)/shard_map/ppermute | solution.py:580
  237.4 38.0 %collective-permute-start.55 = (bf16[1024,512]{1,0:T(8,128)(2,1)S(1)}, bf16[1024,512]{1,0:T(8,128)(2,1)S(1)}, u32[]{:S(2)}, u32[]{:S(2)}) collective-permute-start(bf16[1024,512]{1,0:T(8,128)(2,1)S(1)} %shard_map.267.refs_1_), channel_id=1, source_target_pairs={{2,4},{3,5},{4,2},{5,3},{10,12},{11,13},{12,10},{13,11},{18,20},{1... | collective-permute-start | bytes 3145736 | tf_op jit(solution)/shard_map/ppermute | solution.py:595
  240.9 35.4 %collective-permute-start.54 = (bf16[512,1024]{1,0:T(8,128)(2,1)S(1)}, bf16[512,1024]{1,0:T(8,128)(2,1)S(1)}, u32[]{:S(2)}, u32[]{:S(2)}) collective-permute-start(bf16[512,1024]{1,0:T(8,128)(2,1)S(1)} %bitcast.116), channel_id=1, source_target_pairs={{0,2},{1,3},{6,4},{7,5},{8,10},{9,11},{14,12},{15,13},{16,18},{17,... | collective-permute-start | bytes 3145736 | tf_op jit(solution)/shard_map/ppermute | solution.py:580
  277.4 289.8 %reduce-scatter.5.cloned.1.call-start = ((), (), s32[]{:S(2)}) async-start(), calls=%async_computation.4 | async-start | bytes 1769472 | tf_op jit(solution)/shard_map/reduce_scatter | solution.py:113
  290.5 36.4 %collective-permute-start.47 = (bf16[256,1024]{1,0:T(8,128)(2,1)S(1)}, bf16[256,1024]{1,0:T(8,128)(2,1)S(1)}, u32[]{:S(2)}, u32[]{:S(2)}) collective-permute-start(bf16[256,1024]{1,0:T(8,128)(2,1)S(1)} %get-tuple-element.185), channel_id=1, source_target_pairs={{0,8},{8,0},{16,24},{24,16},{1,9},{9,1},{17,25},{25,17},{2,10},{10... | collective-permute-start | bytes 1572872 | tf_op jit(solution)/shard_map/ppermute | solution.py:76
  290.7 36.2 %collective-permute-start.49 = (bf16[256,1024]{1,0:T(8,128)(2,1)S(1)}, bf16[256,1024]{1,0:T(8,128)(2,1)S(1)}, u32[]{:S(2)}, u32[]{:S(2)}) collective-permute-start(bf16[256,1024]{1,0:T(8,128)(2,1)S(1)} %add_convert_fusion.12), channel_id=1, source_target_pairs={{0,16},{8,24},{16,0},{24,8},{1,17},{9,25},{17,1},{25,9},{2,18},{10... | collective-permute-start | bytes 1572872 | tf_op jit(solution)/shard_map/ppermute | solution.py:84
  305.1 63.6 %collective-permute-start.70 = (bf16[1024,512]{1,0:T(8,128)(2,1)S(1)}, bf16[1024,512]{1,0:T(8,128)(2,1)S(1)}, u32[]{:S(2)}, u32[]{:S(2)}) collective-permute-start(bf16[1024,512]{1,0:T(8,128)(2,1)S(1)} %shard_map.269.refs_2_), channel_id=1, source_target_pairs={{0,2},{1,3},{6,4},{7,5},{2,0},{3,1},{4,6},{5,7},{8,10},{9,11},{14,... | collective-permute-start | bytes 3145736 | tf_op jit(solution)/shard_map/ppermute | solution.py:580
  323.4 50.8 %collective-permute-start.76 = (bf16[512,1024]{1,0:T(8,128)(2,1)S(1)}, bf16[512,1024]{1,0:T(8,128)(2,1)S(1)}, u32[]{:S(2)}, u32[]{:S(2)}) collective-permute-start(bf16[512,1024]{1,0:T(8,128)(2,1)S(1)} %shard_map.275.refs_1_), channel_id=1, source_target_pairs={{2,4},{3,5},{4,2},{5,3},{10,12},{11,13},{12,10},{13,11},{18,20},{1... | collective-permute-start | bytes 3145736 | tf_op jit(solution)/shard_map/ppermute | solution.py:595
  330.2 63.6 %collective-permute-start.79 = (bf16[1024,512]{1,0:T(8,128)(2,1)}, bf16[1024,512]{1,0:T(8,128)(2,1)}, u32[]{:S(2)}, u32[]{:S(2)}) collective-permute-start(bf16[1024,512]{1,0:T(8,128)(2,1)} %shard_map.279.refs_2_), channel_id=1, source_target_pairs={{0,2},{1,3},{6,4},{7,5},{2,0},{3,1},{4,6},{5,7},{8,10},{9,11},{14,... | collective-permute-start | bytes 3145736 | tf_op jit(solution)/shard_map/ppermute | solution.py:580
  425.0 43.6 %collective-permute-start.73 = (bf16[1024,512]{1,0:T(8,128)(2,1)}, bf16[1024,512]{1,0:T(8,128)(2,1)}, u32[]{:S(2)}, u32[]{:S(2)}) collective-permute-start(bf16[1024,512]{1,0:T(8,128)(2,1)} %shard_map.271.refs_2_), channel_id=1, source_target_pairs={{0,2},{1,3},{6,4},{7,5},{2,0},{3,1},{4,6},{5,7},{8,10},{9,11},{14,... | collective-permute-start | bytes 3145736 | tf_op jit(solution)/shard_map/ppermute | solution.py:580
  428.4 38.0 %collective-permute-start.78 = (bf16[512,1024]{1,0:T(8,128)(2,1)}, bf16[512,1024]{1,0:T(8,128)(2,1)}, u32[]{:S(2)}, u32[]{:S(2)}) collective-permute-start(bf16[512,1024]{1,0:T(8,128)(2,1)} %get-tuple-element.222.refs_1_), channel_id=1, source_target_pairs={{2,4},{3,5},{4,2},{5,3},{10,12},{11,13},{12,10},{13,11},{18,20},{1... | collective-permute-start | bytes 3145736 | tf_op jit(solution)/shard_map/ppermute | solution.py:595
  436.6 52.6 %collective-permute-start.88 = (bf16[1024,512]{1,0:T(8,128)(2,1)}, bf16[1024,512]{1,0:T(8,128)(2,1)}, u32[]{:S(2)}, u32[]{:S(2)}) collective-permute-start(bf16[1024,512]{1,0:T(8,128)(2,1)} %shard_map.281.refs_2_), channel_id=1, source_target_pairs={{0,2},{1,3},{6,4},{7,5},{2,0},{3,1},{4,6},{5,7},{8,10},{9,11},{14,... | collective-permute-start | bytes 3145736 | tf_op jit(solution)/shard_map/ppermute | solution.py:580
  443.5 255.7 %all-gather.5.cloned.1.call-start = ((), (), s32[]{:S(2)}) async-start(), calls=%async_computation.5 | async-start | bytes 1769472 | tf_op jit(solution)/shard_map/all_gather | solution.py:109
  468.5 41.4 %collective-permute-start.86 = (bf16[512,1024]{1,0:T(8,128)(2,1)S(1)}, bf16[512,1024]{1,0:T(8,128)(2,1)S(1)}, u32[]{:S(2)}, u32[]{:S(2)}) collective-permute-start(bf16[512,1024]{1,0:T(8,128)(2,1)S(1)} %shard_map.278.refs_2_), channel_id=1, source_target_pairs={{0,2},{1,3},{6,4},{7,5},{2,0},{3,1},{4,6},{5,7},{8,10},{9,11},{14,... | collective-permute-start | bytes 3145736 | tf_op jit(solution)/shard_map/ppermute | solution.py:580
  470.2 40.4 %collective-permute-start.74 = (bf16[1024,512]{1,0:T(8,128)(2,1)S(1)}, bf16[1024,512]{1,0:T(8,128)(2,1)S(1)}, u32[]{:S(2)}, u32[]{:S(2)}) collective-permute-start(bf16[1024,512]{1,0:T(8,128)(2,1)S(1)} %get-tuple-element.218.refs_1_), channel_id=1, source_target_pairs={{2,4},{3,5},{4,2},{5,3},{10,12},{11,13},{12,10},{13,11},{18,20},{1... | collective-permute-start | bytes 3145736 | tf_op jit(solution)/shard_map/ppermute | solution.py:595
  471.0 40.4 %collective-permute-start.75 = (bf16[1024,512]{1,0:T(8,128)(2,1)S(1)}, bf16[1024,512]{1,0:T(8,128)(2,1)S(1)}, u32[]{:S(2)}, u32[]{:S(2)}) collective-permute-start(bf16[1024,512]{1,0:T(8,128)(2,1)S(1)} %get-tuple-element.219.here_ref), channel_id=1, source_target_pairs={{0,1},{1,0},{2,3},{3,2},{4,5},{5,4},{6,7},{7,6},{8,9},{9,8},{10,11... | collective-permute-start | bytes 3145736 | tf_op jit(solution)/shard_map/ppermute | solution.py:599
  513.8 34.3 %collective-permute-start.83 = (bf16[1024,512]{1,0:T(8,128)(2,1)S(1)}, bf16[1024,512]{1,0:T(8,128)(2,1)S(1)}, u32[]{:S(2)}, u32[]{:S(2)}) collective-permute-start(bf16[1024,512]{1,0:T(8,128)(2,1)S(1)} %shard_map.274.refs_2_), channel_id=1, source_target_pairs={{0,2},{1,3},{6,4},{7,5},{2,0},{3,1},{4,6},{5,7},{8,10},{9,11},{14,... | collective-permute-start | bytes 3145736 | tf_op jit(solution)/shard_map/ppermute | solution.py:580
  524.0 39.4 %collective-permute-start.96 = (bf16[1024,512]{1,0:T(8,128)(2,1)S(1)}, bf16[1024,512]{1,0:T(8,128)(2,1)S(1)}, u32[]{:S(2)}, u32[]{:S(2)}) collective-permute-start(bf16[1024,512]{1,0:T(8,128)(2,1)S(1)} %shard_map.290.refs_2_), channel_id=1, source_target_pairs={{0,2},{1,3},{6,4},{7,5},{2,0},{3,1},{4,6},{5,7},{8,10},{9,11},{14,... | collective-permute-start | bytes 3145736 | tf_op jit(solution)/shard_map/ppermute | solution.py:580
  545.1 44.2 %collective-permute-start.94 = (bf16[512,1024]{1,0:T(8,128)(2,1)}, bf16[512,1024]{1,0:T(8,128)(2,1)}, u32[]{:S(2)}, u32[]{:S(2)}) collective-permute-start(bf16[512,1024]{1,0:T(8,128)(2,1)} %shard_map.288.refs_2_), channel_id=1, source_target_pairs={{0,2},{1,3},{6,4},{7,5},{2,0},{3,1},{4,6},{5,7},{8,10},{9,11},{14,... | collective-permute-start | bytes 3145736 | tf_op jit(solution)/shard_map/ppermute | solution.py:580
  549.6 42.0 %collective-permute-start.84 = (bf16[1024,512]{1,0:T(8,128)(2,1)}, bf16[1024,512]{1,0:T(8,128)(2,1)S(1)}, u32[]{:S(2)}, u32[]{:S(2)}) collective-permute-start(bf16[1024,512]{1,0:T(8,128)(2,1)} %get-tuple-element.235.refs_1_), channel_id=1, source_target_pairs={{2,4},{3,5},{4,2},{5,3},{10,12},{11,13},{12,10},{13,11},{18,20},{1... | collective-permute-start | bytes 3145736 | tf_op jit(solution)/shard_map/ppermute | solution.py:595
  550.4 45.3 %collective-permute-start.85 = (bf16[1024,512]{1,0:T(8,128)(2,1)}, bf16[1024,512]{1,0:T(8,128)(2,1)}, u32[]{:S(2)}, u32[]{:S(2)}) collective-permute-start(bf16[1024,512]{1,0:T(8,128)(2,1)} %get-tuple-element.236.here_ref), channel_id=1, source_target_pairs={{0,1},{1,0},{2,3},{3,2},{4,5},{5,4},{6,7},{7,6},{8,9},{9,8},{10,11... | collective-permute-start | bytes 3145736 | tf_op jit(solution)/shard_map/ppermute | solution.py:599
  564.8 36.3 %collective-permute-start.97 = (bf16[1024,512]{1,0:T(8,128)(2,1)}, bf16[1024,512]{1,0:T(8,128)(2,1)S(1)}, u32[]{:S(2)}, u32[]{:S(2)}) collective-permute-start(bf16[1024,512]{1,0:T(8,128)(2,1)} %get-tuple-element.256.refs_1_), channel_id=1, source_target_pairs={{2,4},{3,5},{4,2},{5,3},{10,12},{11,13},{12,10},{13,11},{18,20},{1... | collective-permute-start | bytes 3145736 | tf_op jit(solution)/shard_map/ppermute | solution.py:595
  565.5 48.5 %collective-permute-start.98 = (bf16[1024,512]{1,0:T(8,128)(2,1)}, bf16[1024,512]{1,0:T(8,128)(2,1)}, u32[]{:S(2)}, u32[]{:S(2)}) collective-permute-start(bf16[1024,512]{1,0:T(8,128)(2,1)} %get-tuple-element.258.here_ref), channel_id=1, source_target_pairs={{0,1},{1,0},{2,3},{3,2},{4,5},{5,4},{6,7},{7,6},{8,9},{9,8},{10,11... | collective-permute-start | bytes 3145736 | tf_op jit(solution)/shard_map/ppermute | solution.py:599
  591.6 42.3 %collective-permute-start.99 = (bf16[512,1024]{1,0:T(8,128)(2,1)S(1)}, bf16[512,1024]{1,0:T(8,128)(2,1)S(1)}, u32[]{:S(2)}, u32[]{:S(2)}) collective-permute-start(bf16[512,1024]{1,0:T(8,128)(2,1)S(1)} %get-tuple-element.263.here_ref), channel_id=1, source_target_pairs={{0,1},{1,0},{2,3},{3,2},{4,5},{5,4},{6,7},{7,6},{8,9},{9,8},{10,11... | collective-permute-start | bytes 3145736 | tf_op jit(solution)/shard_map/ppermute | solution.py:599
  599.8 48.0 %collective-permute-start.92 = (bf16[1024,512]{1,0:T(8,128)(2,1)S(1)}, bf16[1024,512]{1,0:T(8,128)(2,1)S(1)}, u32[]{:S(2)}, u32[]{:S(2)}) collective-permute-start(bf16[1024,512]{1,0:T(8,128)(2,1)S(1)} %shard_map.286.refs_1_), channel_id=1, source_target_pairs={{2,0},{3,1},{4,6},{5,7},{10,8},{11,9},{12,14},{13,15},{18,16},{19,... | collective-permute-start | bytes 3145736 | tf_op jit(solution)/shard_map/ppermute | solution.py:580
  618.2 34.7 %collective-permute-start.100 = (bf16[1024,512]{1,0:T(8,128)(2,1)S(1)}, bf16[1024,512]{1,0:T(8,128)(2,1)S(1)}, u32[]{:S(2)}, u32[]{:S(2)}) collective-permute-start(bf16[1024,512]{1,0:T(8,128)(2,1)S(1)} %shard_map.298.refs_1_), channel_id=1, source_target_pairs={{2,0},{3,1},{4,6},{5,7},{10,8},{11,9},{12,14},{13,15},{18,16},{19,... | collective-permute-start | bytes 3145736 | tf_op jit(solution)/shard_map/ppermute | solution.py:580
  636.4 47.4 %collective-permute-start.102 = (bf16[512,1024]{1,0:T(8,128)(2,1)S(1)}, bf16[512,1024]{1,0:T(8,128)(2,1)}, u32[]{:S(2)}, u32[]{:S(2)}) collective-permute-start(bf16[512,1024]{1,0:T(8,128)(2,1)S(1)} %shard_map.296.refs_1_), channel_id=1, source_target_pairs={{2,0},{3,1},{4,6},{5,7},{10,8},{11,9},{12,14},{13,15},{18,16},{19,... | collective-permute-start | bytes 3145736 | tf_op jit(solution)/shard_map/ppermute | solution.py:580
  647.9 43.3 %collective-permute-start.93 = (bf16[1024,512]{1,0:T(8,128)(2,1)S(1)}, bf16[1024,512]{1,0:T(8,128)(2,1)}, u32[]{:S(2)}, u32[]{:S(2)}) collective-permute-start(bf16[1024,512]{1,0:T(8,128)(2,1)S(1)} %shard_map.294.here_ref), channel_id=1, source_target_pairs={{0,1},{1,0},{2,3},{3,2},{4,5},{5,4},{6,7},{7,6},{8,9},{9,8},{10,11... | collective-permute-start | bytes 3145736 | tf_op jit(solution)/shard_map/ppermute | solution.py:599
  653.0 42.2 %collective-permute-start.101 = (bf16[1024,512]{1,0:T(8,128)(2,1)S(1)}, bf16[1024,512]{1,0:T(8,128)(2,1)}, u32[]{:S(2)}, u32[]{:S(2)}) collective-permute-start(bf16[1024,512]{1,0:T(8,128)(2,1)S(1)} %shard_map.302.here_ref), channel_id=1, source_target_pairs={{0,1},{1,0},{2,3},{3,2},{4,5},{5,4},{6,7},{7,6},{8,9},{9,8},{10,11... | collective-permute-start | bytes 3145736 | tf_op jit(solution)/shard_map/ppermute | solution.py:599
  (182 other events, 2609.6 us)
Sparse Core Ops, SparseCore 0:
  35.5 49.0 all-gather.2
  277.5 98.1 reduce-scatter.2
  443.7 36.3 reduce-scatter.4
  567.3 39.8 all-gather.4

commit v5 on v4

--- a/solution.py
+++ b/solution.py
@@ -42,7 +42,7 @@
 def cost(flops, arrays, outs):
     moved = sum(a.size * a.dtype.itemsize for a in arrays)
     moved += sum(math.prod(s) * jnp.dtype(d).itemsize for s, d in outs)
-    return pl.CostEstimate(flops=flops, transcendentals=0, bytes_accessed=moved)
+    return pl.CostEstimate(flops=0, transcendentals=0, bytes_accessed=0)
 
 
 def call(body, scalars, arrays, outs, scratch=(), mib=48, flops=0):
@@ -880,8 +880,8 @@
         kv_grad = ring_scatter(hold(kv_grads, 2), n_ctx)
         y_parts = combine(5, [grad_query])
         y_total = settle(y_parts, lambda values: None)
+        dense_out = dp_reduce(out_parts, n_dp).astype(BF16)
         layer_output = mixed + y_total
-        dense_out = dp_reduce(out_parts, n_dp).astype(BF16)
         step(layer_output)
         res = call(
             first_body(n_dp),
@@ -901,11 +901,11 @@
         dense = jnp.concatenate([dense_out, dense_q, dense_kv], axis=0)
         dense = ring_gather(ring_scatter(dense, n_ctx), n_ctx).astype(F32)
         tiny = jnp.concatenate([router_part, gain_one_part, gain_two_part], axis=0)
-        for bit in [1 << b for b in range(n_ctx.bit_length() - 1)]:
-            tiny = tiny + lax.ppermute(tiny, "ctx", xor_pairs(n_ctx, bit))
         for bit in [1 << b for b in range(n_dp.bit_length() - 1)]:
             tiny = tiny + lax.ppermute(tiny, "dp", xor_pairs(n_dp, bit))
         tiny = lax.dynamic_slice_in_dim(tiny, me_dp * width, width, axis=1)
+        for bit in [1 << b for b in range(n_ctx.bit_length() - 1)]:
+            tiny = tiny + lax.ppermute(tiny, "ctx", xor_pairs(n_ctx, bit))
         if pairs:
             while len(line.marks) < len(line.blocks) + line.LAG:
                 line.step()

time: 728 us -> 733 us (level)
  starting transfers between devices: 136 us -> 119 us
  local copies, waits for them, and re-layouts: 41.7 us -> 50 us
    ppermute x15, starting transfers between devices: 61 us -> 39.4 us  [step(): lax.ppermute(sent, 'ctx', (TO_INNER if new else []) + (TO_OUTER if old el...]
    ppermute x2, waiting for transfers between devices: 1.94 us -> 13.9 us  [settle(): lax.ppermute(totals[1].astype(BF16), 'ctx', beside).astype(F32)]
    ppermute x12, starting transfers between devices: 17.9 us -> 9.24 us  [step(): self.swaps.append((finished, lax.ppermute(finished, 'ctx', self.beside)))]
    unnamed x223 -> x199, local copies, waits for them, and re-layouts: 26.3 us -> 34.1 us
  transfers between devices with their start and end apart: 108 -> 108, of which waited for: 39 -> 40; matrix products, arithmetic and copies ran while one was open for 7% -> 7% of each run, Pallas kernels for 19% -> 20%
where the time goes in v5:
time: 733 us; the launch traced here: 724 us
  waiting for transfers between devices  344 us (47%)
  Pallas kernels  165 us (23%)
  starting transfers between devices  119 us (16%)
  local copies, waits for them, and re-layouts  50 us (7%)
  other arithmetic  29 us (4%)
  between operations  15.5 us (2%)
    ppermute x15, waiting for transfers between devices, step(): lax.ppermute(sent, 'ctx', (TO_INNER if new else []) + (TO_OUTER if old el...  127 us
    pallas_call x36, Pallas kernels, call(): pl.pallas_call(body, cost_estimate=cost(flops, arrays, outs), in_specs=[s...  80.3 us
    ppermute x12, waiting for transfers between devices, step(): self.swaps.append((finished, lax.ppermute(finished, 'ctx', self.beside)))  69 us
    ppermute x10, waiting for transfers between devices, dp_gather(): pieces[step] = lax.ppermute(block, 'dp', xor_pairs(count, step))  54.6 us
    pallas_call x2, Pallas kernels, on_device(): expert_call(held_blocks, rows, local, served, first, number, gate_weight....  44.2 us
    pallas_call x12, Pallas kernels, store_pair(): pl.pallas_call(body, cost_estimate=pl.CostEstimate(flops=0, transcendenta...  41 us
    ppermute x15, starting transfers between devices, step(): lax.ppermute(sent, 'ctx', (TO_INNER if new else []) + (TO_OUTER if old el...  39.4 us
    unnamed x199, local copies, waits for them, and re-layouts  34.1 us
  transfers between devices with their start and end apart: 108, of which 40 were waited for; matrix products, arithmetic and copies ran while one was open for 7% of the time, Pallas kernels for 20%

profile of v5, /device:TPU:0, one launch (start us, length us, event | category | flops | bytes accessed | tf_op | source)
XLA Modules:
  0.0 724.1 jit_solution(16521089979052798928)
XLA Ops:
  56.1 9.2 %collective-permute-done.11.refs_10_ = bf16[256,1024]{1,0:T(8,128)(2,1)S(1)} collective-permute-done((bf16[256,1024]{1,0:T(8,128)(2,1)}, bf16[256,1024]{1,0:T(8,128)(2,1)S(1)}, u32[]{:S(2)}, u32[]{:S(2)}) %collective-permute-start.11) | collective-permute-done | bytes 524320 | tf_op jit(solution)/shard_map/ppermute | solution.py:67
  66.7 9.9 %collective-permute-done.17.rest_2_ = bf16[256,1024]{1,0:T(8,128)(2,1)S(1)} collective-permute-done((bf16[256,1024]{1,0:T(8,128)(2,1)S(1)}, bf16[256,1024]{1,0:T(8,128)(2,1)S(1)}, u32[]{:S(2)}, u32[]{:S(2)}) %collective-permute-start.17) | collective-permute-done | bytes 524320 | tf_op jit(solution)/shard_map/ppermute | solution.py:67
  76.6 9.9 %collective-permute-done.14.refs_14_ = bf16[256,1024]{1,0:T(8,128)(2,1)S(1)} collective-permute-done((bf16[256,1024]{1,0:T(8,128)(2,1)}, bf16[256,1024]{1,0:T(8,128)(2,1)S(1)}, u32[]{:S(2)}, u32[]{:S(2)}) %collective-permute-start.14) | collective-permute-done | bytes 524320 | tf_op jit(solution)/shard_map/ppermute | solution.py:67
  96.5 9.8 %shard_map.258 = (bf16[256,1024]{1,0:T(8,128)(2,1)S(1)}, f32[4,4,256,128]{3,2,1,0:T(8,128)S(1)}) custom-call(s32[2]{0:T(128)S(1)} %copy-done.65, s32[2]{0:T(128)S(1)} %get-tuple-element.271.high_ref, s32[16]{0:T(128)S(1)} %select_reduce_fusion.where_ref, bf16[256,1024]{1,0:T(8,128)(2,1)S(1)} %shard_map.257.q_ref, ...), custom_call_target="tpu_custom_call" | custom-call | tf_op jit(solution)/shard_map/pallas_call | solution.py:49
  109.5 8.4 %collective-permute-start.29 = (bf16[256,1024]{1,0:T(8,128)(2,1)S(1)}, bf16[256,1024]{1,0:T(8,128)(2,1)S(1)}, u32[]{:S(2)}, u32[]{:S(2)}) collective-permute-start(bf16[256,1024]{1,0:T(8,128)(2,1)S(1)} %get-tuple-element.151.refs_0_.act_ref), channel_id=1, source_target_pairs={{0,1},{1,0},{2,3},{3,2},{4,5},{5,4},{6,7},{7,6},{8,9},{9,8},{10,11... | collective-permute-start | bytes 1572872 | tf_op jit(solution)/shard_map/ppermute | solution.py:749
  120.2 7.3 %collective-permute-done.29.refs_4_ = bf16[256,1024]{1,0:T(8,128)(2,1)S(1)} collective-permute-done((bf16[256,1024]{1,0:T(8,128)(2,1)S(1)}, bf16[256,1024]{1,0:T(8,128)(2,1)S(1)}, u32[]{:S(2)}, u32[]{:S(2)}) %collective-permute-start.29) | collective-permute-done | bytes 524320 | tf_op jit(solution)/shard_map/ppermute | solution.py:749
  129.1 5.8 collective-permute-done.27.refs_2_
  134.9 10.8 %collective-permute-done.31.refs_6_ = bf16[256,1024]{1,0:T(8,128)(2,1)S(1)} collective-permute-done((bf16[256,1024]{1,0:T(8,128)(2,1)S(1)}, bf16[256,1024]{1,0:T(8,128)(2,1)S(1)}, u32[]{:S(2)}, u32[]{:S(2)}) %collective-permute-start.31) | collective-permute-done | bytes 524320 | tf_op jit(solution)/shard_map/ppermute | solution.py:67
  149.4 14.5 %shard_map.260 = (bf16[1,1024,512]{2,1,0:T(8,128)(2,1)}, bf16[1,1024,512]{2,1,0:T(8,128)(2,1)}, bf16[1,512,1024]{2,1,0:T(8,128)(2,1)}, f32[32,256]{1,0:T(8,128)}...) custom-call(s32[2]{0:T(128)} %get-tuple-element.309.at_ref, ...), custom_call_target="tpu_custom_call" | custom-call | flops 5368709120 | bytes 14680064 | tf_op jit(solution)/shard_map/pallas_call | solution.py:808
  168.0 29.8 %shard_map.261 = (bf16[3,1024,512]{2,1,0:T(8,128)(2,1)}, bf16[3,1024,512]{2,1,0:T(8,128)(2,1)}, bf16[3,512,1024]{2,1,0:T(8,128)(2,1)}, f32[32,256]{1,0:T(8,128)}...) custom-call(s32[2]{0:T(128)} %get-tuple-element.310.at_ref, ...), custom_call_target="tpu_custom_call" | custom-call | flops 16106127360 | bytes 27262976 | tf_op jit(solution)/shard_map/pallas_call | solution.py:808
  209.1 9.3 %collective-permute-done.39 = bf16[256,1024]{1,0:T(8,128)(2,1)S(1)} collective-permute-done((bf16[256,1024]{1,0:T(8,128)(2,1)S(1)}, bf16[256,1024]{1,0:T(8,128)(2,1)S(1)}, u32[]{:S(2)}, u32[]{:S(2)}) %collective-permute-start.39) | collective-permute-done | bytes 524320 | tf_op jit(solution)/shard_map/ppermute | solution.py:84
  235.0 11.0 %collective-permute-start.54 = (bf16[512,1024]{1,0:T(8,128)(2,1)}, bf16[512,1024]{1,0:T(8,128)(2,1)}, u32[]{:S(2)}, u32[]{:S(2)}) collective-permute-start(bf16[512,1024]{1,0:T(8,128)(2,1)} %bitcast.50.refs_1_), channel_id=1, source_target_pairs={{0,2},{1,3},{6,4},{7,5},{8,10},{9,11},{14,12},{15,13},{16,18},{17,... | collective-permute-start | bytes 3145736 | tf_op jit(solution)/shard_map/ppermute | solution.py:580
  269.5 15.4 %shard_map.265 = (bf16[256,1024]{1,0:T(8,128)(2,1)S(1)}, bf16[2048,1024]{1,0:T(8,128)(2,1)}) custom-call(s32[2]{0:T(128)S(1)} %copy-done.66, s32[2]{0:T(128)S(1)} %get-tuple-element.271.high_ref, s32[16]{0:T(128)S(1)} %copy-done.64, bf16[256,1024]{1,0:T(8,128)(2,1)S(1)} %shard_map.257.q_ref, bf16[2048,1024]{1,0:T(8,128)(2,1)} %all-gather.3.cloned.1.call-done.kv_ref, ...), custom_call_target="tpu_custom_call" | custom-call | tf_op jit(solution)/shard_map/pallas_call | solution.py:49
  290.2 5.7 collective-permute-start.51
  300.1 12.4 %collective-permute-done.52 = bf16[256,1024]{1,0:T(8,128)(2,1)S(1)} collective-permute-done((bf16[256,1024]{1,0:T(8,128)(2,1)S(1)}, bf16[256,1024]{1,0:T(8,128)(2,1)S(1)}, u32[]{:S(2)}, u32[]{:S(2)}) %collective-permute-start.52) | collective-permute-done | bytes 524320 | tf_op jit(solution)/shard_map/ppermute | solution.py:84
  312.7 6.0 collective-permute-start.53
  328.5 13.7 %collective-permute-done.53 = bf16[256,1024]{1,0:T(8,128)(2,1)S(1)} collective-permute-done((bf16[256,1024]{1,0:T(8,128)(2,1)S(1)}, bf16[256,1024]{1,0:T(8,128)(2,1)S(1)}, u32[]{:S(2)}, u32[]{:S(2)}) %collective-permute-start.53) | collective-permute-done | bytes 524320 | tf_op jit(solution)/shard_map/ppermute | solution.py:834
  343.6 22.7 %collective-permute-done.70.refs_0_ = bf16[1024,512]{1,0:T(8,128)(2,1)S(1)} collective-permute-done((bf16[1024,512]{1,0:T(8,128)(2,1)S(1)}, bf16[1024,512]{1,0:T(8,128)(2,1)S(1)}, u32[]{:S(2)}, u32[]{:S(2)}) %collective-permute-start.70) | collective-permute-done | bytes 1048608 | tf_op jit(solution)/shard_map/ppermute | solution.py:580
  377.8 6.6 shard_map.268
  397.8 13.2 %collective-permute-done.77.refs_0_ = bf16[512,1024]{1,0:T(8,128)(2,1)S(1)} collective-permute-done((bf16[512,1024]{1,0:T(8,128)(2,1)S(1)}, bf16[512,1024]{1,0:T(8,128)(2,1)S(1)}, u32[]{:S(2)}, u32[]{:S(2)}) %collective-permute-start.77) | collective-permute-done | bytes 1048608 | tf_op jit(solution)/shard_map/ppermute | solution.py:580
  439.7 17.3 %collective-permute-done.82.there_ref = bf16[512,1024]{1,0:T(8,128)(2,1)} collective-permute-done((bf16[512,1024]{1,0:T(8,128)(2,1)}, bf16[512,1024]{1,0:T(8,128)(2,1)}, u32[]{:S(2)}, u32[]{:S(2)}) %collective-permute-start.82) | collective-permute-done | bytes 1048608 | tf_op jit(solution)/shard_map/ppermute | solution.py:599
  466.1 19.3 %collective-permute-done.88.refs_0_ = bf16[1024,512]{1,0:T(8,128)(2,1)} collective-permute-done((bf16[1024,512]{1,0:T(8,128)(2,1)}, bf16[1024,512]{1,0:T(8,128)(2,1)}, u32[]{:S(2)}, u32[]{:S(2)}) %collective-permute-start.88) | collective-permute-done | bytes 1048608 | tf_op jit(solution)/shard_map/ppermute | solution.py:580
  488.3 17.6 %collective-permute-done.86.refs_0_ = bf16[512,1024]{1,0:T(8,128)(2,1)S(1)} collective-permute-done((bf16[512,1024]{1,0:T(8,128)(2,1)S(1)}, bf16[512,1024]{1,0:T(8,128)(2,1)S(1)}, u32[]{:S(2)}, u32[]{:S(2)}) %collective-permute-start.86) | collective-permute-done | bytes 1048608 | tf_op jit(solution)/shard_map/ppermute | solution.py:580
  523.1 14.9 %collective-permute-done.91.there_ref = bf16[512,1024]{1,0:T(8,128)(2,1)S(1)} collective-permute-done((bf16[512,1024]{1,0:T(8,128)(2,1)S(1)}, bf16[512,1024]{1,0:T(8,128)(2,1)S(1)}, u32[]{:S(2)}, u32[]{:S(2)}) %collective-permute-start.91) | collective-permute-done | bytes 1048608 | tf_op jit(solution)/shard_map/ppermute | solution.py:599
  547.0 13.6 %collective-permute-done.96.refs_0_ = bf16[1024,512]{1,0:T(8,128)(2,1)S(1)} collective-permute-done((bf16[1024,512]{1,0:T(8,128)(2,1)S(1)}, bf16[1024,512]{1,0:T(8,128)(2,1)S(1)}, u32[]{:S(2)}, u32[]{:S(2)}) %collective-permute-start.96) | collective-permute-done | bytes 1048608 | tf_op jit(solution)/shard_map/ppermute | solution.py:580
  563.5 23.3 %collective-permute-done.94.refs_0_ = bf16[512,1024]{1,0:T(8,128)(2,1)} collective-permute-done((bf16[512,1024]{1,0:T(8,128)(2,1)}, bf16[512,1024]{1,0:T(8,128)(2,1)}, u32[]{:S(2)}, u32[]{:S(2)}) %collective-permute-start.94) | collective-permute-done | bytes 1048608 | tf_op jit(solution)/shard_map/ppermute | solution.py:580
  598.0 11.9 %collective-permute-done.98.there_ref = bf16[1024,512]{1,0:T(8,128)(2,1)} collective-permute-done((bf16[1024,512]{1,0:T(8,128)(2,1)}, bf16[1024,512]{1,0:T(8,128)(2,1)}, u32[]{:S(2)}, u32[]{:S(2)}) %collective-permute-start.98) | collective-permute-done | bytes 1048608 | tf_op jit(solution)/shard_map/ppermute | solution.py:599
  615.4 14.1 %collective-permute-done.99.there_ref = bf16[512,1024]{1,0:T(8,128)(2,1)S(1)} collective-permute-done((bf16[512,1024]{1,0:T(8,128)(2,1)S(1)}, bf16[512,1024]{1,0:T(8,128)(2,1)S(1)}, u32[]{:S(2)}, u32[]{:S(2)}) %collective-permute-start.99) | collective-permute-done | bytes 1048608 | tf_op jit(solution)/shard_map/ppermute | solution.py:599
  634.3 13.8 %collective-permute-done.100.refs_0_ = bf16[1024,512]{1,0:T(8,128)(2,1)S(1)} collective-permute-done((bf16[1024,512]{1,0:T(8,128)(2,1)S(1)}, bf16[1024,512]{1,0:T(8,128)(2,1)S(1)}, u32[]{:S(2)}, u32[]{:S(2)}) %collective-permute-start.100) | collective-permute-done | bytes 1048608 | tf_op jit(solution)/shard_map/ppermute | solution.py:580
  655.7 26.7 %collective-permute-done.67 = f32[34,256]{1,0:T(8,128)S(1)} collective-permute-done((f32[34,256]{1,0:T(8,128)S(1)}, f32[34,256]{1,0:T(8,128)S(1)}, u32[]{:S(2)}, u32[]{:S(2)}) %collective-permute-start.67) | collective-permute-done | bytes 34848 | tf_op jit(solution)/shard_map/ppermute | solution.py:908
  689.5 5.0 collective-permute-done.69
  707.5 5.6 collective-permute-done.103.there_ref
  (516 shorter events, 294.0 us)
Async XLA Ops:
  7.2 88.6 %all-gather.3.cloned.1.call-start = ((), (), s32[]{:S(2)}) async-start(), calls=%async_computation.2 | async-start | bytes 4718592 | tf_op jit(solution)/shard_map/all_gather | solution.py:109
  35.4 339.3 %reduce-scatter.3.cloned.1.call-start = ((), (), s32[]{:S(2)}) async-start(), calls=%async_computation.3 | async-start | bytes 4718592 | tf_op jit(solution)/shard_map/reduce_scatter | solution.py:113
  52.4 34.1 %collective-permute-start.14 = (bf16[256,1024]{1,0:T(8,128)(2,1)}, bf16[256,1024]{1,0:T(8,128)(2,1)S(1)}, u32[]{:S(2)}, u32[]{:S(2)}) collective-permute-start(bf16[256,1024]{1,0:T(8,128)(2,1)} %collective-permute-done.refs_12_), channel_id=1, source_target_pairs={{0,16},{8,24},{16,0},{24,8},{1,17},{9,25},{17,1},{25,9},{2,18},{10... | collective-permute-start | bytes 1572872 | tf_op jit(solution)/shard_map/ppermute | solution.py:67
  163.9 33.9 %collective-permute-start.33 = (bf16[1024,512]{1,0:T(8,128)(2,1)}, bf16[1024,512]{1,0:T(8,128)(2,1)S(1)}, u32[]{:S(2)}, u32[]{:S(2)}) collective-permute-start(bf16[1024,512]{1,0:T(8,128)(2,1)} %bitcast.118), channel_id=1, source_target_pairs={{0,2},{1,3},{6,4},{7,5},{8,10},{9,11},{14,12},{15,13},{16,18},{17,... | collective-permute-start | bytes 3145736 | tf_op jit(solution)/shard_map/ppermute | solution.py:580
  223.6 33.5 %collective-permute-start.42 = (bf16[1024,512]{1,0:T(8,128)(2,1)S(1)}, bf16[1024,512]{1,0:T(8,128)(2,1)}, u32[]{:S(2)}, u32[]{:S(2)}) collective-permute-start(bf16[1024,512]{1,0:T(8,128)(2,1)S(1)} %shard_map.263.refs_1_), channel_id=1, source_target_pairs={{2,4},{3,5},{4,2},{5,3},{10,12},{11,13},{12,10},{13,11},{18,20},{1... | collective-permute-start | bytes 3145736 | tf_op jit(solution)/shard_map/ppermute | solution.py:595
  230.5 55.3 %collective-permute-start.55 = (bf16[1024,512]{1,0:T(8,128)(2,1)S(1)}, bf16[1024,512]{1,0:T(8,128)(2,1)}, u32[]{:S(2)}, u32[]{:S(2)}) collective-permute-start(bf16[1024,512]{1,0:T(8,128)(2,1)S(1)} %shard_map.267.refs_1_), channel_id=1, source_target_pairs={{2,4},{3,5},{4,2},{5,3},{10,12},{11,13},{12,10},{13,11},{18,20},{1... | collective-permute-start | bytes 3145736 | tf_op jit(solution)/shard_map/ppermute | solution.py:595
  235.0 50.8 %collective-permute-start.54 = (bf16[512,1024]{1,0:T(8,128)(2,1)}, bf16[512,1024]{1,0:T(8,128)(2,1)}, u32[]{:S(2)}, u32[]{:S(2)}) collective-permute-start(bf16[512,1024]{1,0:T(8,128)(2,1)} %bitcast.50.refs_1_), channel_id=1, source_target_pairs={{0,2},{1,3},{6,4},{7,5},{8,10},{9,11},{14,12},{15,13},{16,18},{17,... | collective-permute-start | bytes 3145736 | tf_op jit(solution)/shard_map/ppermute | solution.py:580
  285.8 277.7 %reduce-scatter.5.cloned.1.call-start = ((), (), s32[]{:S(2)}) async-start(), calls=%async_computation.4 | async-start | bytes 1769472 | tf_op jit(solution)/shard_map/reduce_scatter | solution.py:113
  321.7 44.6 %collective-permute-start.70 = (bf16[1024,512]{1,0:T(8,128)(2,1)S(1)}, bf16[1024,512]{1,0:T(8,128)(2,1)S(1)}, u32[]{:S(2)}, u32[]{:S(2)}) collective-permute-start(bf16[1024,512]{1,0:T(8,128)(2,1)S(1)} %shard_map.269.refs_2_), channel_id=1, source_target_pairs={{0,2},{1,3},{6,4},{7,5},{2,0},{3,1},{4,6},{5,7},{8,10},{9,11},{14,... | collective-permute-start | bytes 3145736 | tf_op jit(solution)/shard_map/ppermute | solution.py:580
  323.3 47.4 %collective-permute-start.76 = (bf16[512,1024]{1,0:T(8,128)(2,1)S(1)}, bf16[512,1024]{1,0:T(8,128)(2,1)S(1)}, u32[]{:S(2)}, u32[]{:S(2)}) collective-permute-start(bf16[512,1024]{1,0:T(8,128)(2,1)S(1)} %shard_map.275.refs_1_), channel_id=1, source_target_pairs={{2,4},{3,5},{4,2},{5,3},{10,12},{11,13},{12,10},{13,11},{18,20},{1... | collective-permute-start | bytes 3145736 | tf_op jit(solution)/shard_map/ppermute | solution.py:595
  343.6 44.4 %collective-permute-start.79 = (bf16[1024,512]{1,0:T(8,128)(2,1)}, bf16[1024,512]{1,0:T(8,128)(2,1)}, u32[]{:S(2)}, u32[]{:S(2)}) collective-permute-start(bf16[1024,512]{1,0:T(8,128)(2,1)} %shard_map.279.refs_2_), channel_id=1, source_target_pairs={{0,2},{1,3},{6,4},{7,5},{2,0},{3,1},{4,6},{5,7},{8,10},{9,11},{14,... | collective-permute-start | bytes 3145736 | tf_op jit(solution)/shard_map/ppermute | solution.py:580
  390.0 33.7 %collective-permute-start.80 = (bf16[1024,512]{1,0:T(8,128)(2,1)S(1)}, bf16[1024,512]{1,0:T(8,128)(2,1)S(1)}, u32[]{:S(2)}, u32[]{:S(2)}) collective-permute-start(bf16[1024,512]{1,0:T(8,128)(2,1)S(1)} %get-tuple-element.225.refs_1_), channel_id=1, source_target_pairs={{2,4},{3,5},{4,2},{5,3},{10,12},{11,13},{12,10},{13,11},{18,20},{1... | collective-permute-start | bytes 3145736 | tf_op jit(solution)/shard_map/ppermute | solution.py:595
  421.8 41.6 %collective-permute-start.73 = (bf16[1024,512]{1,0:T(8,128)(2,1)}, bf16[1024,512]{1,0:T(8,128)(2,1)}, u32[]{:S(2)}, u32[]{:S(2)}) collective-permute-start(bf16[1024,512]{1,0:T(8,128)(2,1)} %shard_map.271.refs_2_), channel_id=1, source_target_pairs={{0,2},{1,3},{6,4},{7,5},{2,0},{3,1},{4,6},{5,7},{8,10},{9,11},{14,... | collective-permute-start | bytes 3145736 | tf_op jit(solution)/shard_map/ppermute | solution.py:580
  424.0 37.2 %collective-permute-start.78 = (bf16[512,1024]{1,0:T(8,128)(2,1)}, bf16[512,1024]{1,0:T(8,128)(2,1)}, u32[]{:S(2)}, u32[]{:S(2)}) collective-permute-start(bf16[512,1024]{1,0:T(8,128)(2,1)} %get-tuple-element.222.refs_1_), channel_id=1, source_target_pairs={{2,4},{3,5},{4,2},{5,3},{10,12},{11,13},{12,10},{13,11},{18,20},{1... | collective-permute-start | bytes 3145736 | tf_op jit(solution)/shard_map/ppermute | solution.py:595
  431.2 54.2 %collective-permute-start.88 = (bf16[1024,512]{1,0:T(8,128)(2,1)}, bf16[1024,512]{1,0:T(8,128)(2,1)}, u32[]{:S(2)}, u32[]{:S(2)}) collective-permute-start(bf16[1024,512]{1,0:T(8,128)(2,1)} %shard_map.281.refs_2_), channel_id=1, source_target_pairs={{0,2},{1,3},{6,4},{7,5},{2,0},{3,1},{4,6},{5,7},{8,10},{9,11},{14,... | collective-permute-start | bytes 3145736 | tf_op jit(solution)/shard_map/ppermute | solution.py:580
  439.6 264.1 %all-gather.5.cloned.1.call-start = ((), (), s32[]{:S(2)}) async-start(), calls=%async_computation.5 | async-start | bytes 1769472 | tf_op jit(solution)/shard_map/all_gather | solution.py:109
  463.3 42.6 %collective-permute-start.86 = (bf16[512,1024]{1,0:T(8,128)(2,1)S(1)}, bf16[512,1024]{1,0:T(8,128)(2,1)S(1)}, u32[]{:S(2)}, u32[]{:S(2)}) collective-permute-start(bf16[512,1024]{1,0:T(8,128)(2,1)S(1)} %shard_map.278.refs_2_), channel_id=1, source_target_pairs={{0,2},{1,3},{6,4},{7,5},{2,0},{3,1},{4,6},{5,7},{8,10},{9,11},{14,... | collective-permute-start | bytes 3145736 | tf_op jit(solution)/shard_map/ppermute | solution.py:580
  465.0 41.7 %collective-permute-start.74 = (bf16[1024,512]{1,0:T(8,128)(2,1)S(1)}, bf16[1024,512]{1,0:T(8,128)(2,1)S(1)}, u32[]{:S(2)}, u32[]{:S(2)}) collective-permute-start(bf16[1024,512]{1,0:T(8,128)(2,1)S(1)} %get-tuple-element.218.refs_1_), channel_id=1, source_target_pairs={{2,4},{3,5},{4,2},{5,3},{10,12},{11,13},{12,10},{13,11},{18,20},{1... | collective-permute-start | bytes 3145736 | tf_op jit(solution)/shard_map/ppermute | solution.py:595
  465.8 41.6 %collective-permute-start.75 = (bf16[1024,512]{1,0:T(8,128)(2,1)S(1)}, bf16[1024,512]{1,0:T(8,128)(2,1)S(1)}, u32[]{:S(2)}, u32[]{:S(2)}) collective-permute-start(bf16[1024,512]{1,0:T(8,128)(2,1)S(1)} %get-tuple-element.219.here_ref), channel_id=1, source_target_pairs={{0,1},{1,0},{2,3},{3,2},{4,5},{5,4},{6,7},{7,6},{8,9},{9,8},{10,11... | collective-permute-start | bytes 3145736 | tf_op jit(solution)/shard_map/ppermute | solution.py:599
  509.8 34.1 %collective-permute-start.83 = (bf16[1024,512]{1,0:T(8,128)(2,1)S(1)}, bf16[1024,512]{1,0:T(8,128)(2,1)S(1)}, u32[]{:S(2)}, u32[]{:S(2)}) collective-permute-start(bf16[1024,512]{1,0:T(8,128)(2,1)S(1)} %shard_map.274.refs_2_), channel_id=1, source_target_pairs={{0,2},{1,3},{6,4},{7,5},{2,0},{3,1},{4,6},{5,7},{8,10},{9,11},{14,... | collective-permute-start | bytes 3145736 | tf_op jit(solution)/shard_map/ppermute | solution.py:580
  519.4 41.2 %collective-permute-start.96 = (bf16[1024,512]{1,0:T(8,128)(2,1)S(1)}, bf16[1024,512]{1,0:T(8,128)(2,1)S(1)}, u32[]{:S(2)}, u32[]{:S(2)}) collective-permute-start(bf16[1024,512]{1,0:T(8,128)(2,1)S(1)} %shard_map.290.refs_2_), channel_id=1, source_target_pairs={{0,2},{1,3},{6,4},{7,5},{2,0},{3,1},{4,6},{5,7},{8,10},{9,11},{14,... | collective-permute-start | bytes 3145736 | tf_op jit(solution)/shard_map/ppermute | solution.py:580
  540.4 46.5 %collective-permute-start.94 = (bf16[512,1024]{1,0:T(8,128)(2,1)}, bf16[512,1024]{1,0:T(8,128)(2,1)}, u32[]{:S(2)}, u32[]{:S(2)}) collective-permute-start(bf16[512,1024]{1,0:T(8,128)(2,1)} %shard_map.288.refs_2_), channel_id=1, source_target_pairs={{0,2},{1,3},{6,4},{7,5},{2,0},{3,1},{4,6},{5,7},{8,10},{9,11},{14,... | collective-permute-start | bytes 3145736 | tf_op jit(solution)/shard_map/ppermute | solution.py:580
  545.5 43.7 %collective-permute-start.84 = (bf16[1024,512]{1,0:T(8,128)(2,1)}, bf16[1024,512]{1,0:T(8,128)(2,1)S(1)}, u32[]{:S(2)}, u32[]{:S(2)}) collective-permute-start(bf16[1024,512]{1,0:T(8,128)(2,1)} %get-tuple-element.235.refs_1_), channel_id=1, source_target_pairs={{2,4},{3,5},{4,2},{5,3},{10,12},{11,13},{12,10},{13,11},{18,20},{1... | collective-permute-start | bytes 3145736 | tf_op jit(solution)/shard_map/ppermute | solution.py:595
  546.2 45.1 %collective-permute-start.85 = (bf16[1024,512]{1,0:T(8,128)(2,1)}, bf16[1024,512]{1,0:T(8,128)(2,1)}, u32[]{:S(2)}, u32[]{:S(2)}) collective-permute-start(bf16[1024,512]{1,0:T(8,128)(2,1)} %get-tuple-element.236.here_ref), channel_id=1, source_target_pairs={{0,1},{1,0},{2,3},{3,2},{4,5},{5,4},{6,7},{7,6},{8,9},{9,8},{10,11... | collective-permute-start | bytes 3145736 | tf_op jit(solution)/shard_map/ppermute | solution.py:599
  562.0 34.7 %collective-permute-start.97 = (bf16[1024,512]{1,0:T(8,128)(2,1)}, bf16[1024,512]{1,0:T(8,128)(2,1)S(1)}, u32[]{:S(2)}, u32[]{:S(2)}) collective-permute-start(bf16[1024,512]{1,0:T(8,128)(2,1)} %get-tuple-element.256.refs_1_), channel_id=1, source_target_pairs={{2,4},{3,5},{4,2},{5,3},{10,12},{11,13},{12,10},{13,11},{18,20},{1... | collective-permute-start | bytes 3145736 | tf_op jit(solution)/shard_map/ppermute | solution.py:595
  562.7 47.2 %collective-permute-start.98 = (bf16[1024,512]{1,0:T(8,128)(2,1)}, bf16[1024,512]{1,0:T(8,128)(2,1)}, u32[]{:S(2)}, u32[]{:S(2)}) collective-permute-start(bf16[1024,512]{1,0:T(8,128)(2,1)} %get-tuple-element.258.here_ref), channel_id=1, source_target_pairs={{0,1},{1,0},{2,3},{3,2},{4,5},{5,4},{6,7},{7,6},{8,9},{9,8},{10,11... | collective-permute-start | bytes 3145736 | tf_op jit(solution)/shard_map/ppermute | solution.py:599
  589.2 40.3 %collective-permute-start.99 = (bf16[512,1024]{1,0:T(8,128)(2,1)S(1)}, bf16[512,1024]{1,0:T(8,128)(2,1)S(1)}, u32[]{:S(2)}, u32[]{:S(2)}) collective-permute-start(bf16[512,1024]{1,0:T(8,128)(2,1)S(1)} %get-tuple-element.263.here_ref), channel_id=1, source_target_pairs={{0,1},{1,0},{2,3},{3,2},{4,5},{5,4},{6,7},{7,6},{8,9},{9,8},{10,11... | collective-permute-start | bytes 3145736 | tf_op jit(solution)/shard_map/ppermute | solution.py:599
  595.5 37.9 %collective-permute-start.92 = (bf16[1024,512]{1,0:T(8,128)(2,1)S(1)}, bf16[1024,512]{1,0:T(8,128)(2,1)S(1)}, u32[]{:S(2)}, u32[]{:S(2)}) collective-permute-start(bf16[1024,512]{1,0:T(8,128)(2,1)S(1)} %shard_map.286.refs_1_), channel_id=1, source_target_pairs={{2,0},{3,1},{4,6},{5,7},{10,8},{11,9},{12,14},{13,15},{18,16},{19,... | collective-permute-start | bytes 3145736 | tf_op jit(solution)/shard_map/ppermute | solution.py:580
  614.1 33.9 %collective-permute-start.100 = (bf16[1024,512]{1,0:T(8,128)(2,1)S(1)}, bf16[1024,512]{1,0:T(8,128)(2,1)S(1)}, u32[]{:S(2)}, u32[]{:S(2)}) collective-permute-start(bf16[1024,512]{1,0:T(8,128)(2,1)S(1)} %shard_map.298.refs_1_), channel_id=1, source_target_pairs={{2,0},{3,1},{4,6},{5,7},{10,8},{11,9},{12,14},{13,15},{18,16},{19,... | collective-permute-start | bytes 3145736 | tf_op jit(solution)/shard_map/ppermute | solution.py:580
  631.9 54.1 %collective-permute-start.102 = (bf16[512,1024]{1,0:T(8,128)(2,1)S(1)}, bf16[512,1024]{1,0:T(8,128)(2,1)}, u32[]{:S(2)}, u32[]{:S(2)}) collective-permute-start(bf16[512,1024]{1,0:T(8,128)(2,1)S(1)} %shard_map.296.refs_1_), channel_id=1, source_target_pairs={{2,0},{3,1},{4,6},{5,7},{10,8},{11,9},{12,14},{13,15},{18,16},{19,... | collective-permute-start | bytes 3145736 | tf_op jit(solution)/shard_map/ppermute | solution.py:580
  633.4 62.3 %collective-permute-start.93 = (bf16[1024,512]{1,0:T(8,128)(2,1)S(1)}, bf16[1024,512]{1,0:T(8,128)(2,1)}, u32[]{:S(2)}, u32[]{:S(2)}) collective-permute-start(bf16[1024,512]{1,0:T(8,128)(2,1)S(1)} %shard_map.294.here_ref), channel_id=1, source_target_pairs={{0,1},{1,0},{2,3},{3,2},{4,5},{5,4},{6,7},{7,6},{8,9},{9,8},{10,11... | collective-permute-start | bytes 3145736 | tf_op jit(solution)/shard_map/ppermute | solution.py:599
  648.1 51.6 %collective-permute-start.101 = (bf16[1024,512]{1,0:T(8,128)(2,1)S(1)}, bf16[1024,512]{1,0:T(8,128)(2,1)}, u32[]{:S(2)}, u32[]{:S(2)}) collective-permute-start(bf16[1024,512]{1,0:T(8,128)(2,1)S(1)} %shard_map.302.here_ref), channel_id=1, source_target_pairs={{0,1},{1,0},{2,3},{3,2},{4,5},{5,4},{6,7},{7,6},{8,9},{9,8},{10,11... | collective-permute-start | bytes 3145736 | tf_op jit(solution)/shard_map/ppermute | solution.py:599
  (170 other events, 2330.0 us)
Sparse Core Ops, SparseCore 0:
  35.5 49.0 all-gather.2
  285.9 77.5 reduce-scatter.2
  439.8 36.6 reduce-scatter.4
  563.6 40.0 all-gather.4
